TPU v7x, 32 devices: a whole 2x2x4 slice. The times are simulated.
32 devices in a mesh: dp: 4 (over x, core), mp: 8 (over z, y).
Axes of the slice: x: 2, y: 2, z: 4, core: 2. Of those that a mesh axis runs over, the one named last changes fastest.
Arguments:
- partial_grads: bfloat16 [4, 48, 512, 512], P('dp', None, 'mp'), may hold values from -5 to 5
- owner_device: int32 [48], replicated, may hold values from 0 to 31, as said below
- layer_of: int32 [48], replicated, may hold values from 0 to 3
- stat_left: float32 [64, 512, 512], P(('dp', 'mp')), as said below
- stat_right: float32 [64, 512, 512], P(('dp', 'mp')), as said below
- basis_left: float32 [64, 512, 512], P(('dp', 'mp'))
- basis_right: float32 [64, 512, 512], P(('dp', 'mp'))
- moment_first: float32 [64, 512, 512], P(('dp', 'mp')), may hold values from -4 to 4
- moment_second: float32 [64, 512, 512], P(('dp', 'mp')), may hold values from 0.02 to 2
Outputs:
- update: bfloat16 [48, 512, 512], P('dp', 'mp')
- stat_left_next: float32 [64, 512, 512], P(('dp', 'mp'))
- stat_right_next: float32 [64, 512, 512], P(('dp', 'mp'))
- basis_left_next: float32 [64, 512, 512], P(('dp', 'mp'))
- basis_right_next: float32 [64, 512, 512], P(('dp', 'mp'))
- moment_first_next: float32 [64, 512, 512], P(('dp', 'mp'))
- moment_second_next: float32 [64, 512, 512], P(('dp', 'mp'))
Inputs may be any that keep to these rules, and one draw needn't show every extreme that they name: `owner_device`: no device index is named by more than 2 blocks, and some device is named by exactly 2. `stat_left`: every slot's matrix is symmetric. `stat_right`: every slot's matrix is symmetric.
All inputs are finite; a program needn't handle non-finite values.
Results may differ from a plain program's by a relative error of at most 0.001.
Values may be sent and summed in bfloat16 or wider, within the bound.
No kernel may reach another device: no remote copies, remote signals or barrier semaphores. Data moves between devices by JAX's collectives and lax.ppermute only.
A program may use at most 128 MiB of HBM per device.

v0:
```python
import math

import jax
import jax.numpy as jnp
from jax import lax
from jax.sharding import PartitionSpec as P

ITERS = 4


PRECISE = lax.Precision.HIGHEST
BETA_ONE = 0.9
BETA_TWO = 0.95
SHRINK = math.log(0.8)


def matmul(left_side, right_side):
    return jnp.dot(left_side, right_side, precision=PRECISE, preferred_element_type=jnp.float32)


def orthogonal(basis_in):
    scaling = 0.4 / (
        jnp.sqrt(jnp.float32(basis_in.shape[0])) * jnp.sqrt(jnp.mean(basis_in * basis_in) + 1e-06)
    )
    current = basis_in * scaling
    for _ in range(ITERS):
        gram_matrix = matmul(current.T, current)
        current = 1.5 * current - 0.5 * matmul(current, gram_matrix)
    return current


def soap_block(
    gradient,
    left_stat,
    right_stat,
    left_base,
    right_base,
    first_moment,
    second_moment,
    scale_factor,
):
    first_new = BETA_ONE * first_moment + (1.0 - BETA_ONE) * gradient
    grad_rot = matmul(matmul(left_base.T, gradient), right_base)
    first_rot = matmul(matmul(left_base.T, first_new), right_base)
    second_new = BETA_TWO * second_moment + (1.0 - BETA_TWO) * grad_rot * grad_rot
    normed = first_rot / (jnp.sqrt(second_new) + 1e-08)
    direction = matmul(matmul(left_base, normed), right_base.T)
    block_update = (scale_factor * direction).astype(jnp.bfloat16)
    left_new = BETA_TWO * left_stat + (1.0 - BETA_TWO) * matmul(gradient, gradient.T)
    right_new = BETA_TWO * right_stat + (1.0 - BETA_TWO) * matmul(gradient.T, gradient)
    left_base_new = orthogonal(matmul(left_new, left_base))
    right_base_new = orthogonal(matmul(right_new, right_base))
    return (block_update, left_new, right_new, left_base_new, right_base_new, first_new, second_new)


def slot_numbers(owner_device, capacity):
    block_count = owner_device.shape[0]
    same_owner = owner_device[:, None] == owner_device[None, :]
    earlier = jnp.arange(block_count)[None, :] < jnp.arange(block_count)[:, None]
    owner_rank = jnp.sum((same_owner & earlier).astype(jnp.int32), axis=1)
    return owner_device * capacity + owner_rank


def local(
    partial_grads,
    owner_device,
    layer_of,
    stat_left,
    stat_right,
    basis_left,
    basis_right,
    moment_first,
    moment_second,
):
    capacity = stat_left.shape[0]
    model_width = stat_left.shape[1]
    block_count = owner_device.shape[0]
    device_count = lax.axis_size(("dp", "mp"))
    group_count = lax.axis_size("dp")
    member_count = lax.axis_size("mp")
    slot_total = capacity * device_count
    group_blocks = block_count // group_count
    group_index = lax.axis_index("dp")
    slot_of = slot_numbers(owner_device, capacity)
    slot_hit = slot_of[None, :] == jnp.arange(slot_total)[:, None]
    hit_count = slot_hit.astype(jnp.int32)
    block_at = jnp.sum(hit_count * jnp.arange(block_count)[None, :], axis=1)
    slot_live = jnp.sum(hit_count, axis=1) > 0
    layer_at = jnp.sum(hit_count * layer_of[None, :], axis=1)
    own_index = lax.axis_index(("dp", "mp"))
    own_live = lax.dynamic_slice_in_dim(slot_live, own_index * capacity, capacity)
    own_layer = lax.dynamic_slice_in_dim(layer_at, own_index * capacity, capacity)
    local_rows = partial_grads[0]
    row_count = local_rows.shape[1]
    packed = jnp.where(
        slot_live[:, None, None], local_rows[block_at], jnp.zeros((), local_rows.dtype)
    )
    packed = packed.reshape(device_count, capacity, row_count, model_width)
    arrived = lax.all_to_all(packed, ("dp", "mp"), split_axis=0, concat_axis=0, tiled=True)
    arrived = arrived.reshape(group_count, member_count, capacity, row_count, model_width)
    summed = jnp.sum(arrived.astype(jnp.float32), axis=0)
    own_grads = summed.transpose(1, 0, 2, 3).reshape(capacity, model_width, model_width)
    factors = jnp.exp(SHRINK * (group_count - 1 - own_layer).astype(jnp.float32))

    def one_slot(items):
        return soap_block(*items)

    olds = (stat_left, stat_right, basis_left, basis_right, moment_first, moment_second)
    results = lax.map(one_slot, (own_grads,) + olds + (factors,))
    kept = tuple(
        (
            jnp.where(own_live[:, None, None], new_state, old_state)
            for new_state, old_state in zip(results[1:], olds)
        )
    )
    own_blocks = lax.dynamic_slice_in_dim(block_at, own_index * capacity, capacity)
    target_group = own_blocks // group_blocks
    pieces = (
        results[0].reshape(capacity, member_count, row_count, model_width).transpose(1, 0, 2, 3)
    )
    wanted = (target_group[None, :] == jnp.arange(group_count)[:, None]) & own_live[None, :]
    outgoing = jnp.where(wanted[:, None, :, None, None], pieces[None], jnp.zeros((), jnp.bfloat16))
    flat = outgoing.reshape(device_count, capacity, row_count, model_width)
    returned = lax.all_to_all(flat, ("dp", "mp"), split_axis=0, concat_axis=0, tiled=True)
    returned = returned.reshape(slot_total, row_count, model_width)
    my_slots = lax.dynamic_slice_in_dim(slot_of, group_index * group_blocks, group_blocks)
    update_rows = returned[my_slots]
    return (update_rows, kept[0], kept[1], kept[2], kept[3], kept[4], kept[5])


def solution(mesh):
    in_specs = (
        P("dp", None, "mp", None),
        P(),
        P(),
        P(("dp", "mp"), None, None),
        P(("dp", "mp"), None, None),
        P(("dp", "mp"), None, None),
        P(("dp", "mp"), None, None),
        P(("dp", "mp"), None, None),
        P(("dp", "mp"), None, None),
    )
    out_specs = (
        P("dp", "mp", None),
        P(("dp", "mp"), None, None),
        P(("dp", "mp"), None, None),
        P(("dp", "mp"), None, None),
        P(("dp", "mp"), None, None),
        P(("dp", "mp"), None, None),
        P(("dp", "mp"), None, None),
    )
    return jax.shard_map(local, mesh=mesh, in_specs=in_specs, out_specs=out_specs, check_vma=False)
```

profile of v0, /device:TPU:5, one launch (start us, length us, event | category | flops | bytes accessed | tf_op | source)
XLA Modules:
  0.0 357.0 jit_solution(1516523463314127880)
XLA Ops:
  3.2 2.8 gather_fusion
  6.0 4.5 %broadcast_select_fusion = bf16[32,2,64,512]{3,2,1,0:T(8,128)(2,1)} fusion(bf16[32,2,64,512]{3,2,1,0:T(8,128)(2,1)} %bitcast.219, pred[32,2]{1,0:T(8,128)(4,1)S(1)} %gt.11), kind=kLoop, calls=%fused_computation.93 | loop fusion | flops 2097152 | bytes 8388672 | tf_op jit(solution)/shard_map/jit(_where)/select_n | solution.py:95
  10.5 6.5 %all-to-all-start = ((bf16[32,2,64,512]{3,2,1,0:T(8,128)(2,1)}), bf16[32,2,64,512]{3,2,1,0:T(8,128)(2,1)}, u32[]{:S(2)}, u32[]{:S(2)}) async-start(bf16[32,2,64,512]{3,2,1,0:T(8,128)(2,1)} %broadcast_select_fusion), calls=%async_computation | async-start | bytes 8388608 | tf_op jit(solution)/shard_map/all_to_all | solution.py:99
  17.5 93.6 %all-to-all-done = bf16[32,2,64,512]{3,2,1,0:T(8,128)(2,1)} async-done(((bf16[32,2,64,512]{3,2,1,0:T(8,128)(2,1)}), bf16[32,2,64,512]{3,2,1,0:T(8,128)(2,1)}, u32[]{:S(2)}, u32[]{:S(2)}) %all-to-all-start) | async-done | bytes 4194336 | tf_op jit(solution)/shard_map/all_to_all | solution.py:99
  111.0 3.2 convert_reduce_fusion
  114.5 134.2 %while.22 = (s32[]{:T(128)}, bf16[2,512,512]{2,1,0:T(8,128)(2,1)}, f32[2,512,512]{2,1,0:T(8,128)}, f32[2,512,512]{2,1,0:T(8,128)}, f32[2,512,512]{2,1,0:T(8,128)...) while((s32[]{:T(128)}, bf16[2,512,512]{2,1,0:T(8,128)(2,1)}, ...), condition=%wide.region_8.9_spmd, body=%wide.region_5.8_spmd.sunk | while | flops 41890086912 | bytes 210248016 | solution.py:109
  114.8 4.3 %bitcast_dynamic-update-slice_fusion.8 = (f32[2,512,512]{2,1,0:T(8,128)}, f32[512,512]{1,0:T(8,128)S(1)}) fusion(f32[2,512,512]{2,1,0:T(8,128)} %get-tuple-element.294, s32[]{:T(128)} %get-tuple-element.291, f32[2,512,512]{2,1,0:T(8,128)S(1)} %get-tuple-element.323, f32[2,512,512]{2,1,0:T(8,128)} %get-tuple-element.327), kind=kOutput, calls=%fused_computation.34.clone.1 | convolution fusion | flops 1611399168 | bytes 4195328 | tf_op jit(solution)/shard_map/while/body/eval_jaxpr/dot_general | solution.py:18
  119.1 2.6 multiply_reduce_fusion.5
  122.7 1.9 fusion.232
  124.6 3.4 fusion.233
  128.0 1.9 fusion.234
  129.9 1.9 fusion.235
  131.7 2.4 fusion.236
  134.2 1.9 fusion.237
  136.0 1.9 fusion.238
  137.9 1.9 fusion.239
  141.1 1.9 bitcast_dynamic-update-slice_fusion.7
  143.1 2.6 multiply_reduce_fusion.4
  146.7 2.1 fusion.224
  148.8 3.4 fusion.225
  152.2 1.9 fusion.226
  154.1 1.9 fusion.227
  156.0 1.9 fusion.228
  157.8 1.9 fusion.229
  159.7 1.9 fusion.230
  161.6 3.2 fusion.231
  164.8 1.9 fusion.221
  166.8 1.9 bitcast_dynamic-update-slice_fusion.6
  168.8 2.0 fusion.220
  170.8 2.0 convolution_divide_fusion.2
  172.9 1.8 fusion.222
  175.3 2.5 fusion.223
  180.3 4.3 %bitcast_dynamic-update-slice_fusion.8 = (f32[2,512,512]{2,1,0:T(8,128)}, f32[512,512]{1,0:T(8,128)S(1)}) fusion(f32[2,512,512]{2,1,0:T(8,128)} %get-tuple-element.294, s32[]{:T(128)} %get-tuple-element.291, f32[2,512,512]{2,1,0:T(8,128)S(1)} %get-tuple-element.323, f32[2,512,512]{2,1,0:T(8,128)} %get-tuple-element.327), kind=kOutput, calls=%fused_computation.34.clone.1 | convolution fusion | flops 1611399168 | bytes 4195328 | tf_op jit(solution)/shard_map/while/body/eval_jaxpr/dot_general | solution.py:18
  184.6 2.6 multiply_reduce_fusion.5
  188.1 1.9 fusion.232
  190.0 3.4 fusion.233
  193.5 1.9 fusion.234
  195.3 1.9 fusion.235
  197.2 2.1 fusion.236
  199.3 1.9 fusion.237
  201.2 1.9 fusion.238
  203.1 1.9 fusion.239
  205.0 1.3 copy-done.16
  206.3 1.9 bitcast_dynamic-update-slice_fusion.7
  208.3 2.6 multiply_reduce_fusion.4
  211.9 2.4 fusion.224
  214.2 3.4 fusion.225
  217.7 1.9 fusion.226
  219.5 1.9 fusion.227
  221.4 1.9 fusion.228
  223.3 1.9 fusion.229
  225.2 1.9 fusion.230
  227.0 3.0 fusion.231
  230.1 1.9 fusion.221
  232.0 1.9 bitcast_dynamic-update-slice_fusion.6
  234.0 2.0 fusion.220
  236.0 2.0 convolution_divide_fusion.2
  238.1 1.8 fusion.222
  240.6 2.5 fusion.223
  248.7 4.8 %bitcast_select_fusion = bf16[32,2,64,512]{3,2,1,0:T(8,128)(2,1)} fusion(pred[32,2]{1,0:T(8,128)(4,1)S(1)} %broadcast_bitcast_fusion, bf16[8,2,64,512]{3,2,0,1:T(8,128)(2,1)} %bitcast.221), kind=kLoop, calls=%fused_computation.92 | loop fusion | flops 2097152 | bytes 5242944 | tf_op jit(solution)/shard_map/jit(_where)/select_n | solution.py:122
  253.5 5.3 %all-to-all-start.1 = ((bf16[32,2,64,512]{3,2,1,0:T(8,128)(2,1)}), bf16[32,2,64,512]{3,2,1,0:T(8,128)(2,1)}, u32[]{:S(2)}, u32[]{:S(2)}) async-start(bf16[32,2,64,512]{3,2,1,0:T(8,128)(2,1)} %bitcast_select_fusion), calls=%async_computation.1 | async-start | bytes 8388608 | tf_op jit(solution)/shard_map/all_to_all | solution.py:124
  258.9 14.2 %broadcast_select_fusion.1 = (f32[2,512,512]{2,1,0:T(8,128)}, f32[2,512,512]{2,1,0:T(8,128)}, f32[2,512,512]{2,1,0:T(8,128)}, f32[2,512,512]{2,1,0:T(8,128)}, f32[2,512,512]{2,1,0:T(8,128)}, /*index=5*/f32[2,512,512]{2,1,0:T(8,128)}) fusion(f32[2,512,512]{2,1,0:T(8,128)} %get-tuple-element.101, f32[2,512,512]{2,1,0:T(8,128)} %get-tuple-element.338, ...), kind=kLoop, calls=%fused_computation.94 | loop fusion | flops 3145728 | bytes 37748736 | tf_op jit(solution)/shard_map/jit(_where)/select_n | solution.py:112
  273.1 80.0 %all-to-all-done.1 = bf16[32,2,64,512]{3,2,1,0:T(8,128)(2,1)} async-done(((bf16[32,2,64,512]{3,2,1,0:T(8,128)(2,1)}), bf16[32,2,64,512]{3,2,1,0:T(8,128)(2,1)}, u32[]{:S(2)}, u32[]{:S(2)}) %all-to-all-start.1) | async-done | bytes 4194336 | tf_op jit(solution)/shard_map/all_to_all | solution.py:124
  353.1 3.7 %gather_fusion.1 = bf16[12,64,512]{2,1,0:T(8,128)(2,1)} fusion(bf16[64,64,512]{2,1,0:T(8,128)(2,1)} %bitcast.25, s32[1024]{0:T(1024)S(1)} %pad_clamp_fusion), kind=kCustom, calls=%fused_computation.1 | custom fusion | bytes 1572912 | tf_op jit(solution)/shard_map/gather | solution.py:127
  (98 shorter events, 11.6 us)
Async XLA Ops:
  0.6 2.6 copy-start
  10.5 100.5 %all-to-all-start = ((bf16[32,2,64,512]{3,2,1,0:T(8,128)(2,1)}), bf16[32,2,64,512]{3,2,1,0:T(8,128)(2,1)}, u32[]{:S(2)}, u32[]{:S(2)}) async-start(bf16[32,2,64,512]{3,2,1,0:T(8,128)(2,1)} %broadcast_select_fusion), calls=%async_computation | async-start | bytes 8388608 | tf_op jit(solution)/shard_map/all_to_all | solution.py:99
  114.8 4.3 %copy-start.6 = (f32[2,512,512]{2,1,0:T(8,128)S(1)}, f32[2,512,512]{2,1,0:T(8,128)}, u32[]{:S(2)}) copy-start(f32[2,512,512]{2,1,0:T(8,128)} %get-tuple-element.324) | copy-start | bytes 6291460 | tf_op jit(solution)/shard_map/while
  121.7 1.0 copy-start.5
  134.1 3.8 %copy-start.15 = (f32[2,512,512]{2,1,0:T(8,128)S(1)}, f32[2,512,512]{2,1,0:T(8,128)}, u32[]{:S(2)}) copy-start(f32[2,512,512]{2,1,0:T(8,128)} %get-tuple-element.296) | copy-start | bytes 6291460 | tf_op jit(solution)/shard_map/while
  136.0 5.1 %copy-start.13 = (f32[2,512,512]{2,1,0:T(8,128)S(1)}, f32[2,512,512]{2,1,0:T(8,128)}, u32[]{:S(2)}) copy-start(f32[2,512,512]{2,1,0:T(8,128)} %get-tuple-element.293) | copy-start | bytes 6291460 | tf_op jit(solution)/shard_map/while
  137.9 3.2 copy-start.9
  139.8 1.3 copy-start.16
  141.1 2.0 copy-start.2
  143.1 2.6 copy-start.14
  145.7 1.0 copy-start.4
  159.7 7.1 %copy-start.11 = (f32[2,512,512]{2,1,0:T(8,128)S(1)}, f32[2,512,512]{2,1,0:T(8,128)}, u32[]{:S(2)}) copy-start(f32[2,512,512]{2,1,0:T(8,128)} %get-tuple-element.298) | copy-start | bytes 6291460 | tf_op jit(solution)/shard_map/while
  161.6 3.3 copy-start.3
  161.6 5.2 %copy-start.10 = (f32[2,512,512]{2,1,0:T(8,128)S(1)}, f32[2,512,512]{2,1,0:T(8,128)}, u32[]{:S(2)}) copy-start(f32[2,512,512]{2,1,0:T(8,128)} %get-tuple-element.325) | copy-start | bytes 6291460 | tf_op jit(solution)/shard_map/while
  164.8 2.0 copy-start.7
  166.8 2.0 copy-start.8
  168.8 2.0 copy-start.12
  172.9 2.5 copy-start.17
  177.8 1.1 copy-start.18
  180.3 4.3 %copy-start.6 = (f32[2,512,512]{2,1,0:T(8,128)S(1)}, f32[2,512,512]{2,1,0:T(8,128)}, u32[]{:S(2)}) copy-start(f32[2,512,512]{2,1,0:T(8,128)} %get-tuple-element.324) | copy-start | bytes 6291460 | tf_op jit(solution)/shard_map/while
  187.2 1.0 copy-start.5
  199.3 3.8 %copy-start.15 = (f32[2,512,512]{2,1,0:T(8,128)S(1)}, f32[2,512,512]{2,1,0:T(8,128)}, u32[]{:S(2)}) copy-start(f32[2,512,512]{2,1,0:T(8,128)} %get-tuple-element.296) | copy-start | bytes 6291460 | tf_op jit(solution)/shard_map/while
  201.2 5.1 %copy-start.13 = (f32[2,512,512]{2,1,0:T(8,128)S(1)}, f32[2,512,512]{2,1,0:T(8,128)}, u32[]{:S(2)}) copy-start(f32[2,512,512]{2,1,0:T(8,128)} %get-tuple-element.293) | copy-start | bytes 6291460 | tf_op jit(solution)/shard_map/while
  203.1 3.2 copy-start.9
  205.0 1.3 copy-start.16
  206.3 2.0 copy-start.2
  208.2 2.6 copy-start.14
  210.9 1.0 copy-start.4
  225.1 6.9 %copy-start.11 = (f32[2,512,512]{2,1,0:T(8,128)S(1)}, f32[2,512,512]{2,1,0:T(8,128)}, u32[]{:S(2)}) copy-start(f32[2,512,512]{2,1,0:T(8,128)} %get-tuple-element.298) | copy-start | bytes 6291460 | tf_op jit(solution)/shard_map/while
  227.0 3.0 copy-start.3
  227.0 5.0 %copy-start.10 = (f32[2,512,512]{2,1,0:T(8,128)S(1)}, f32[2,512,512]{2,1,0:T(8,128)}, u32[]{:S(2)}) copy-start(f32[2,512,512]{2,1,0:T(8,128)} %get-tuple-element.325) | copy-start | bytes 6291460 | tf_op jit(solution)/shard_map/while
  230.1 2.0 copy-start.7
  232.0 2.0 copy-start.8
  234.0 2.0 copy-start.12
  238.1 2.5 copy-start.17
  243.1 1.1 copy-start.18
  253.5 99.6 %all-to-all-start.1 = ((bf16[32,2,64,512]{3,2,1,0:T(8,128)(2,1)}), bf16[32,2,64,512]{3,2,1,0:T(8,128)(2,1)}, u32[]{:S(2)}, u32[]{:S(2)}) async-start(bf16[32,2,64,512]{3,2,1,0:T(8,128)(2,1)} %bitcast_select_fusion), calls=%async_computation.1 | async-start | bytes 8388608 | tf_op jit(solution)/shard_map/all_to_all | solution.py:124
  258.9 97.9 %copy-start.1 = (bf16[1,48,64,512]{3,2,1,0:T(8,128)(2,1)S(1)}, bf16[1,48,64,512]{3,2,1,0:T(8,128)(2,1)}, u32[]{:S(2)}) copy-start(bf16[1,48,64,512]{3,2,1,0:T(8,128)(2,1)} %param.11) | copy-start | bytes 9437188
where the time goes:
time: 363 us; the launch traced here: 357 us
  waiting for transfers between devices  174 us (48%)
  matrix products  117 us (32%)
  other arithmetic  31.9 us (9%)
  local copies, waits for them, and re-layouts  14.1 us (4%)
  starting transfers between devices  11.8 us (3%)
  loops' own time  7.33 us (2%)
    dot_general x52, matrix products, matmul(): jnp.dot(left_side, right_side, precision=PRECISE, preferred_element_type=...  117 us
    all_to_all x1, waiting for transfers between devices, local(): lax.all_to_all(packed, ('dp', 'mp'), split_axis=0, concat_axis=0, tiled=T...  93.6 us
    all_to_all x1, waiting for transfers between devices, local(): lax.all_to_all(flat, ('dp', 'mp'), split_axis=0, concat_axis=0, tiled=True)  80 us
    select_n x1, other arithmetic, local(): jnp.where(own_live[:, None, None], new_state, old_state)  14.2 us
    another operation x1, loops' own time, local(): results = lax.map(one_slot, (own_grads,) + olds + (factors,))  7.33 us
  transfers between devices with their start and end apart: 2, of which 2 were waited for; matrix products, arithmetic and copies ran while one was open for 4% of the time, Pallas kernels for 0%

commit v1 on v0

v1 whole, which is shorter than its diff:
```python
import functools
import math

import jax
import jax.numpy as jnp
from jax import lax
from jax.experimental import pallas as pl
from jax.experimental.pallas import tpu as pltpu
from jax.sharding import PartitionSpec as P

ITERS = 4
BETA_ONE = 0.9
BETA_TWO = 0.95
SHRINK = math.log(0.8)
LANES = 128
TAIL = 16
MIB = 1 << 20
F32 = jnp.float32
BF16 = jnp.bfloat16
ANY = pl.BlockSpec(memory_space=pl.ANY)
SMEM = pl.BlockSpec(memory_space=pltpu.SMEM)


def params(limit=48 * MIB):
    return pltpu.CompilerParams(vmem_limit_bytes=limit)


def cost(flops, moved):
    return pl.CostEstimate(flops=int(flops), bytes_accessed=int(moved), transcendentals=0)


def table_kernel(devices, capacity, owner_ref, layer_ref, block_ref, rank_ref, count_ref, depth_ref):
    def clear(d, carry):
        count_ref[d] = 0
        for k in range(capacity):
            block_ref[k * devices + d] = 0
            depth_ref[k * devices + d] = 0
        return carry

    lax.fori_loop(0, devices, clear, 0)

    def place(b, carry):
        owner = owner_ref[b]
        rank = count_ref[owner]
        rank_ref[b] = rank
        block_ref[rank * devices + owner] = b
        depth_ref[rank * devices + owner] = layer_ref[b]
        count_ref[owner] = rank + 1
        return carry

    lax.fori_loop(0, owner_ref.shape[0], place, 0)


def tables(owner_device, layer_of, devices, capacity):
    blocks = owner_device.shape[0]
    flat = jax.ShapeDtypeStruct((capacity * devices,), jnp.int32)
    return pl.pallas_call(
        functools.partial(table_kernel, devices, capacity),
        out_shape=(
            flat,
            jax.ShapeDtypeStruct((blocks,), jnp.int32),
            jax.ShapeDtypeStruct((devices,), jnp.int32),
            flat,
        ),
        in_specs=[SMEM, SMEM],
        out_specs=(SMEM,) * 4,
        name="tables",
    )(owner_device, layer_of)


def pack_kernel(base, halves, members, place_ref, block_ref, grads_ref, out_ref, sems):
    def piece(i):
        group = place_ref[0] ^ (2 * (i // members) + 1)
        block = block_ref[base + group * members + i % members]
        return pltpu.make_async_copy(
            grads_ref.at[block], out_ref.at[i // members, i % members], sems.at[i]
        )

    def start(i, carry):
        piece(i).start()
        return carry

    def wait(i, carry):
        piece(i).wait()
        return carry

    lax.fori_loop(0, halves * members, start, 0)
    lax.fori_loop(0, halves * members, wait, 0)


def pack(rank, place, block_at, grads, halves, members, devices):
    rows, width = grads.shape[1:]
    return pl.pallas_call(
        functools.partial(pack_kernel, rank * devices, halves, members),
        out_shape=jax.ShapeDtypeStruct((halves, members, rows, width), grads.dtype),
        in_specs=[SMEM, SMEM, ANY],
        out_specs=ANY,
        scratch_shapes=[pltpu.SemaphoreType.DMA((halves * members,))],
        cost_estimate=cost(0, 4 * halves * members * rows * width),
        name="pack",
    )(place, block_at, grads)


def decode_scale(ref, lead, rows, panels):
    tail = ref[lead + (pl.ds(panels * rows, TAIL), slice(None))].astype(jnp.int32).astype(F32)
    power = jnp.concatenate([tail] * (LANES // TAIL), axis=0).T
    return jnp.exp2(-power[:rows])


def decode(ref, lead, rows, panel, scale):
    part = ref[lead + (pl.ds(panel * rows, rows), slice(None))]
    return part.astype(jnp.int32).astype(F32) * scale


def fold_kernel(earlier, tables_refs, raw_ref, core_ref, *refs):
    out_ref = refs[earlier]
    rows, width = raw_ref.shape[1:]
    panels = width // LANES
    total = raw_ref[0].astype(F32) + core_ref[0, 0].astype(F32)
    if earlier:
        parts = []
        scales = [decode_scale(refs[n], (0, 0), rows, panels) for n in range(earlier)]
        for p in range(panels):
            part = total[:, p * LANES : (p + 1) * LANES]
            for n in range(earlier):
                part = part + decode(refs[n], (0, 0), rows, p, scales[n])
            parts.append(part)
        total = jnp.concatenate(parts, axis=1)
    largest = jnp.max(jnp.abs(total), axis=1, keepdims=True)
    power = jnp.floor(14.99 - jnp.log2(jnp.maximum(largest, 1e-26)))
    scaled = jnp.round(total * jnp.exp2(power)).astype(jnp.int32)
    for p in range(panels):
        out_ref[0, 0, pl.ds(p * rows, rows), :] = scaled[:, p * LANES : (p + 1) * LANES].astype(jnp.int16)
    wide = jnp.broadcast_to(power, (rows, LANES))
    if rows < LANES:
        wide = jnp.concatenate([wide, jnp.zeros((LANES - rows, LANES), F32)], axis=0)
    out_ref[0, 0, pl.ds(panels * rows, TAIL), :] = wide.T[:TAIL].astype(jnp.int32).astype(jnp.int16)


def fold(rank, first, count, place, block_at, grads, from_core, from_x, members, devices):
    rows, width = grads.shape[1:]
    tall = (width // LANES) * rows + TAIL

    def raw_map(i, place_ref, block_ref):
        group = place_ref[0] ^ (2 * (first + i // members))
        return (block_ref[rank * devices + group * members + i % members], 0, 0)

    def sent_map(i, place_ref, block_ref):
        return (first + i // members, i % members, 0, 0)

    def out_map(i, place_ref, block_ref):
        return (i // members, i % members, 0, 0)

    def body(place_ref, block_ref, *refs):
        fold_kernel(len(from_x), None, *refs)

    return pl.pallas_call(
        body,
        grid_spec=pltpu.PrefetchScalarGridSpec(
            num_scalar_prefetch=2,
            grid=(count * members,),
            in_specs=[pl.BlockSpec((1, rows, width), raw_map), pl.BlockSpec((1, 1, rows, width), sent_map)]
            + [pl.BlockSpec((1, 1, tall, LANES), sent_map) for _ in from_x],
            out_specs=pl.BlockSpec((1, 1, tall, LANES), out_map),
        ),
        out_shape=jax.ShapeDtypeStruct((count, members, tall, LANES), jnp.int16),
        cost_estimate=cost(0, 8 * count * members * rows * width),
        name="fold",
    )(place, block_at, grads, from_core, *from_x)


def split(x):
    high = x.astype(BF16)
    return high, (x - high.astype(F32)).astype(BF16)


def put_cols(ref, rows, x, order):
    width = x.shape[1]
    pieces = split(x)
    for n, which in enumerate(order):
        ref[rows, pl.ds(n * width, width)] = pieces[which]


def put_rows(ref, start, height, x):
    high, low = split(x)
    size = x.shape[0]
    ref[pl.ds(start, size), :] = high
    ref[pl.ds(height + start, size), :] = low
    ref[pl.ds(2 * height + start, size), :] = high


def dot_nn(a, b):
    return lax.dot_general(a, b, (((1,), (0,)), ((), ())), preferred_element_type=F32)


def dot_nt(a, b):
    return lax.dot_general(a, b, (((1,), (1,)), ((), ())), preferred_element_type=F32)


LEFT = (0, 0, 1)
BOTH = (0, 0, 1, 0)


def tiles(height, size=256):
    return [pl.ds(s, size) for s in range(0, height, size)]


def update_kernel(rank, slot, info_ref, pay_ref, ql_ref, qr_ref, m_ref, v_ref, *refs):
    g_ref, u_ref, m1_ref, v1_ref, qlt_ref, ql3_ref, qrs_ref, qrp_ref, bs_ref, as_ref, mrot_ref = refs[-11:]
    width = g_ref.shape[0]
    members = pay_ref.shape[0]
    rows = width // members
    panels = width // LANES
    live = info_ref[0] > rank

    @pl.when(jnp.logical_not(live))
    def _():
        u_ref[...] = jnp.zeros_like(u_ref)
        m1_ref[0] = m_ref[0]
        v1_ref[0] = v_ref[0]

    @pl.when(live)
    def _():
        put_cols(qlt_ref, slice(None), ql_ref[0].T, LEFT)
        put_rows(qrs_ref, 0, width, qr_ref[0])

        def bring(member, carry):
            scale = decode_scale(pay_ref, (member,), rows, panels)
            at = pl.multiple_of(member * rows, rows)
            for p in range(panels):
                g_ref[pl.ds(at, rows), pl.ds(p * LANES, LANES)] = decode(pay_ref, (member,), rows, p, scale)
            return carry

        lax.fori_loop(0, members, bring, 0)
        m1_ref[0] = BETA_ONE * m_ref[0] + (1.0 - BETA_ONE) * g_ref[...]

        put_rows(bs_ref, 0, width, m1_ref[0])
        for t in tiles(width):
            put_cols(as_ref, t, dot_nn(qlt_ref[t, :], bs_ref[...]), LEFT)
        for t in tiles(width):
            mrot_ref[t, :] = dot_nn(as_ref[t, :], qrs_ref[...])

        put_rows(bs_ref, 0, width, g_ref[...])
        for t in tiles(width):
            put_cols(as_ref, t, dot_nn(qlt_ref[t, :], bs_ref[...]), LEFT)
        for t in tiles(width):
            rot = dot_nn(as_ref[t, :], qrs_ref[...])
            second = BETA_TWO * v_ref[0, t, :] + (1.0 - BETA_TWO) * rot * rot
            v1_ref[0, t, :] = second
            put_rows(bs_ref, t.start, width, mrot_ref[t, :] / (jnp.sqrt(second) + 1e-08))
        put_cols(ql3_ref, slice(None), ql_ref[0], LEFT)
        put_cols(qrp_ref, slice(None), qr_ref[0], (0, 1, 0))
        depth = info_ref[1].astype(F32)
        factor = jnp.exp(SHRINK * jnp.full((1, width), depth, F32))
        for t in tiles(width):
            put_cols(as_ref, t, dot_nn(ql3_ref[t, :], bs_ref[...]), LEFT)
        for t in tiles(width):
            u_ref[t, :] = (factor * dot_nt(as_ref[t, :], qrp_ref[...])).astype(BF16)


def slot_block(slot, width):
    return pl.BlockSpec((1, width, width), lambda *_: (slot, 0, 0))


def update_call(rank, info, pay, ql, qr, m, v, carried):
    width = ql.shape[1]
    own = slot_block(rank, width)
    whole = pl.BlockSpec((width, width), lambda *_: (0, 0))
    state = jax.ShapeDtypeStruct(m.shape, F32)
    operands = [info, pay, ql, qr, m, v] + list(carried)
    aliases = {6: 2, 7: 3} if carried else {}
    wide = lambda n: pltpu.VMEM((width, n * width), BF16)
    tall = pltpu.VMEM((3 * width, width), BF16)
    return pl.pallas_call(
        functools.partial(update_kernel, rank, rank),
        grid=(1,),
        out_shape=(
            jax.ShapeDtypeStruct((width, width), F32),
            jax.ShapeDtypeStruct((width, width), BF16),
            state,
            state,
        ),
        in_specs=[SMEM, pl.BlockSpec(pay.shape, lambda *_: (0, 0, 0)), own, own, own, own] + [ANY] * len(carried),
        out_specs=(whole, whole, own, own),
        scratch_shapes=[wide(3), wide(3), tall, wide(3), tall, wide(3), pltpu.VMEM((width, width), F32)],
        input_output_aliases=aliases,
        compiler_params=params(),
        cost_estimate=cost(6 * 3 * 2 * width**3, 10 * 4 * width**2),
        name="update",
    )(*operands)


def basis_kernel(rank, left, info_ref, g_ref, s_ref, q_ref, *refs):
    s1_ref, q1_ref, y_ref, cols_ref, a_ref, b_ref = refs[-6:]
    width = g_ref.shape[0]
    live = info_ref[0] > rank
    fits = pl.ds(0, 3 * width), pl.ds(width, 3 * width)

    @pl.when(jnp.logical_not(live))
    def _():
        s1_ref[0] = s_ref[0]
        q1_ref[0] = q_ref[0]

    @pl.when(live)
    def _():
        grad = g_ref[...] if left else g_ref[...].T
        put_cols(cols_ref, slice(None), grad, BOTH)
        put_cols(a_ref, slice(None), q_ref[0].T, LEFT)
        for t in tiles(width):
            outer = dot_nt(cols_ref[t, fits[0]], cols_ref[:, fits[1]])
            stat = BETA_TWO * s_ref[0, t, :] + (1.0 - BETA_TWO) * outer
            s1_ref[0, t, :] = stat
            put_rows(b_ref, t.start, width, stat)
        squares = jnp.zeros((1, width), F32)
        for t in tiles(width):
            turned = dot_nn(a_ref[t, :], b_ref[...])
            y_ref[t, :] = turned
            squares = squares + jnp.sum(turned * turned, axis=0, keepdims=True)
        mean = jnp.sum(squares, axis=1, keepdims=True) * (1.0 / (width * width))
        scaling = 0.4 / (math.sqrt(width) * jnp.sqrt(mean + 1e-06))
        y_ref[...] = y_ref[...] * scaling

        def step(i, carry):
            for t in tiles(width):
                put_cols(cols_ref, t, y_ref[t, :], BOTH)
                put_rows(b_ref, t.start, width, y_ref[t, :])
            for t in tiles(width):
                put_cols(a_ref, t, dot_nt(cols_ref[t, fits[0]], cols_ref[:, fits[1]]), LEFT)
            for t in tiles(width):
                y_ref[t, :] = 1.5 * y_ref[t, :] - 0.5 * dot_nn(a_ref[t, :], b_ref[...])
            return carry

        lax.fori_loop(0, ITERS, step, 0)
        q1_ref[0] = y_ref[...].T


def basis_call(rank, left, info, grad, stat, basis, carried):
    width = grad.shape[0]
    own = slot_block(rank, width)
    whole = pl.BlockSpec((width, width), lambda *_: (0, 0))
    state = jax.ShapeDtypeStruct(stat.shape, F32)
    return pl.pallas_call(
        functools.partial(basis_kernel, rank, left),
        grid=(1,),
        out_shape=(state, state),
        in_specs=[SMEM, whole, own, own] + [ANY] * len(carried),
        out_specs=(own, own),
        scratch_shapes=[
            pltpu.VMEM((width, width), F32),
            pltpu.VMEM((width, 4 * width), BF16),
            pltpu.VMEM((width, 3 * width), BF16),
            pltpu.VMEM((3 * width, width), BF16),
        ],
        input_output_aliases={4: 0, 5: 1} if carried else {},
        compiler_params=params(),
        cost_estimate=cost((2 + 2 * ITERS) * 3 * 2 * width**3, 5 * 4 * width**2),
        name="basis_left" if left else "basis_right",
    )(info, grad, stat, basis, *carried)


def pick_kernel(groups, members, count, place_ref, owner_ref, rank_ref, *refs):
    sources, out_ref, sems = refs[:-2], refs[-2], refs[-1]

    def start(i, carry):
        block = place_ref[0] * count + i
        owner = owner_ref[block]
        which = rank_ref[block] * groups + ((owner // members) ^ place_ref[0])
        for n, source in enumerate(sources):

            @pl.when(which == n)
            def _():
                pltpu.make_async_copy(source.at[owner % members], out_ref.at[i], sems.at[i]).start()

        return carry

    def wait(i, carry):
        pltpu.make_async_copy(sources[0].at[0], out_ref.at[i], sems.at[i]).wait()
        return carry

    lax.fori_loop(0, count, start, 0)
    lax.fori_loop(0, count, wait, 0)


def pick(place, owner_device, rank_of, sources, groups, members):
    rows, width = sources[0].shape[1:]
    count = owner_device.shape[0] // groups
    return pl.pallas_call(
        functools.partial(pick_kernel, groups, members, count),
        out_shape=jax.ShapeDtypeStruct((count, rows, width), BF16),
        in_specs=[SMEM] * 3 + [ANY] * len(sources),
        out_specs=ANY,
        scratch_shapes=[pltpu.SemaphoreType.DMA((count,))],
        cost_estimate=cost(0, 4 * count * rows * width),
        name="pick",
    )(place, owner_device, rank_of, *sources)


def local(
    partial_grads,
    owner_device,
    layer_of,
    stat_left,
    stat_right,
    basis_left,
    basis_right,
    moment_first,
    moment_second,
):
    capacity = stat_left.shape[0]
    width = stat_left.shape[1]
    groups = lax.axis_size("dp")
    members = lax.axis_size("mp")
    devices = groups * members
    halves = groups // 2
    grads = partial_grads[0]
    rows = grads.shape[1]
    place = jnp.reshape(lax.axis_index("dp"), (1,))
    own = lax.axis_index(("dp", "mp"))

    def flip(x, bits):
        return lax.ppermute(x, "dp", [(i, i ^ bits) for i in range(groups)])

    block_at, rank_of, counts, layer_at = tables(owner_device, layer_of, devices, capacity)
    own_count = lax.dynamic_index_in_dim(counts, own, keepdims=False)

    infos, from_core = [], []
    for k in range(capacity):
        layer = lax.dynamic_index_in_dim(layer_at, k * devices + own, keepdims=False)
        infos.append(jnp.stack([own_count, groups - 1 - layer]))
        from_core.append(flip(pack(k, place, block_at, grads, halves, members, devices), 1))

    arrived = []
    for k in range(capacity):
        from_x = []
        step = halves // 2
        while step:
            sent = fold(k, step, step, place, block_at, grads, from_core[k], from_x, members, devices)
            from_x.append(flip(sent, 2 * step))
            step //= 2
        ready = fold(k, 0, 1, place, block_at, grads, from_core[k], from_x, members, devices)
        arrived.append(lax.all_to_all(ready[0], "mp", split_axis=0, concat_axis=0, tiled=True))

    sources, gradients, moments = [], [], ()
    for k in range(capacity):
        grad, block_update, *moments = update_call(
            k, infos[k], arrived[k], basis_left, basis_right, moment_first, moment_second, tuple(moments)
        )
        gradients.append(grad)
        pieces = lax.all_to_all(
            block_update.reshape(members, rows, width), "mp", split_axis=0, concat_axis=0, tiled=True
        )
        held = [pieces]
        step = 1
        while step < halves:
            held = held + [flip(part, 2 * step) for part in held]
            step *= 2
        for part in held:
            sources += [part, flip(part, 1)]

    lefts, rights = (), ()
    for k in range(capacity):
        lefts = basis_call(k, True, infos[k], gradients[k], stat_left, basis_left, tuple(lefts))
        rights = basis_call(k, False, infos[k], gradients[k], stat_right, basis_right, tuple(rights))

    update_rows = pick(place, owner_device, rank_of, sources, groups, members)
    return (update_rows, lefts[0], rights[0], lefts[1], rights[1], moments[0], moments[1])


def solution(mesh):
    slots = P(("dp", "mp"), None, None)
    in_specs = (P("dp", None, "mp", None), P(), P()) + (slots,) * 6
    out_specs = (P("dp", "mp", None),) + (slots,) * 6
    return jax.shard_map(local, mesh=mesh, in_specs=in_specs, out_specs=out_specs, check_vma=False)
```

time: 363 us -> 273 us (0.75)
  Pallas kernels: 0 us -> 192 us
  waiting for transfers between devices: 174 us -> 23.9 us
  matrix products: 117 us -> 0 us
  other arithmetic: 31.9 us -> 1.44 us
  starting transfers between devices: 11.8 us -> 37.2 us
  loops' own time: 7.33 us -> 0 us
    pallas_call x0 -> x14, Pallas kernels: none -> 192 us  [the longest x2 67.4 us: pack(): pl.pallas_call(functools.partial(pack_kernel, rank * devices, halves, mem...]
    all_to_all x2 -> x4, waiting for transfers between devices: 174 us -> 0.01 us  [the longest x2 0.01 us: local(): lax.all_to_all(ready[0], 'mp', split_axis=0, concat_axis=0, tiled=True)]
    dot_general x52 -> x0, matrix products: 117 us -> none  [matmul(): jnp.dot(left_side, right_side, precision=PRECISE, preferred_element_type=...]
    ppermute x0 -> x10, waiting for transfers between devices: none -> 23.9 us  [flip(): return lax.ppermute(x, 'dp', [(i, i ^ bits) for i in range(groups)])]
    select_n x6 -> x0, other arithmetic: 23.6 us -> none  [the longest x1 14.2 us: local(): jnp.where(own_live[:, None, None], new_state, old_state)]
    ppermute x0 -> x10, starting transfers between devices: none -> 15.1 us  [flip(): return lax.ppermute(x, 'dp', [(i, i ^ bits) for i in range(groups)])]
    unnamed x5 -> x48, local copies, waits for them, and re-layouts: 0.13 us -> 12.8 us
    all_to_all x2 -> x4, starting transfers between devices: 11.8 us -> 22.1 us  [the longest x2 11.2 us: local(): lax.all_to_all(ready[0], 'mp', split_axis=0, concat_axis=0, tiled=True)]
  transfers between devices with their start and end apart: 2 -> 14, of which waited for: 2 -> 2; matrix products, arithmetic and copies ran while one was open for 4% -> 1% of each run, Pallas kernels for 0% -> 48%
where the time goes in v1:
time: 273 us; the launch traced here: 270 us
  Pallas kernels  192 us (70%)
  starting transfers between devices  37.2 us (14%)
  waiting for transfers between devices  23.9 us (9%)
  local copies, waits for them, and re-layouts  14 us (5%)
    pallas_call x2, Pallas kernels, pack(): pl.pallas_call(functools.partial(pack_kernel, rank * devices, halves, mem...  67.4 us
    pallas_call x4, Pallas kernels, basis_call(): pl.pallas_call(functools.partial(basis_kernel, rank, left), grid=(1,), ou...  50 us
    pallas_call x4, Pallas kernels, fold(): pl.pallas_call(body, grid_spec=pltpu.PrefetchScalarGridSpec(num_scalar_pr...  25.7 us
    pallas_call x1, Pallas kernels, pick(): pl.pallas_call(functools.partial(pick_kernel, groups, members, count), ou...  25.7 us
    ppermute x10, waiting for transfers between devices, flip(): return lax.ppermute(x, 'dp', [(i, i ^ bits) for i in range(groups)])  23.9 us
    pallas_call x2, Pallas kernels, update_call(): pl.pallas_call(functools.partial(update_kernel, rank, rank), grid=(1,), o...  20.6 us
    ppermute x10, starting transfers between devices, flip(): return lax.ppermute(x, 'dp', [(i, i ^ bits) for i in range(groups)])  15.1 us
    unnamed x48, local copies, waits for them, and re-layouts  12.8 us
  transfers between devices with their start and end apart: 14, of which 2 were waited for; matrix products, arithmetic and copies ran while one was open for 1% of the time, Pallas kernels for 48%

profile of v1, /device:TPU:5, one launch (start us, length us, event | category | flops | bytes accessed | tf_op | source)
XLA Modules:
  0.0 270.5 jit_solution(1579920479028693542)
XLA Ops:
  0.6 2.1 tables.1
  2.8 33.7 %pack.2 = bf16[2,8,64,512]{3,2,1,0:T(8,128)(2,1)} custom-call(s32[1]{0:T(128)} %bitcast.place_ref, s32[64]{0:T(128)} %get-tuple-element.30.block_ref, bf16[48,64,512]{2,1,0:T(8,128)(2,1)} %bitcast.6), custom_call_target="tpu_custom_call" | custom-call | bytes 2097152 | tf_op jit(solution)/shard_map/pack/pallas_call | solution.py:93
  36.5 0.7 collective-permute-start
  37.2 33.7 %pack.3 = bf16[2,8,64,512]{3,2,1,0:T(8,128)(2,1)} custom-call(s32[1]{0:T(128)} %bitcast.place_ref, s32[64]{0:T(128)} %get-tuple-element.30.block_ref, bf16[48,64,512]{2,1,0:T(8,128)(2,1)} %bitcast.7), custom_call_target="tpu_custom_call" | custom-call | bytes 2097152 | tf_op jit(solution)/shard_map/pack/pallas_call | solution.py:93
  70.9 0.1 collective-permute-start.5
  71.0 0.0 collective-permute-done.refs_1_
  71.0 0.0 copy-start.14
  71.0 1.0 copy-done.14
  72.0 6.2 %fold.4 = s16[1,8,272,128]{3,2,1,0:T(8,128)(2,1)} custom-call(s32[1]{0:T(128)} %bitcast.place_ref, s32[64]{0:T(128)} %get-tuple-element.30.block_ref, bf16[48,64,512]{2,1,0:T(8,128)(2,1)} %bitcast.8, bf16[2,8,64,512]{3,2,1,0:T(8,128)(2,1)} %copy-done.14), custom_call_target="tpu_custom_call" | custom-call | bytes 2097152 | tf_op jit(solution)/shard_map/fold/pallas_call | solution.py:157
  78.1 1.2 collective-permute-start.1
  79.4 12.7 %collective-permute-done.1.refs_2_ = s16[1,8,272,128]{3,2,1,0:T(8,128)(2,1)S(1)} collective-permute-done((s16[1,8,272,128]{3,2,1,0:T(8,128)(2,1)}, s16[1,8,272,128]{3,2,1,0:T(8,128)(2,1)S(1)}, u32[]{:S(2)}, u32[]{:S(2)}) %collective-permute-start.1) | collective-permute-done | bytes 557088 | tf_op jit(solution)/shard_map/ppermute | solution.py:421
  92.1 0.8 copy-done.16
  92.9 6.7 %fold.5 = s16[1,8,272,128]{3,2,1,0:T(8,128)(2,1)} custom-call(s32[1]{0:T(128)} %bitcast.place_ref, s32[64]{0:T(128)} %get-tuple-element.30.block_ref, bf16[48,64,512]{2,1,0:T(8,128)(2,1)} %bitcast.9, bf16[2,8,64,512]{3,2,1,0:T(8,128)(2,1)} %copy-done.14, s16[1,8,272,128]{3,2,1,0:T(8,128)(2,1)} %copy-done.16), custom_call_target="tpu_custom_call" | custom-call | bytes 2097152 | tf_op jit(solution)/shard_map/fold/pallas_call | solution.py:157
  99.6 5.8 %all-to-all-start = ((s16[8,272,128]{2,1,0:T(8,128)(2,1)}), s16[8,272,128]{2,1,0:T(8,128)(2,1)S(1)}, u32[]{:S(2)}, u32[]{:S(2)}) async-start(s16[8,272,128]{2,1,0:T(8,128)(2,1)} %bitcast.13), calls=%async_computation | async-start | bytes 1114112 | tf_op jit(solution)/shard_map/all_to_all | solution.py:441
  105.3 0.0 collective-permute-done.5.refs_1_
  105.4 1.0 copy-done.13
  106.3 6.2 %fold.6 = s16[1,8,272,128]{3,2,1,0:T(8,128)(2,1)} custom-call(s32[1]{0:T(128)} %bitcast.place_ref, s32[64]{0:T(128)} %get-tuple-element.30.block_ref, bf16[48,64,512]{2,1,0:T(8,128)(2,1)} %bitcast.10, bf16[2,8,64,512]{3,2,1,0:T(8,128)(2,1)} %copy-done.13), custom_call_target="tpu_custom_call" | custom-call | bytes 2097152 | tf_op jit(solution)/shard_map/fold/pallas_call | solution.py:157
  112.5 1.3 collective-permute-start.6
  113.8 11.2 %collective-permute-done.6.refs_2_ = s16[1,8,272,128]{3,2,1,0:T(8,128)(2,1)S(1)} collective-permute-done((s16[1,8,272,128]{3,2,1,0:T(8,128)(2,1)}, s16[1,8,272,128]{3,2,1,0:T(8,128)(2,1)S(1)}, u32[]{:S(2)}, u32[]{:S(2)}) %collective-permute-start.6) | collective-permute-done | bytes 557088 | tf_op jit(solution)/shard_map/ppermute | solution.py:421
  125.0 0.8 copy-done.15
  125.8 6.7 %fold.7 = s16[1,8,272,128]{3,2,1,0:T(8,128)(2,1)} custom-call(s32[1]{0:T(128)} %bitcast.place_ref, s32[64]{0:T(128)} %get-tuple-element.30.block_ref, bf16[48,64,512]{2,1,0:T(8,128)(2,1)} %bitcast.11, bf16[2,8,64,512]{3,2,1,0:T(8,128)(2,1)} %copy-done.13, s16[1,8,272,128]{3,2,1,0:T(8,128)(2,1)} %copy-done.15), custom_call_target="tpu_custom_call" | custom-call | bytes 2097152 | tf_op jit(solution)/shard_map/fold/pallas_call | solution.py:157
  132.5 0.0 all-to-all-done.pay_ref
  132.5 5.4 %all-to-all-start.2 = ((s16[8,272,128]{2,1,0:T(8,128)(2,1)}), s16[8,272,128]{2,1,0:T(8,128)(2,1)S(1)}, u32[]{:S(2)}, u32[]{:S(2)}) async-start(s16[8,272,128]{2,1,0:T(8,128)(2,1)} %bitcast.12), calls=%async_computation.2 | async-start | bytes 1114112 | tf_op jit(solution)/shard_map/all_to_all | solution.py:441
  137.9 0.0 copy-done.23
  138.0 0.6 dynamic_slice.11
  138.5 0.0 copy-done.22
  138.5 0.6 fusion
  139.8 0.7 pad_add_fusion.info_ref
  140.5 0.0 copy-done.3
  140.5 10.2 %update.2 = (f32[512,512]{1,0:T(8,128)S(1)}, bf16[512,512]{1,0:T(8,128)(2,1)}, f32[2,512,512]{2,1,0:T(8,128)}, f32[2,512,512]{2,1,0:T(8,128)}) custom-call(s32[2]{0:T(128)S(1)} %pad_add_fusion.info_ref, s16[8,272,128]{2,1,0:T(8,128)(2,1)S(1)} %all-to-all-done.pay_ref, f32[2,512,512]{2,1,0:T(8,128)S(1)} %copy-done.3, f32[2,512,512]{2,1,0:T(8,128)} %q_ref.7, ...), custom_call_target="tpu_custom_call" | custom-call | flops 4831838208 | bytes 10485760 | tf_op jit(solution)/shard_map/update/pallas_call | solution.py:274
  150.7 1.0 copy-done.11
  151.6 0.0 all-to-all-done.2.pay_ref
  151.6 5.4 %all-to-all-start.1 = ((bf16[8,64,512]{2,1,0:T(8,128)(2,1)}), bf16[8,64,512]{2,1,0:T(8,128)(2,1)}, u32[]{:S(2)}, u32[]{:S(2)}) async-start(bf16[8,64,512]{2,1,0:T(8,128)(2,1)} %bitcast.3), calls=%async_computation.1 | async-start | bytes 1048576 | tf_op jit(solution)/shard_map/all_to_all | solution.py:449
  157.7 0.7 pad_add_fusion.1.info_ref
  158.4 1.6 copy-done.4
  160.0 10.5 %update.3 = (f32[512,512]{1,0:T(8,128)S(1)}, bf16[512,512]{1,0:T(8,128)(2,1)}, f32[2,512,512]{2,1,0:T(8,128)}, f32[2,512,512]{2,1,0:T(8,128)}) custom-call(s32[2]{0:T(128)S(1)} %pad_add_fusion.1.info_ref, s16[8,272,128]{2,1,0:T(8,128)(2,1)S(1)} %all-to-all-done.2.pay_ref, ...), custom_call_target="tpu_custom_call", output_to_operand_aliasing={{2}: (6, {}), {3}: (7, {})} | custom-call | flops 4831838208 | bytes 10485760 | tf_op jit(solution)/shard_map/update/pallas_call | solution.py:274
  170.5 1.0 copy-done.9
  171.5 0.0 all-to-all-done.1.refs_0_
  171.5 5.4 %all-to-all-start.3 = ((bf16[8,64,512]{2,1,0:T(8,128)(2,1)}), bf16[8,64,512]{2,1,0:T(8,128)(2,1)}, u32[]{:S(2)}, u32[]{:S(2)}) async-start(bf16[8,64,512]{2,1,0:T(8,128)(2,1)} %bitcast.5), calls=%async_computation.3 | async-start | bytes 1048576 | tf_op jit(solution)/shard_map/all_to_all | solution.py:449
  177.0 1.6 copy-done.1
  178.5 1.2 copy-done.12
  179.8 12.4 %basis_right.2 = (f32[2,512,512]{2,1,0:T(8,128)}, f32[2,512,512]{2,1,0:T(8,128)}) custom-call(s32[2]{0:T(128)S(1)} %pad_add_fusion.info_ref, f32[512,512]{1,0:T(8,128)S(1)} %copy-done.12, f32[2,512,512]{2,1,0:T(8,128)S(1)} %copy-done.1, f32[2,512,512]{2,1,0:T(8,128)S(1)} %copy-done), custom_call_target="tpu_custom_call" | custom-call | flops 8053063680 | bytes 5242880 | tf_op jit(solution)/shard_map/basis_right/pallas_call | solution.py:342
  192.2 12.6 %basis_left.2 = (f32[2,512,512]{2,1,0:T(8,128)}, f32[2,512,512]{2,1,0:T(8,128)}) custom-call(s32[2]{0:T(128)S(1)} %pad_add_fusion.info_ref, f32[512,512]{1,0:T(8,128)S(1)} %copy-done.12, f32[2,512,512]{2,1,0:T(8,128)S(1)} %copy-done.7, f32[2,512,512]{2,1,0:T(8,128)S(1)} %copy-done.5), custom_call_target="tpu_custom_call" | custom-call | flops 8053063680 | bytes 5242880 | tf_op jit(solution)/shard_map/basis_left/pallas_call | solution.py:342
  204.8 0.0 collective-permute-start.3
  204.8 0.0 all-to-all-done.3.refs_4_
  204.8 1.5 collective-permute-start.8
  206.2 1.6 copy-done.2
  207.8 12.4 %basis_right.3 = (f32[2,512,512]{2,1,0:T(8,128)}, f32[2,512,512]{2,1,0:T(8,128)}) custom-call(s32[2]{0:T(128)S(1)} %pad_add_fusion.1.info_ref, f32[512,512]{1,0:T(8,128)S(1)} %copy-done.10, f32[2,512,512]{2,1,0:T(8,128)S(1)} %copy-done.2, f32[2,512,512]{2,1,0:T(8,128)S(1)} %copy-done, ...), custom_call_target="tpu_custom_call", output_to_operand_aliasing={{0}: (4, {}), {1}: (5, {})} | custom-call | flops 8053063680 | bytes 5242880 | tf_op jit(solution)/shard_map/basis_right/pallas_call | solution.py:342
  220.2 5.1 %collective-permute-start.2 = (bf16[8,64,512]{2,1,0:T(8,128)(2,1)}, bf16[8,64,512]{2,1,0:T(8,128)(2,1)S(1)}, u32[]{:S(2)}, u32[]{:S(2)}) collective-permute-start(bf16[8,64,512]{2,1,0:T(8,128)(2,1)} %all-to-all-done.1.refs_0_), channel_id=1, source_target_pairs={{0,8},{8,0},{16,24},{24,16},{1,9},{9,1},{17,25},{25,17},{2,10},{10... | collective-permute-start | bytes 1572872 | tf_op jit(solution)/shard_map/ppermute | solution.py:421
  225.3 0.0 collective-permute-start.7
  225.3 0.0 collective-permute-done.3.refs_2_
  225.3 0.5 collective-permute-start.4
  225.8 0.0 collective-permute-done.8.refs_6_
  225.8 4.7 %collective-permute-start.9 = (bf16[8,64,512]{2,1,0:T(8,128)(2,1)S(1)}, bf16[8,64,512]{2,1,0:T(8,128)(2,1)S(1)}, u32[]{:S(2)}, u32[]{:S(2)}) collective-permute-start(bf16[8,64,512]{2,1,0:T(8,128)(2,1)S(1)} %collective-permute-done.8.refs_6_), channel_id=1, source_target_pairs={{0,8},{8,0},{16,24},{24,16},{1,9},{9,1},{17,25},{25,17},{2,10},{10... | collective-permute-start | bytes 1572872 | tf_op jit(solution)/shard_map/ppermute | solution.py:421
  230.6 12.6 %basis_left.3 = (f32[2,512,512]{2,1,0:T(8,128)}, f32[2,512,512]{2,1,0:T(8,128)}) custom-call(s32[2]{0:T(128)S(1)} %pad_add_fusion.1.info_ref, f32[512,512]{1,0:T(8,128)S(1)} %copy-done.10, f32[2,512,512]{2,1,0:T(8,128)S(1)} %copy-done.8, f32[2,512,512]{2,1,0:T(8,128)S(1)} %copy-done.6, ...), custom_call_target="tpu_custom_call", output_to_operand_aliasing={{0}: (4, {}), {1}: (5, {})} | custom-call | flops 8053063680 | bytes 5242880 | tf_op jit(solution)/shard_map/basis_left/pallas_call | solution.py:342
  243.2 0.0 collective-permute-done.2.refs_1_
  243.2 0.0 collective-permute-done.7.refs_5_
  243.2 0.0 collective-permute-done.4.refs_3_
  243.2 0.0 collective-permute-done.9.refs_7_
  243.2 0.7 copy-done.18
  244.0 0.2 copy-done.19
  244.2 0.2 copy-done.20
  244.3 0.2 copy-done.21
  244.5 25.7 %pick.1 = bf16[12,64,512]{2,1,0:T(8,128)(2,1)} custom-call(s32[1]{0:T(128)} %bitcast.place_ref, s32[48]{0:T(128)} %owner_ref.3, s32[48]{0:T(128)} %get-tuple-element.27.rank_ref, bf16[8,64,512]{2,1,0:T(8,128)(2,1)} %all-to-all-done.1.refs_0_, bf16[8,64,512]{2,1,0:T(8,128)(2,1)} %copy-done.18, bf16[8,64,512]{2,1,0:T(8,128)(2,1)} %collective-permute-done.3.refs_2_, ...), custom_call_target="tpu_custom_call" | custom-call | bytes 1572864 | tf_op jit(solution)/shard_map/pick/pallas_call | solution.py:387
  (30 shorter events, 0.1 us)
Async XLA Ops:
  36.5 34.5 %collective-permute-start = (bf16[2,8,64,512]{3,2,1,0:T(8,128)(2,1)}, bf16[2,8,64,512]{3,2,1,0:T(8,128)(2,1)S(1)}, u32[]{:S(2)}, u32[]{:S(2)}) collective-permute-start(bf16[2,8,64,512]{3,2,1,0:T(8,128)(2,1)} %pack.2), channel_id=1, source_target_pairs={{0,8},{8,0},{16,24},{24,16},{1,9},{9,1},{17,25},{25,17},{2,10},{10... | collective-permute-start | bytes 3145736 | tf_op jit(solution)/shard_map/ppermute | solution.py:421
  70.9 34.4 %collective-permute-start.5 = (bf16[2,8,64,512]{3,2,1,0:T(8,128)(2,1)}, bf16[2,8,64,512]{3,2,1,0:T(8,128)(2,1)S(1)}, u32[]{:S(2)}, u32[]{:S(2)}) collective-permute-start(bf16[2,8,64,512]{3,2,1,0:T(8,128)(2,1)} %pack.3), channel_id=1, source_target_pairs={{0,8},{8,0},{16,24},{24,16},{1,9},{9,1},{17,25},{25,17},{2,10},{10... | collective-permute-start | bytes 3145736 | tf_op jit(solution)/shard_map/ppermute | solution.py:421
  71.0 1.0 copy-start.14
  78.1 13.9 %collective-permute-start.1 = (s16[1,8,272,128]{3,2,1,0:T(8,128)(2,1)}, s16[1,8,272,128]{3,2,1,0:T(8,128)(2,1)S(1)}, u32[]{:S(2)}, u32[]{:S(2)}) collective-permute-start(s16[1,8,272,128]{3,2,1,0:T(8,128)(2,1)} %fold.4), channel_id=1, source_target_pairs={{0,16},{8,24},{16,0},{24,8},{1,17},{9,25},{17,1},{25,9},{2,18},{10... | collective-permute-start | bytes 1671176 | tf_op jit(solution)/shard_map/ppermute | solution.py:421
  92.1 0.8 copy-start.16
  99.6 32.9 %all-to-all-start = ((s16[8,272,128]{2,1,0:T(8,128)(2,1)}), s16[8,272,128]{2,1,0:T(8,128)(2,1)S(1)}, u32[]{:S(2)}, u32[]{:S(2)}) async-start(s16[8,272,128]{2,1,0:T(8,128)(2,1)} %bitcast.13), calls=%async_computation | async-start | bytes 1114112 | tf_op jit(solution)/shard_map/all_to_all | solution.py:441
  105.4 1.0 copy-start.13
  112.5 25.5 %copy-start.23 = (s32[32]{0:T(128)S(1)}, s32[32]{0:T(128)}, u32[]{:S(2)}) copy-start(s32[32]{0:T(128)} %get-tuple-element.28) | copy-start | bytes 388
  112.5 26.0 %copy-start.22 = (s32[64]{0:T(128)S(1)}, s32[64]{0:T(128)}, u32[]{:S(2)}) copy-start(s32[64]{0:T(128)} %get-tuple-element.29) | copy-start | bytes 772
  112.5 28.0 %copy-start.3 = (f32[2,512,512]{2,1,0:T(8,128)S(1)}, f32[2,512,512]{2,1,0:T(8,128)}, u32[]{:S(2)}) copy-start(f32[2,512,512]{2,1,0:T(8,128)} %q_ref.5) | copy-start | bytes 6291460
  112.5 12.5 %collective-permute-start.6 = (s16[1,8,272,128]{3,2,1,0:T(8,128)(2,1)}, s16[1,8,272,128]{3,2,1,0:T(8,128)(2,1)S(1)}, u32[]{:S(2)}, u32[]{:S(2)}) collective-permute-start(s16[1,8,272,128]{3,2,1,0:T(8,128)(2,1)} %fold.6), channel_id=1, source_target_pairs={{0,16},{8,24},{16,0},{24,8},{1,17},{9,25},{17,1},{25,9},{2,18},{10... | collective-permute-start | bytes 1671176 | tf_op jit(solution)/shard_map/ppermute | solution.py:421
  125.0 0.8 copy-start.15
  132.5 19.1 %all-to-all-start.2 = ((s16[8,272,128]{2,1,0:T(8,128)(2,1)}), s16[8,272,128]{2,1,0:T(8,128)(2,1)S(1)}, u32[]{:S(2)}, u32[]{:S(2)}) async-start(s16[8,272,128]{2,1,0:T(8,128)(2,1)} %bitcast.12), calls=%async_computation.2 | async-start | bytes 1114112 | tf_op jit(solution)/shard_map/all_to_all | solution.py:441
  150.7 1.0 copy-start.11
  151.6 19.9 %all-to-all-start.1 = ((bf16[8,64,512]{2,1,0:T(8,128)(2,1)}), bf16[8,64,512]{2,1,0:T(8,128)(2,1)}, u32[]{:S(2)}, u32[]{:S(2)}) async-start(bf16[8,64,512]{2,1,0:T(8,128)(2,1)} %bitcast.3), calls=%async_computation.1 | async-start | bytes 1048576 | tf_op jit(solution)/shard_map/all_to_all | solution.py:449
  158.4 1.6 copy-start.4
  160.0 16.9 %copy-start = (f32[2,512,512]{2,1,0:T(8,128)S(1)}, f32[2,512,512]{2,1,0:T(8,128)}, u32[]{:S(2)}) copy-start(f32[2,512,512]{2,1,0:T(8,128)} %q_ref.7) | copy-start | bytes 6291460
  170.5 1.0 copy-start.9
  171.5 33.3 %all-to-all-start.3 = ((bf16[8,64,512]{2,1,0:T(8,128)(2,1)}), bf16[8,64,512]{2,1,0:T(8,128)(2,1)}, u32[]{:S(2)}, u32[]{:S(2)}) async-start(bf16[8,64,512]{2,1,0:T(8,128)(2,1)} %bitcast.5), calls=%async_computation.3 | async-start | bytes 1048576 | tf_op jit(solution)/shard_map/all_to_all | solution.py:449
  177.0 1.6 copy-start.1
  178.5 1.2 copy-start.12
  179.8 12.4 %copy-start.5 = (f32[2,512,512]{2,1,0:T(8,128)S(1)}, f32[2,512,512]{2,1,0:T(8,128)}, u32[]{:S(2)}) copy-start(f32[2,512,512]{2,1,0:T(8,128)} %q_ref.5) | copy-start | bytes 6291460
  179.8 12.4 %copy-start.7 = (f32[2,512,512]{2,1,0:T(8,128)S(1)}, f32[2,512,512]{2,1,0:T(8,128)}, u32[]{:S(2)}) copy-start(f32[2,512,512]{2,1,0:T(8,128)} %s_ref.5) | copy-start | bytes 6291460
  192.2 14.1 %copy-start.10 = (f32[512,512]{1,0:T(8,128)S(1)}, f32[512,512]{1,0:T(8,128)}, u32[]{:S(2)}) copy-start(f32[512,512]{1,0:T(8,128)} %copy-done.9) | copy-start | bytes 3145732
  204.8 20.5 %collective-permute-start.3 = (bf16[8,64,512]{2,1,0:T(8,128)(2,1)}, bf16[8,64,512]{2,1,0:T(8,128)(2,1)}, u32[]{:S(2)}, u32[]{:S(2)}) collective-permute-start(bf16[8,64,512]{2,1,0:T(8,128)(2,1)} %all-to-all-done.1.refs_0_), channel_id=1, source_target_pairs={{0,16},{8,24},{16,0},{24,8},{1,17},{9,25},{17,1},{25,9},{2,18},{10... | collective-permute-start | bytes 1572872 | tf_op jit(solution)/shard_map/ppermute | solution.py:421
  204.8 21.0 %collective-permute-start.8 = (bf16[8,64,512]{2,1,0:T(8,128)(2,1)}, bf16[8,64,512]{2,1,0:T(8,128)(2,1)S(1)}, u32[]{:S(2)}, u32[]{:S(2)}) collective-permute-start(bf16[8,64,512]{2,1,0:T(8,128)(2,1)} %all-to-all-done.3.refs_4_), channel_id=1, source_target_pairs={{0,16},{8,24},{16,0},{24,8},{1,17},{9,25},{17,1},{25,9},{2,18},{10... | collective-permute-start | bytes 1572872 | tf_op jit(solution)/shard_map/ppermute | solution.py:421
  206.2 1.6 copy-start.2
  207.8 22.7 %copy-start.6 = (f32[2,512,512]{2,1,0:T(8,128)S(1)}, f32[2,512,512]{2,1,0:T(8,128)}, u32[]{:S(2)}) copy-start(f32[2,512,512]{2,1,0:T(8,128)} %q_ref.5) | copy-start | bytes 6291460
  207.8 22.7 %copy-start.8 = (f32[2,512,512]{2,1,0:T(8,128)S(1)}, f32[2,512,512]{2,1,0:T(8,128)}, u32[]{:S(2)}) copy-start(f32[2,512,512]{2,1,0:T(8,128)} %s_ref.5) | copy-start | bytes 6291460
  220.2 23.0 %collective-permute-start.2 = (bf16[8,64,512]{2,1,0:T(8,128)(2,1)}, bf16[8,64,512]{2,1,0:T(8,128)(2,1)S(1)}, u32[]{:S(2)}, u32[]{:S(2)}) collective-permute-start(bf16[8,64,512]{2,1,0:T(8,128)(2,1)} %all-to-all-done.1.refs_0_), channel_id=1, source_target_pairs={{0,8},{8,0},{16,24},{24,16},{1,9},{9,1},{17,25},{25,17},{2,10},{10... | collective-permute-start | bytes 1572872 | tf_op jit(solution)/shard_map/ppermute | solution.py:421
  225.3 17.9 %collective-permute-start.7 = (bf16[8,64,512]{2,1,0:T(8,128)(2,1)}, bf16[8,64,512]{2,1,0:T(8,128)(2,1)S(1)}, u32[]{:S(2)}, u32[]{:S(2)}) collective-permute-start(bf16[8,64,512]{2,1,0:T(8,128)(2,1)} %all-to-all-done.3.refs_4_), channel_id=1, source_target_pairs={{0,8},{8,0},{16,24},{24,16},{1,9},{9,1},{17,25},{25,17},{2,10},{10... | collective-permute-start | bytes 1572872 | tf_op jit(solution)/shard_map/ppermute | solution.py:421
  225.3 17.9 %collective-permute-start.4 = (bf16[8,64,512]{2,1,0:T(8,128)(2,1)}, bf16[8,64,512]{2,1,0:T(8,128)(2,1)S(1)}, u32[]{:S(2)}, u32[]{:S(2)}) collective-permute-start(bf16[8,64,512]{2,1,0:T(8,128)(2,1)} %collective-permute-done.3.refs_2_), channel_id=1, source_target_pairs={{0,8},{8,0},{16,24},{24,16},{1,9},{9,1},{17,25},{25,17},{2,10},{10... | collective-permute-start | bytes 1572872 | tf_op jit(solution)/shard_map/ppermute | solution.py:421
  225.8 17.4 %copy-start.17 = (bf16[8,64,512]{2,1,0:T(8,128)(2,1)}, bf16[8,64,512]{2,1,0:T(8,128)(2,1)S(1)}, u32[]{:S(2)}) copy-start(bf16[8,64,512]{2,1,0:T(8,128)(2,1)S(1)} %collective-permute-done.8.refs_6_) | copy-start | bytes 1572868
  225.8 17.4 %collective-permute-start.9 = (bf16[8,64,512]{2,1,0:T(8,128)(2,1)S(1)}, bf16[8,64,512]{2,1,0:T(8,128)(2,1)S(1)}, u32[]{:S(2)}, u32[]{:S(2)}) collective-permute-start(bf16[8,64,512]{2,1,0:T(8,128)(2,1)S(1)} %collective-permute-done.8.refs_6_), channel_id=1, source_target_pairs={{0,8},{8,0},{16,24},{24,16},{1,9},{9,1},{17,25},{25,17},{2,10},{10... | collective-permute-start | bytes 1572872 | tf_op jit(solution)/shard_map/ppermute | solution.py:421
  243.2 0.8 copy-start.18
  243.2 1.0 copy-start.19
  243.2 1.1 copy-start.20
  243.2 1.3 copy-start.21

commit v2 on v1

--- a/solution.py
+++ b/solution.py
@@ -21,7 +21,7 @@
 SMEM = pl.BlockSpec(memory_space=pltpu.SMEM)
 
 
-def params(limit=48 * MIB):
+def params(limit=60 * MIB):
     return pltpu.CompilerParams(vmem_limit_bytes=limit)
 
 
@@ -29,74 +29,71 @@
     return pl.CostEstimate(flops=int(flops), bytes_accessed=int(moved), transcendentals=0)
 
 
-def table_kernel(devices, capacity, owner_ref, layer_ref, block_ref, rank_ref, count_ref, depth_ref):
-    def clear(d, carry):
+def gather(base, halves, members, place_ref, block_ref, grads_ref, out_ref, sems):
+    copies = []
+    for i in range(halves * members):
+        group = place_ref[0] ^ (2 * (i // members) + 1)
+        block = block_ref[base + group * members + i % members]
+        copies.append(
+            pltpu.make_async_copy(grads_ref.at[block], out_ref.at[i // members, i % members], sems.at[i])
+        )
+        copies[-1].start()
+    for copy in copies:
+        copy.wait()
+
+
+def route_kernel(
+    capacity, halves, members, owner_ref, layer_ref, place_ref, grads_ref,
+    block_ref, rank_ref, count_ref, depth_ref, out_ref, sems,
+):
+    devices = 2 * halves * members
+    for d in range(devices):
         count_ref[d] = 0
         for k in range(capacity):
             block_ref[k * devices + d] = 0
             depth_ref[k * devices + d] = 0
-        return carry
-
-    lax.fori_loop(0, devices, clear, 0)
-
-    def place(b, carry):
+    for b in range(owner_ref.shape[0]):
         owner = owner_ref[b]
         rank = count_ref[owner]
         rank_ref[b] = rank
         block_ref[rank * devices + owner] = b
         depth_ref[rank * devices + owner] = layer_ref[b]
         count_ref[owner] = rank + 1
-        return carry
-
-    lax.fori_loop(0, owner_ref.shape[0], place, 0)
-
-
-def tables(owner_device, layer_of, devices, capacity):
-    blocks = owner_device.shape[0]
+    gather(0, halves, members, place_ref, block_ref, grads_ref, out_ref, sems)
+
+
+def route(owner_device, layer_of, place, grads, capacity, halves, members):
+    devices = 2 * halves * members
+    packed = (halves, members) + grads.shape[1:]
     flat = jax.ShapeDtypeStruct((capacity * devices,), jnp.int32)
     return pl.pallas_call(
-        functools.partial(table_kernel, devices, capacity),
+        functools.partial(route_kernel, capacity, halves, members),
         out_shape=(
             flat,
-            jax.ShapeDtypeStruct((blocks,), jnp.int32),
+            jax.ShapeDtypeStruct(owner_device.shape, jnp.int32),
             jax.ShapeDtypeStruct((devices,), jnp.int32),
             flat,
+            jax.ShapeDtypeStruct(packed, grads.dtype),
         ),
-        in_specs=[SMEM, SMEM],
-        out_specs=(SMEM,) * 4,
-        name="tables",
-    )(owner_device, layer_of)
-
-
-def pack_kernel(base, halves, members, place_ref, block_ref, grads_ref, out_ref, sems):
-    def piece(i):
-        group = place_ref[0] ^ (2 * (i // members) + 1)
-        block = block_ref[base + group * members + i % members]
-        return pltpu.make_async_copy(
-            grads_ref.at[block], out_ref.at[i // members, i % members], sems.at[i]
-        )
-
-    def start(i, carry):
-        piece(i).start()
-        return carry
-
-    def wait(i, carry):
-        piece(i).wait()
-        return carry
-
-    lax.fori_loop(0, halves * members, start, 0)
-    lax.fori_loop(0, halves * members, wait, 0)
-
-
-def pack(rank, place, block_at, grads, halves, members, devices):
-    rows, width = grads.shape[1:]
-    return pl.pallas_call(
-        functools.partial(pack_kernel, rank * devices, halves, members),
-        out_shape=jax.ShapeDtypeStruct((halves, members, rows, width), grads.dtype),
+        in_specs=[SMEM, SMEM, SMEM, ANY],
+        out_specs=(SMEM,) * 4 + (pl.BlockSpec(memory_space=pltpu.VMEM),),
+        scratch_shapes=[pltpu.SemaphoreType.DMA((halves * members,))],
+        compiler_params=params(),
+        cost_estimate=cost(0, 4 * math.prod(packed)),
+        name="route",
+    )(owner_device, layer_of, place, grads)
+
+
+def pack(rank, place, block_at, grads, halves, members):
+    packed = (halves, members) + grads.shape[1:]
+    return pl.pallas_call(
+        functools.partial(gather, rank * 2 * halves * members, halves, members),
+        out_shape=jax.ShapeDtypeStruct(packed, grads.dtype),
         in_specs=[SMEM, SMEM, ANY],
-        out_specs=ANY,
+        out_specs=pl.BlockSpec(memory_space=pltpu.VMEM),
         scratch_shapes=[pltpu.SemaphoreType.DMA((halves * members,))],
-        cost_estimate=cost(0, 4 * halves * members * rows * width),
+        compiler_params=params(),
+        cost_estimate=cost(0, 4 * math.prod(packed)),
         name="pack",
     )(place, block_at, grads)
 
@@ -112,58 +109,63 @@
     return part.astype(jnp.int32).astype(F32) * scale
 
 
-def fold_kernel(earlier, tables_refs, raw_ref, core_ref, *refs):
-    out_ref = refs[earlier]
+def fold_kernel(base, first, members, place_ref, block_ref, grads_ref, core_ref, *refs):
+    earlier, (out_ref, raw_ref, sems) = refs[:-3], refs[-3:]
+    count = out_ref.shape[0]
     rows, width = raw_ref.shape[1:]
     panels = width // LANES
-    total = raw_ref[0].astype(F32) + core_ref[0, 0].astype(F32)
-    if earlier:
-        parts = []
-        scales = [decode_scale(refs[n], (0, 0), rows, panels) for n in range(earlier)]
-        for p in range(panels):
-            part = total[:, p * LANES : (p + 1) * LANES]
-            for n in range(earlier):
-                part = part + decode(refs[n], (0, 0), rows, p, scales[n])
-            parts.append(part)
-        total = jnp.concatenate(parts, axis=1)
-    largest = jnp.max(jnp.abs(total), axis=1, keepdims=True)
-    power = jnp.floor(14.99 - jnp.log2(jnp.maximum(largest, 1e-26)))
-    scaled = jnp.round(total * jnp.exp2(power)).astype(jnp.int32)
-    for p in range(panels):
-        out_ref[0, 0, pl.ds(p * rows, rows), :] = scaled[:, p * LANES : (p + 1) * LANES].astype(jnp.int16)
-    wide = jnp.broadcast_to(power, (rows, LANES))
-    if rows < LANES:
-        wide = jnp.concatenate([wide, jnp.zeros((LANES - rows, LANES), F32)], axis=0)
-    out_ref[0, 0, pl.ds(panels * rows, TAIL), :] = wide.T[:TAIL].astype(jnp.int32).astype(jnp.int16)
-
-
-def fold(rank, first, count, place, block_at, grads, from_core, from_x, members, devices):
+    copies = []
+    for i in range(count * members):
+        group = place_ref[0] ^ (2 * (first + i // members))
+        block = block_ref[base + group * members + i % members]
+        copies.append(pltpu.make_async_copy(grads_ref.at[block], raw_ref.at[i], sems.at[i]))
+        copies[-1].start()
+    for copy in copies:
+        copy.wait()
+
+    def piece(i, carry):
+        at = (i // members, i % members)
+        total = raw_ref[i].astype(F32) + core_ref[at].astype(F32)
+        parts = [total[:, p * LANES : (p + 1) * LANES] for p in range(panels)]
+        for ref in earlier:
+            scale = decode_scale(ref, at, rows, panels)
+            parts = [part + decode(ref, at, rows, p, scale) for p, part in enumerate(parts)]
+        largest = functools.reduce(jnp.maximum, [jnp.abs(part) for part in parts])
+        largest = jnp.max(largest, axis=1, keepdims=True)
+        power = jnp.floor(14.99 - jnp.log2(jnp.maximum(largest, 1e-26)))
+        wide = jnp.broadcast_to(power, (rows, LANES))
+        scale = jnp.exp2(wide)
+        for p, part in enumerate(parts):
+            out_ref[at + (pl.ds(p * rows, rows), slice(None))] = (
+                jnp.round(part * scale).astype(jnp.int32).astype(jnp.int16)
+            )
+        if rows < LANES:
+            wide = jnp.concatenate([wide, jnp.zeros((LANES - rows, LANES), F32)], axis=0)
+        out_ref[at + (pl.ds(panels * rows, TAIL), slice(None))] = (
+            wide.T[:TAIL].astype(jnp.int32).astype(jnp.int16)
+        )
+        return carry
+
+    lax.fori_loop(0, count * members, piece, 0)
+
+
+def fold(rank, first, count, place, block_at, grads, from_core, from_x, members):
     rows, width = grads.shape[1:]
     tall = (width // LANES) * rows + TAIL
-
-    def raw_map(i, place_ref, block_ref):
-        group = place_ref[0] ^ (2 * (first + i // members))
-        return (block_ref[rank * devices + group * members + i % members], 0, 0)
-
-    def sent_map(i, place_ref, block_ref):
-        return (first + i // members, i % members, 0, 0)
-
-    def out_map(i, place_ref, block_ref):
-        return (i // members, i % members, 0, 0)
-
-    def body(place_ref, block_ref, *refs):
-        fold_kernel(len(from_x), None, *refs)
-
-    return pl.pallas_call(
-        body,
-        grid_spec=pltpu.PrefetchScalarGridSpec(
-            num_scalar_prefetch=2,
-            grid=(count * members,),
-            in_specs=[pl.BlockSpec((1, rows, width), raw_map), pl.BlockSpec((1, 1, rows, width), sent_map)]
-            + [pl.BlockSpec((1, 1, tall, LANES), sent_map) for _ in from_x],
-            out_specs=pl.BlockSpec((1, 1, tall, LANES), out_map),
-        ),
+    devices = 2 * from_core.shape[0] * members
+    at = first // count
+    return pl.pallas_call(
+        functools.partial(fold_kernel, rank * devices, first, members),
+        grid=(1,),
+        in_specs=[SMEM, SMEM, ANY, pl.BlockSpec((count, members, rows, width), lambda i: (at, 0, 0, 0))]
+        + [pl.BlockSpec((count, members, tall, LANES), lambda i: (at, 0, 0, 0)) for _ in from_x],
+        out_specs=pl.BlockSpec((count, members, tall, LANES), lambda i: (0, 0, 0, 0)),
         out_shape=jax.ShapeDtypeStruct((count, members, tall, LANES), jnp.int16),
+        scratch_shapes=[
+            pltpu.VMEM((count * members, rows, width), grads.dtype),
+            pltpu.SemaphoreType.DMA((count * members,)),
+        ],
+        compiler_params=params(),
         cost_estimate=cost(0, 8 * count * members * rows * width),
         name="fold",
     )(place, block_at, grads, from_core, *from_x)
@@ -205,13 +207,13 @@
     return [pl.ds(s, size) for s in range(0, height, size)]
 
 
-def update_kernel(rank, slot, info_ref, pay_ref, ql_ref, qr_ref, m_ref, v_ref, *refs):
+def update_kernel(rank, base, place_ref, count_ref, depth_ref, pay_ref, ql_ref, qr_ref, m_ref, v_ref, *refs):
     g_ref, u_ref, m1_ref, v1_ref, qlt_ref, ql3_ref, qrs_ref, qrp_ref, bs_ref, as_ref, mrot_ref = refs[-11:]
     width = g_ref.shape[0]
     members = pay_ref.shape[0]
     rows = width // members
     panels = width // LANES
-    live = info_ref[0] > rank
+    live = count_ref[place_ref[1]] > rank
 
     @pl.when(jnp.logical_not(live))
     def _():
@@ -250,7 +252,7 @@
             put_rows(bs_ref, t.start, width, mrot_ref[t, :] / (jnp.sqrt(second) + 1e-08))
         put_cols(ql3_ref, slice(None), ql_ref[0], LEFT)
         put_cols(qrp_ref, slice(None), qr_ref[0], (0, 1, 0))
-        depth = info_ref[1].astype(F32)
+        depth = (place_ref[2] - 1 - depth_ref[base + place_ref[1]]).astype(F32)
         factor = jnp.exp(SHRINK * jnp.full((1, width), depth, F32))
         for t in tiles(width):
             put_cols(as_ref, t, dot_nn(ql3_ref[t, :], bs_ref[...]), LEFT)
@@ -267,12 +269,12 @@
     own = slot_block(rank, width)
     whole = pl.BlockSpec((width, width), lambda *_: (0, 0))
     state = jax.ShapeDtypeStruct(m.shape, F32)
-    operands = [info, pay, ql, qr, m, v] + list(carried)
-    aliases = {6: 2, 7: 3} if carried else {}
+    operands = list(info) + [pay, ql, qr, m, v] + list(carried)
+    aliases = {8: 2, 9: 3} if carried else {}
     wide = lambda n: pltpu.VMEM((width, n * width), BF16)
     tall = pltpu.VMEM((3 * width, width), BF16)
     return pl.pallas_call(
-        functools.partial(update_kernel, rank, rank),
+        functools.partial(update_kernel, rank, rank * info[1].shape[0]),
         grid=(1,),
         out_shape=(
             jax.ShapeDtypeStruct((width, width), F32),
@@ -280,7 +282,7 @@
             state,
             state,
         ),
-        in_specs=[SMEM, pl.BlockSpec(pay.shape, lambda *_: (0, 0, 0)), own, own, own, own] + [ANY] * len(carried),
+        in_specs=[SMEM] * 3 + [pl.BlockSpec(pay.shape, lambda *_: (0, 0, 0)), own, own, own, own] + [ANY] * len(carried),
         out_specs=(whole, whole, own, own),
         scratch_shapes=[wide(3), wide(3), tall, wide(3), tall, wide(3), pltpu.VMEM((width, width), F32)],
         input_output_aliases=aliases,
@@ -290,10 +292,10 @@
     )(*operands)
 
 
-def basis_kernel(rank, left, info_ref, g_ref, s_ref, q_ref, *refs):
+def basis_kernel(rank, left, place_ref, count_ref, g_ref, s_ref, q_ref, *refs):
     s1_ref, q1_ref, y_ref, cols_ref, a_ref, b_ref = refs[-6:]
     width = g_ref.shape[0]
-    live = info_ref[0] > rank
+    live = count_ref[place_ref[1]] > rank
     fits = pl.ds(0, 3 * width), pl.ds(width, 3 * width)
 
     @pl.when(jnp.logical_not(live))
@@ -343,7 +345,7 @@
         functools.partial(basis_kernel, rank, left),
         grid=(1,),
         out_shape=(state, state),
-        in_specs=[SMEM, whole, own, own] + [ANY] * len(carried),
+        in_specs=[SMEM, SMEM, whole, own, own] + [ANY] * len(carried),
         out_specs=(own, own),
         scratch_shapes=[
             pltpu.VMEM((width, width), F32),
@@ -351,11 +353,11 @@
             pltpu.VMEM((width, 3 * width), BF16),
             pltpu.VMEM((3 * width, width), BF16),
         ],
-        input_output_aliases={4: 0, 5: 1} if carried else {},
+        input_output_aliases={5: 0, 6: 1} if carried else {},
         compiler_params=params(),
         cost_estimate=cost((2 + 2 * ITERS) * 3 * 2 * width**3, 5 * 4 * width**2),
         name="basis_left" if left else "basis_right",
-    )(info, grad, stat, basis, *carried)
+    )(*info[:2], grad, stat, basis, *carried)
 
 
 def pick_kernel(groups, members, count, place_ref, owner_ref, rank_ref, *refs):
@@ -388,8 +390,9 @@
         functools.partial(pick_kernel, groups, members, count),
         out_shape=jax.ShapeDtypeStruct((count, rows, width), BF16),
         in_specs=[SMEM] * 3 + [ANY] * len(sources),
-        out_specs=ANY,
+        out_specs=pl.BlockSpec(memory_space=pltpu.VMEM),
         scratch_shapes=[pltpu.SemaphoreType.DMA((count,))],
+        compiler_params=params(),
         cost_estimate=cost(0, 4 * count * rows * width),
         name="pick",
     )(place, owner_device, rank_of, *sources)
@@ -410,40 +413,38 @@
     width = stat_left.shape[1]
     groups = lax.axis_size("dp")
     members = lax.axis_size("mp")
-    devices = groups * members
     halves = groups // 2
     grads = partial_grads[0]
     rows = grads.shape[1]
-    place = jnp.reshape(lax.axis_index("dp"), (1,))
     own = lax.axis_index(("dp", "mp"))
+    place = jnp.stack([lax.axis_index("dp"), own, groups])
 
     def flip(x, bits):
         return lax.ppermute(x, "dp", [(i, i ^ bits) for i in range(groups)])
 
-    block_at, rank_of, counts, layer_at = tables(owner_device, layer_of, devices, capacity)
-    own_count = lax.dynamic_index_in_dim(counts, own, keepdims=False)
-
-    infos, from_core = [], []
-    for k in range(capacity):
-        layer = lax.dynamic_index_in_dim(layer_at, k * devices + own, keepdims=False)
-        infos.append(jnp.stack([own_count, groups - 1 - layer]))
-        from_core.append(flip(pack(k, place, block_at, grads, halves, members, devices), 1))
+    block_at, rank_of, counts, layer_at, packed = route(
+        owner_device, layer_of, place, grads, capacity, halves, members
+    )
+    info = (place, counts, layer_at)
+    from_core = [flip(packed, 1)]
+    for k in range(1, capacity):
+        from_core.append(flip(pack(k, place, block_at, grads, halves, members), 1))
 
     arrived = []
     for k in range(capacity):
         from_x = []
         step = halves // 2
         while step:
-            sent = fold(k, step, step, place, block_at, grads, from_core[k], from_x, members, devices)
+            sent = fold(k, step, step, place, block_at, grads, from_core[k], from_x, members)
             from_x.append(flip(sent, 2 * step))
             step //= 2
-        ready = fold(k, 0, 1, place, block_at, grads, from_core[k], from_x, members, devices)
+        ready = fold(k, 0, 1, place, block_at, grads, from_core[k], from_x, members)
         arrived.append(lax.all_to_all(ready[0], "mp", split_axis=0, concat_axis=0, tiled=True))
 
     sources, gradients, moments = [], [], ()
     for k in range(capacity):
         grad, block_update, *moments = update_call(
-            k, infos[k], arrived[k], basis_left, basis_right, moment_first, moment_second, tuple(moments)
+            k, info, arrived[k], basis_left, basis_right, moment_first, moment_second, tuple(moments)
         )
         gradients.append(grad)
         pieces = lax.all_to_all(
@@ -459,8 +460,8 @@
 
     lefts, rights = (), ()
     for k in range(capacity):
-        lefts = basis_call(k, True, infos[k], gradients[k], stat_left, basis_left, tuple(lefts))
-        rights = basis_call(k, False, infos[k], gradients[k], stat_right, basis_right, tuple(rights))
+        lefts = basis_call(k, True, info, gradients[k], stat_left, basis_left, tuple(lefts))
+        rights = basis_call(k, False, info, gradients[k], stat_right, basis_right, tuple(rights))
 
     update_rows = pick(place, owner_device, rank_of, sources, groups, members)
     return (update_rows, lefts[0], rights[0], lefts[1], rights[1], moments[0], moments[1])

time: 273 us -> 177 us (0.65)
  Pallas kernels: 192 us -> 106 us
  local copies, waits for them, and re-layouts: 14 us -> 4.69 us
  waiting for transfers between devices: 23.9 us -> 30.5 us
  starting transfers between devices: 37.2 us -> 33 us
    pallas_call x9 -> x8, Pallas kernels: 116 us -> 47.7 us  [the longest x2 22.1 us: update_call(): pl.pallas_call(functools.partial(update_kernel, rank, rank * info[1].shap...]
    pallas_call x1, Pallas kernels: 25.7 us -> 2.89 us  [pick(): pl.pallas_call(functools.partial(pick_kernel, groups, members, count), ou...]
    unnamed x48 -> x26, local copies, waits for them, and re-layouts: 12.8 us -> 4.69 us
    ppermute x10, waiting for transfers between devices: 23.9 us -> 29.8 us  [flip(): return lax.ppermute(x, 'dp', [(i, i ^ bits) for i in range(groups)])]
    ppermute x10, starting transfers between devices: 15.1 us -> 9.43 us  [flip(): return lax.ppermute(x, 'dp', [(i, i ^ bits) for i in range(groups)])]
    pallas_call x4, Pallas kernels: 50 us -> 55.2 us  [basis_call(): pl.pallas_call(functools.partial(basis_kernel, rank, left), grid=(1,), ou...]
  transfers between devices with their start and end apart: 14 -> 14, of which waited for: 2 -> 5; matrix products, arithmetic and copies ran while one was open for 1% -> 0% of each run, Pallas kernels for 48% -> 57%
where the time goes in v2:
time: 177 us; the launch traced here: 176 us
  Pallas kernels  106 us (60%)
  starting transfers between devices  33 us (19%)
  waiting for transfers between devices  30.5 us (17%)
  local copies, waits for them, and re-layouts  4.69 us (3%)
    pallas_call x4, Pallas kernels, basis_call(): pl.pallas_call(functools.partial(basis_kernel, rank, left), grid=(1,), ou...  55.2 us
    ppermute x10, waiting for transfers between devices, flip(): return lax.ppermute(x, 'dp', [(i, i ^ bits) for i in range(groups)])  29.8 us
    pallas_call x2, Pallas kernels, update_call(): pl.pallas_call(functools.partial(update_kernel, rank, rank * info[1].shap...  22.1 us
    pallas_call x4, Pallas kernels, fold(): pl.pallas_call(functools.partial(fold_kernel, rank * devices, first, memb...  19 us
    all_to_all x2, starting transfers between devices, local(): lax.all_to_all(block_update.reshape(members, rows, width), 'mp', split_ax...  12.4 us
    all_to_all x2, starting transfers between devices, local(): lax.all_to_all(ready[0], 'mp', split_axis=0, concat_axis=0, tiled=True)  11.2 us
    ppermute x10, starting transfers between devices, flip(): return lax.ppermute(x, 'dp', [(i, i ^ bits) for i in range(groups)])  9.43 us
    unnamed x26, local copies, waits for them, and re-layouts  4.69 us
  transfers between devices with their start and end apart: 14, of which 5 were waited for; matrix products, arithmetic and copies ran while one was open for 0% of the time, Pallas kernels for 57%

profile of v2, /device:TPU:5, one launch (start us, length us, event | category | flops | bytes accessed | tf_op | source)
XLA Modules:
  0.0 175.7 jit_solution(17486835591074214719)
XLA Ops:
  0.6 0.6 pad_add_fusion.place_ref
  1.2 3.4 %route.1 = (s32[64]{0:T(128)}, s32[48]{0:T(128)}, s32[32]{0:T(128)}, s32[64]{0:T(128)}, bf16[2,8,64,512]{3,2,1,0:T(8,128)(2,1)}) custom-call(s32[48]{0:T(128)} %owner_ref.3, s32[48]{0:T(128)} %layer_ref.1, s32[3]{0:T(128)} %pad_add_fusion.place_ref, bf16[48,64,512]{2,1,0:T(8,128)(2,1)} %bitcast.7), custom_call_target="tpu_custom_call" | custom-call | bytes 2097152 | tf_op jit(solution)/shard_map/route/pallas_call | solution.py:69
  4.7 0.7 collective-permute-start
  5.4 3.2 %pack.1 = bf16[2,8,64,512]{3,2,1,0:T(8,128)(2,1)} custom-call(s32[3]{0:T(128)} %pad_add_fusion.place_ref, s32[64]{0:T(128)} %get-tuple-element.31.block_ref, bf16[48,64,512]{2,1,0:T(8,128)(2,1)} %bitcast.8), custom_call_target="tpu_custom_call" | custom-call | bytes 2097152 | tf_op jit(solution)/shard_map/pack/pallas_call | solution.py:89
  8.6 0.1 collective-permute-start.5
  8.7 0.0 collective-permute-done.core_ref
  8.7 0.0 copy-start.1
  8.7 1.0 copy-done.1
  9.7 4.3 %fold.4 = s16[1,8,272,128]{3,2,1,0:T(8,128)(2,1)} custom-call(s32[3]{0:T(128)} %pad_add_fusion.place_ref, s32[64]{0:T(128)} %get-tuple-element.31.block_ref, bf16[48,64,512]{2,1,0:T(8,128)(2,1)} %bitcast.9, bf16[2,8,64,512]{3,2,1,0:T(8,128)(2,1)} %copy-done.1), custom_call_target="tpu_custom_call" | custom-call | bytes 2097152 | tf_op jit(solution)/shard_map/fold/pallas_call | solution.py:157
  14.0 1.3 collective-permute-start.1
  15.3 12.7 %collective-permute-done.1.refs_0_ = s16[1,8,272,128]{3,2,1,0:T(8,128)(2,1)S(1)} collective-permute-done((s16[1,8,272,128]{3,2,1,0:T(8,128)(2,1)}, s16[1,8,272,128]{3,2,1,0:T(8,128)(2,1)S(1)}, u32[]{:S(2)}, u32[]{:S(2)}) %collective-permute-start.1) | collective-permute-done | bytes 557088 | tf_op jit(solution)/shard_map/ppermute | solution.py:423
  28.0 0.0 copy-start.5
  28.0 0.8 copy-done.5
  28.8 5.1 %fold.5 = s16[1,8,272,128]{3,2,1,0:T(8,128)(2,1)} custom-call(s32[3]{0:T(128)} %pad_add_fusion.place_ref, s32[64]{0:T(128)} %get-tuple-element.31.block_ref, bf16[48,64,512]{2,1,0:T(8,128)(2,1)} %bitcast.10, bf16[2,8,64,512]{3,2,1,0:T(8,128)(2,1)} %copy-done.1, s16[1,8,272,128]{3,2,1,0:T(8,128)(2,1)} %copy-done.5), custom_call_target="tpu_custom_call" | custom-call | bytes 2097152 | tf_op jit(solution)/shard_map/fold/pallas_call | solution.py:157
  33.9 5.8 %all-to-all-start = ((s16[8,272,128]{2,1,0:T(8,128)(2,1)}), s16[8,272,128]{2,1,0:T(8,128)(2,1)S(1)}, u32[]{:S(2)}, u32[]{:S(2)}) async-start(s16[8,272,128]{2,1,0:T(8,128)(2,1)} %bitcast.13), calls=%async_computation | async-start | bytes 1114112 | tf_op jit(solution)/shard_map/all_to_all | solution.py:442
  39.7 0.0 collective-permute-done.5.core_ref
  39.7 0.0 copy-start
  39.7 1.0 copy-done
  40.7 4.4 %fold.6 = s16[1,8,272,128]{3,2,1,0:T(8,128)(2,1)} custom-call(s32[3]{0:T(128)} %pad_add_fusion.place_ref, s32[64]{0:T(128)} %get-tuple-element.31.block_ref, bf16[48,64,512]{2,1,0:T(8,128)(2,1)} %bitcast.11, bf16[2,8,64,512]{3,2,1,0:T(8,128)(2,1)} %copy-done), custom_call_target="tpu_custom_call" | custom-call | bytes 2097152 | tf_op jit(solution)/shard_map/fold/pallas_call | solution.py:157
  45.1 1.3 collective-permute-start.6
  46.4 11.2 %collective-permute-done.6.refs_0_ = s16[1,8,272,128]{3,2,1,0:T(8,128)(2,1)S(1)} collective-permute-done((s16[1,8,272,128]{3,2,1,0:T(8,128)(2,1)}, s16[1,8,272,128]{3,2,1,0:T(8,128)(2,1)S(1)}, u32[]{:S(2)}, u32[]{:S(2)}) %collective-permute-start.6) | collective-permute-done | bytes 557088 | tf_op jit(solution)/shard_map/ppermute | solution.py:423
  57.6 0.0 copy-start.4
  57.6 0.8 copy-done.4
  58.4 5.1 %fold.7 = s16[1,8,272,128]{3,2,1,0:T(8,128)(2,1)} custom-call(s32[3]{0:T(128)} %pad_add_fusion.place_ref, s32[64]{0:T(128)} %get-tuple-element.31.block_ref, bf16[48,64,512]{2,1,0:T(8,128)(2,1)} %bitcast.12, bf16[2,8,64,512]{3,2,1,0:T(8,128)(2,1)} %copy-done, s16[1,8,272,128]{3,2,1,0:T(8,128)(2,1)} %copy-done.4), custom_call_target="tpu_custom_call" | custom-call | bytes 2097152 | tf_op jit(solution)/shard_map/fold/pallas_call | solution.py:157
  63.6 0.0 all-to-all-done.pay_ref
  63.6 0.0 copy-start.6
  63.6 5.4 %all-to-all-start.2 = ((s16[8,272,128]{2,1,0:T(8,128)(2,1)}), s16[8,272,128]{2,1,0:T(8,128)(2,1)S(1)}, u32[]{:S(2)}, u32[]{:S(2)}) async-start(s16[8,272,128]{2,1,0:T(8,128)(2,1)} %bitcast.14), calls=%async_computation.2 | async-start | bytes 1114112 | tf_op jit(solution)/shard_map/all_to_all | solution.py:442
  69.1 0.0 copy-done.6
  69.1 11.0 %update.2 = (f32[512,512]{1,0:T(8,128)}, bf16[512,512]{1,0:T(8,128)(2,1)}, f32[2,512,512]{2,1,0:T(8,128)}, f32[2,512,512]{2,1,0:T(8,128)}) custom-call(s32[3]{0:T(128)} %pad_add_fusion.place_ref, s32[32]{0:T(128)} %get-tuple-element.29.count_ref, s32[64]{0:T(128)} %get-tuple-element.30.depth_ref, s16[8,272,128]{2,1,0:T(8,128)(2,1)} %copy-done.6, ...), custom_call_target="tpu_custom_call" | custom-call | flops 4831838208 | bytes 10485760 | tf_op jit(solution)/shard_map/update/pallas_call | solution.py:276
  80.1 0.6 all-to-all-done.2.pay_ref
  80.7 0.0 copy-start.7
  80.7 6.3 %all-to-all-start.1 = ((bf16[8,64,512]{2,1,0:T(8,128)(2,1)}), bf16[8,64,512]{2,1,0:T(8,128)(2,1)S(1)}, u32[]{:S(2)}, u32[]{:S(2)}) async-start(bf16[8,64,512]{2,1,0:T(8,128)(2,1)} %bitcast.16), calls=%async_computation.1 | async-start | bytes 1048576 | tf_op jit(solution)/shard_map/all_to_all | solution.py:450
  86.9 0.0 copy-done.7
  86.9 11.2 %update.3 = (f32[512,512]{1,0:T(8,128)}, bf16[512,512]{1,0:T(8,128)(2,1)}, f32[2,512,512]{2,1,0:T(8,128)}, f32[2,512,512]{2,1,0:T(8,128)}) custom-call(s32[3]{0:T(128)} %pad_add_fusion.place_ref, s32[32]{0:T(128)} %get-tuple-element.29.count_ref, s32[64]{0:T(128)} %get-tuple-element.30.depth_ref, ...), custom_call_target="tpu_custom_call", output_to_operand_aliasing={{2}: (8, {}), {3}: (9, {})} | custom-call | flops 4831838208 | bytes 10485760 | tf_op jit(solution)/shard_map/update/pallas_call | solution.py:276
  98.1 0.2 all-to-all-done.1.refs_0_
  98.2 6.1 %all-to-all-start.3 = ((bf16[8,64,512]{2,1,0:T(8,128)(2,1)}), bf16[8,64,512]{2,1,0:T(8,128)(2,1)S(1)}, u32[]{:S(2)}, u32[]{:S(2)}) async-start(bf16[8,64,512]{2,1,0:T(8,128)(2,1)} %bitcast.15), calls=%async_computation.3 | async-start | bytes 1048576 | tf_op jit(solution)/shard_map/all_to_all | solution.py:450
  104.3 13.7 %basis_right.2 = (f32[2,512,512]{2,1,0:T(8,128)}, f32[2,512,512]{2,1,0:T(8,128)}) custom-call(s32[3]{0:T(128)} %pad_add_fusion.place_ref, s32[32]{0:T(128)} %get-tuple-element.29.count_ref, f32[512,512]{1,0:T(8,128)} %get-tuple-element.38.g_ref, f32[2,512,512]{2,1,0:T(8,128)} %s_ref.7, f32[2,512,512]{2,1,0:T(8,128)} %q_ref.7), custom_call_target="tpu_custom_call" | custom-call | flops 8053063680 | bytes 5242880 | tf_op jit(solution)/shard_map/basis_right/pallas_call | solution.py:344
  118.1 13.9 %basis_left.2 = (f32[2,512,512]{2,1,0:T(8,128)}, f32[2,512,512]{2,1,0:T(8,128)}) custom-call(s32[3]{0:T(128)} %pad_add_fusion.place_ref, s32[32]{0:T(128)} %get-tuple-element.29.count_ref, f32[512,512]{1,0:T(8,128)} %get-tuple-element.38.g_ref, f32[2,512,512]{2,1,0:T(8,128)} %s_ref.5, f32[2,512,512]{2,1,0:T(8,128)} %q_ref.5), custom_call_target="tpu_custom_call" | custom-call | flops 8053063680 | bytes 5242880 | tf_op jit(solution)/shard_map/basis_left/pallas_call | solution.py:344
  131.9 1.3 collective-permute-start.3
  133.2 0.0 all-to-all-done.3.refs_4_
  133.2 0.2 collective-permute-start.8
  133.4 13.7 %basis_right.3 = (f32[2,512,512]{2,1,0:T(8,128)}, f32[2,512,512]{2,1,0:T(8,128)}) custom-call(s32[3]{0:T(128)} %pad_add_fusion.place_ref, s32[32]{0:T(128)} %get-tuple-element.29.count_ref, f32[512,512]{1,0:T(8,128)} %get-tuple-element.37.g_ref, f32[2,512,512]{2,1,0:T(8,128)} %s_ref.7, ...), custom_call_target="tpu_custom_call", output_to_operand_aliasing={{0}: (5, {}), {1}: (6, {})} | custom-call | flops 8053063680 | bytes 5242880 | tf_op jit(solution)/shard_map/basis_right/pallas_call | solution.py:344
  147.1 0.0 copy-done.2
  147.1 0.0 collective-permute-start.2
  147.1 0.0 copy-done.3
  147.1 0.5 collective-permute-start.7
  147.6 0.0 collective-permute-done.3.refs_2_
  147.6 1.1 collective-permute-start.4
  148.8 5.8 %collective-permute-done.8.refs_6_ = bf16[8,64,512]{2,1,0:T(8,128)(2,1)S(1)} collective-permute-done((bf16[8,64,512]{2,1,0:T(8,128)(2,1)S(1)}, bf16[8,64,512]{2,1,0:T(8,128)(2,1)S(1)}, u32[]{:S(2)}, u32[]{:S(2)}) %collective-permute-start.8) | collective-permute-done | bytes 524320 | tf_op jit(solution)/shard_map/ppermute | solution.py:423
  154.6 2.9 %collective-permute-start.9 = (bf16[8,64,512]{2,1,0:T(8,128)(2,1)S(1)}, bf16[8,64,512]{2,1,0:T(8,128)(2,1)}, u32[]{:S(2)}, u32[]{:S(2)}) collective-permute-start(bf16[8,64,512]{2,1,0:T(8,128)(2,1)S(1)} %collective-permute-done.8.refs_6_), channel_id=1, source_target_pairs={{0,8},{8,0},{16,24},{24,16},{1,9},{9,1},{17,25},{25,17},{2,10},{10... | collective-permute-start | bytes 1572872 | tf_op jit(solution)/shard_map/ppermute | solution.py:423
  157.5 13.9 %basis_left.3 = (f32[2,512,512]{2,1,0:T(8,128)}, f32[2,512,512]{2,1,0:T(8,128)}) custom-call(s32[3]{0:T(128)} %pad_add_fusion.place_ref, s32[32]{0:T(128)} %get-tuple-element.29.count_ref, f32[512,512]{1,0:T(8,128)} %get-tuple-element.37.g_ref, f32[2,512,512]{2,1,0:T(8,128)} %s_ref.5, ...), custom_call_target="tpu_custom_call", output_to_operand_aliasing={{0}: (5, {}), {1}: (6, {})} | custom-call | flops 8053063680 | bytes 5242880 | tf_op jit(solution)/shard_map/basis_left/pallas_call | solution.py:344
  171.4 0.0 copy-done.8
  171.4 0.0 copy-done.9
  171.4 0.0 collective-permute-done.2.refs_1_
  171.4 0.0 copy-start.10
  171.4 0.0 collective-permute-done.7.refs_5_
  171.4 0.0 copy-start.11
  171.4 0.0 collective-permute-done.4.refs_3_
  171.4 0.0 copy-start.12
  171.4 0.0 collective-permute-done.9.refs_7_
  171.4 0.7 copy-done.10
  172.2 0.2 copy-done.11
  172.4 0.2 copy-done.12
  172.6 2.9 %pick.1 = bf16[12,64,512]{2,1,0:T(8,128)(2,1)} custom-call(s32[3]{0:T(128)} %pad_add_fusion.place_ref, s32[48]{0:T(128)} %owner_ref.3, s32[48]{0:T(128)} %get-tuple-element.28.rank_ref, bf16[8,64,512]{2,1,0:T(8,128)(2,1)} %copy-done.2, bf16[8,64,512]{2,1,0:T(8,128)(2,1)} %copy-done.10, bf16[8,64,512]{2,1,0:T(8,128)(2,1)} %copy-done.8, ...), custom_call_target="tpu_custom_call" | custom-call | bytes 1572864 | tf_op jit(solution)/shard_map/pick/pallas_call | solution.py:389
  (4 shorter events, 0.0 us)
Async XLA Ops:
  4.7 4.0 %collective-permute-start = (bf16[2,8,64,512]{3,2,1,0:T(8,128)(2,1)}, bf16[2,8,64,512]{3,2,1,0:T(8,128)(2,1)S(1)}, u32[]{:S(2)}, u32[]{:S(2)}) collective-permute-start(bf16[2,8,64,512]{3,2,1,0:T(8,128)(2,1)} %get-tuple-element.32), channel_id=1, source_target_pairs={{0,8},{8,0},{16,24},{24,16},{1,9},{9,1},{17,25},{25,17},{2,10},{10... | collective-permute-start | bytes 3145736 | tf_op jit(solution)/shard_map/ppermute | solution.py:423
  8.6 31.1 %collective-permute-start.5 = (bf16[2,8,64,512]{3,2,1,0:T(8,128)(2,1)}, bf16[2,8,64,512]{3,2,1,0:T(8,128)(2,1)S(1)}, u32[]{:S(2)}, u32[]{:S(2)}) collective-permute-start(bf16[2,8,64,512]{3,2,1,0:T(8,128)(2,1)} %pack.1), channel_id=1, source_target_pairs={{0,8},{8,0},{16,24},{24,16},{1,9},{9,1},{17,25},{25,17},{2,10},{10... | collective-permute-start | bytes 3145736 | tf_op jit(solution)/shard_map/ppermute | solution.py:423
  8.7 1.0 copy-start.1
  14.0 14.0 %collective-permute-start.1 = (s16[1,8,272,128]{3,2,1,0:T(8,128)(2,1)}, s16[1,8,272,128]{3,2,1,0:T(8,128)(2,1)S(1)}, u32[]{:S(2)}, u32[]{:S(2)}) collective-permute-start(s16[1,8,272,128]{3,2,1,0:T(8,128)(2,1)} %fold.4), channel_id=1, source_target_pairs={{0,16},{8,24},{16,0},{24,8},{1,17},{9,25},{17,1},{25,9},{2,18},{10... | collective-permute-start | bytes 1671176 | tf_op jit(solution)/shard_map/ppermute | solution.py:423
  28.0 0.8 copy-start.5
  33.9 29.6 %all-to-all-start = ((s16[8,272,128]{2,1,0:T(8,128)(2,1)}), s16[8,272,128]{2,1,0:T(8,128)(2,1)S(1)}, u32[]{:S(2)}, u32[]{:S(2)}) async-start(s16[8,272,128]{2,1,0:T(8,128)(2,1)} %bitcast.13), calls=%async_computation | async-start | bytes 1114112 | tf_op jit(solution)/shard_map/all_to_all | solution.py:442
  39.7 1.0 copy-start
  45.1 12.5 %collective-permute-start.6 = (s16[1,8,272,128]{3,2,1,0:T(8,128)(2,1)}, s16[1,8,272,128]{3,2,1,0:T(8,128)(2,1)S(1)}, u32[]{:S(2)}, u32[]{:S(2)}) collective-permute-start(s16[1,8,272,128]{3,2,1,0:T(8,128)(2,1)} %fold.6), channel_id=1, source_target_pairs={{0,16},{8,24},{16,0},{24,8},{1,17},{9,25},{17,1},{25,9},{2,18},{10... | collective-permute-start | bytes 1671176 | tf_op jit(solution)/shard_map/ppermute | solution.py:423
  57.6 0.8 copy-start.4
  63.6 5.5 %copy-start.6 = (s16[8,272,128]{2,1,0:T(8,128)(2,1)}, s16[8,272,128]{2,1,0:T(8,128)(2,1)S(1)}, u32[]{:S(2)}) copy-start(s16[8,272,128]{2,1,0:T(8,128)(2,1)S(1)} %all-to-all-done.pay_ref) | copy-start | bytes 1671172
  63.6 17.0 %all-to-all-start.2 = ((s16[8,272,128]{2,1,0:T(8,128)(2,1)}), s16[8,272,128]{2,1,0:T(8,128)(2,1)S(1)}, u32[]{:S(2)}, u32[]{:S(2)}) async-start(s16[8,272,128]{2,1,0:T(8,128)(2,1)} %bitcast.14), calls=%async_computation.2 | async-start | bytes 1114112 | tf_op jit(solution)/shard_map/all_to_all | solution.py:442
  80.7 6.3 %copy-start.7 = (s16[8,272,128]{2,1,0:T(8,128)(2,1)}, s16[8,272,128]{2,1,0:T(8,128)(2,1)S(1)}, u32[]{:S(2)}) copy-start(s16[8,272,128]{2,1,0:T(8,128)(2,1)S(1)} %all-to-all-done.2.pay_ref) | copy-start | bytes 1671172
  80.7 17.6 %all-to-all-start.1 = ((bf16[8,64,512]{2,1,0:T(8,128)(2,1)}), bf16[8,64,512]{2,1,0:T(8,128)(2,1)S(1)}, u32[]{:S(2)}, u32[]{:S(2)}) async-start(bf16[8,64,512]{2,1,0:T(8,128)(2,1)} %bitcast.16), calls=%async_computation.1 | async-start | bytes 1048576 | tf_op jit(solution)/shard_map/all_to_all | solution.py:450
  98.2 48.9 %copy-start.2 = (bf16[8,64,512]{2,1,0:T(8,128)(2,1)}, bf16[8,64,512]{2,1,0:T(8,128)(2,1)S(1)}, u32[]{:S(2)}) copy-start(bf16[8,64,512]{2,1,0:T(8,128)(2,1)S(1)} %all-to-all-done.1.refs_0_) | copy-start | bytes 1572868
  98.2 35.0 %all-to-all-start.3 = ((bf16[8,64,512]{2,1,0:T(8,128)(2,1)}), bf16[8,64,512]{2,1,0:T(8,128)(2,1)S(1)}, u32[]{:S(2)}, u32[]{:S(2)}) async-start(bf16[8,64,512]{2,1,0:T(8,128)(2,1)} %bitcast.15), calls=%async_computation.3 | async-start | bytes 1048576 | tf_op jit(solution)/shard_map/all_to_all | solution.py:450
  131.9 15.7 %collective-permute-start.3 = (bf16[8,64,512]{2,1,0:T(8,128)(2,1)S(1)}, bf16[8,64,512]{2,1,0:T(8,128)(2,1)S(1)}, u32[]{:S(2)}, u32[]{:S(2)}) collective-permute-start(bf16[8,64,512]{2,1,0:T(8,128)(2,1)S(1)} %all-to-all-done.1.refs_0_), channel_id=1, source_target_pairs={{0,16},{8,24},{16,0},{24,8},{1,17},{9,25},{17,1},{25,9},{2,18},{10... | collective-permute-start | bytes 1572872 | tf_op jit(solution)/shard_map/ppermute | solution.py:423
  133.2 13.9 %copy-start.3 = (bf16[8,64,512]{2,1,0:T(8,128)(2,1)}, bf16[8,64,512]{2,1,0:T(8,128)(2,1)S(1)}, u32[]{:S(2)}) copy-start(bf16[8,64,512]{2,1,0:T(8,128)(2,1)S(1)} %all-to-all-done.3.refs_4_) | copy-start | bytes 1572868
  133.2 21.4 %collective-permute-start.8 = (bf16[8,64,512]{2,1,0:T(8,128)(2,1)S(1)}, bf16[8,64,512]{2,1,0:T(8,128)(2,1)S(1)}, u32[]{:S(2)}, u32[]{:S(2)}) collective-permute-start(bf16[8,64,512]{2,1,0:T(8,128)(2,1)S(1)} %all-to-all-done.3.refs_4_), channel_id=1, source_target_pairs={{0,16},{8,24},{16,0},{24,8},{1,17},{9,25},{17,1},{25,9},{2,18},{10... | collective-permute-start | bytes 1572872 | tf_op jit(solution)/shard_map/ppermute | solution.py:423
  147.1 24.3 %collective-permute-start.2 = (bf16[8,64,512]{2,1,0:T(8,128)(2,1)S(1)}, bf16[8,64,512]{2,1,0:T(8,128)(2,1)S(1)}, u32[]{:S(2)}, u32[]{:S(2)}) collective-permute-start(bf16[8,64,512]{2,1,0:T(8,128)(2,1)S(1)} %all-to-all-done.1.refs_0_), channel_id=1, source_target_pairs={{0,8},{8,0},{16,24},{24,16},{1,9},{9,1},{17,25},{25,17},{2,10},{10... | collective-permute-start | bytes 1572872 | tf_op jit(solution)/shard_map/ppermute | solution.py:423
  147.1 24.3 %collective-permute-start.7 = (bf16[8,64,512]{2,1,0:T(8,128)(2,1)S(1)}, bf16[8,64,512]{2,1,0:T(8,128)(2,1)S(1)}, u32[]{:S(2)}, u32[]{:S(2)}) collective-permute-start(bf16[8,64,512]{2,1,0:T(8,128)(2,1)S(1)} %all-to-all-done.3.refs_4_), channel_id=1, source_target_pairs={{0,8},{8,0},{16,24},{24,16},{1,9},{9,1},{17,25},{25,17},{2,10},{10... | collective-permute-start | bytes 1572872 | tf_op jit(solution)/shard_map/ppermute | solution.py:423
  147.6 23.7 %copy-start.8 = (bf16[8,64,512]{2,1,0:T(8,128)(2,1)}, bf16[8,64,512]{2,1,0:T(8,128)(2,1)S(1)}, u32[]{:S(2)}) copy-start(bf16[8,64,512]{2,1,0:T(8,128)(2,1)S(1)} %collective-permute-done.3.refs_2_) | copy-start | bytes 1572868
  147.6 23.8 %collective-permute-start.4 = (bf16[8,64,512]{2,1,0:T(8,128)(2,1)S(1)}, bf16[8,64,512]{2,1,0:T(8,128)(2,1)S(1)}, u32[]{:S(2)}, u32[]{:S(2)}) collective-permute-start(bf16[8,64,512]{2,1,0:T(8,128)(2,1)S(1)} %collective-permute-done.3.refs_2_), channel_id=1, source_target_pairs={{0,8},{8,0},{16,24},{24,16},{1,9},{9,1},{17,25},{25,17},{2,10},{10... | collective-permute-start | bytes 1572872 | tf_op jit(solution)/shard_map/ppermute | solution.py:423
  154.6 16.8 %copy-start.9 = (bf16[8,64,512]{2,1,0:T(8,128)(2,1)}, bf16[8,64,512]{2,1,0:T(8,128)(2,1)S(1)}, u32[]{:S(2)}) copy-start(bf16[8,64,512]{2,1,0:T(8,128)(2,1)S(1)} %collective-permute-done.8.refs_6_) | copy-start | bytes 1572868
  154.6 16.9 %collective-permute-start.9 = (bf16[8,64,512]{2,1,0:T(8,128)(2,1)S(1)}, bf16[8,64,512]{2,1,0:T(8,128)(2,1)}, u32[]{:S(2)}, u32[]{:S(2)}) collective-permute-start(bf16[8,64,512]{2,1,0:T(8,128)(2,1)S(1)} %collective-permute-done.8.refs_6_), channel_id=1, source_target_pairs={{0,8},{8,0},{16,24},{24,16},{1,9},{9,1},{17,25},{25,17},{2,10},{10... | collective-permute-start | bytes 1572872 | tf_op jit(solution)/shard_map/ppermute | solution.py:423
  171.4 0.8 copy-start.10
  171.4 1.0 copy-start.11
  171.4 1.1 copy-start.12

commit v3 on v2

--- a/solution.py
+++ b/solution.py
@@ -15,6 +15,8 @@
 LANES = 128
 TAIL = 16
 MIB = 1 << 20
+ROOMY = 24 * MIB
+WEIGHT = 1.0
 F32 = jnp.float32
 BF16 = jnp.bfloat16
 ANY = pl.BlockSpec(memory_space=pl.ANY)
@@ -26,7 +28,7 @@
 
 
 def cost(flops, moved):
-    return pl.CostEstimate(flops=int(flops), bytes_accessed=int(moved), transcendentals=0)
+    return pl.CostEstimate(flops=int(flops * WEIGHT), bytes_accessed=int(moved * WEIGHT), transcendentals=0)
 
 
 def gather(base, halves, members, place_ref, block_ref, grads_ref, out_ref, sems):
@@ -109,21 +111,19 @@
     return part.astype(jnp.int32).astype(F32) * scale
 
 
-def fold_kernel(base, first, members, place_ref, block_ref, grads_ref, core_ref, *refs):
-    earlier, (out_ref, raw_ref, sems) = refs[:-3], refs[-3:]
+def fold_kernel(base, first, members, earlier_count, place_ref, block_ref, grads_ref, core_ref, *refs):
+    earlier, (out_ref, done_ref, raw_ref, sems) = refs[:earlier_count], refs[-4:]
+    done_ref[0] = 1
     count = out_ref.shape[0]
     rows, width = raw_ref.shape[1:]
     panels = width // LANES
-    copies = []
     for i in range(count * members):
         group = place_ref[0] ^ (2 * (first + i // members))
         block = block_ref[base + group * members + i % members]
-        copies.append(pltpu.make_async_copy(grads_ref.at[block], raw_ref.at[i], sems.at[i]))
-        copies[-1].start()
-    for copy in copies:
-        copy.wait()
+        pltpu.make_async_copy(grads_ref.at[block], raw_ref.at[i], sems.at[i]).start()
 
     def piece(i, carry):
+        pltpu.make_async_copy(grads_ref.at[0], raw_ref.at[i], sems.at[i]).wait()
         at = (i // members, i % members)
         total = raw_ref[i].astype(F32) + core_ref[at].astype(F32)
         parts = [total[:, p * LANES : (p + 1) * LANES] for p in range(panels)]
@@ -149,26 +149,30 @@
     lax.fori_loop(0, count * members, piece, 0)
 
 
-def fold(rank, first, count, place, block_at, grads, from_core, from_x, members):
+def fold(rank, first, count, place, block_at, grads, from_core, from_x, members, after=()):
     rows, width = grads.shape[1:]
     tall = (width // LANES) * rows + TAIL
     devices = 2 * from_core.shape[0] * members
     at = first // count
     return pl.pallas_call(
-        functools.partial(fold_kernel, rank * devices, first, members),
+        functools.partial(fold_kernel, rank * devices, first, members, len(from_x)),
         grid=(1,),
         in_specs=[SMEM, SMEM, ANY, pl.BlockSpec((count, members, rows, width), lambda i: (at, 0, 0, 0))]
-        + [pl.BlockSpec((count, members, tall, LANES), lambda i: (at, 0, 0, 0)) for _ in from_x],
-        out_specs=pl.BlockSpec((count, members, tall, LANES), lambda i: (0, 0, 0, 0)),
-        out_shape=jax.ShapeDtypeStruct((count, members, tall, LANES), jnp.int16),
+        + [pl.BlockSpec((count, members, tall, LANES), lambda i: (at, 0, 0, 0)) for _ in from_x]
+        + [SMEM] * len(after),
+        out_specs=(pl.BlockSpec((count, members, tall, LANES), lambda i: (0, 0, 0, 0)), SMEM),
+        out_shape=(
+            jax.ShapeDtypeStruct((count, members, tall, LANES), jnp.int16),
+            jax.ShapeDtypeStruct((1,), jnp.int32),
+        ),
         scratch_shapes=[
             pltpu.VMEM((count * members, rows, width), grads.dtype),
             pltpu.SemaphoreType.DMA((count * members,)),
         ],
-        compiler_params=params(),
+        compiler_params=params(ROOMY),
         cost_estimate=cost(0, 8 * count * members * rows * width),
         name="fold",
-    )(place, block_at, grads, from_core, *from_x)
+    )(place, block_at, grads, from_core, *from_x, *after)
 
 
 def split(x):
@@ -203,12 +207,66 @@
 BOTH = (0, 0, 1, 0)
 
 
-def tiles(height, size=256):
+def tiles(height, size=512):
     return [pl.ds(s, size) for s in range(0, height, size)]
 
 
-def update_kernel(rank, base, place_ref, count_ref, depth_ref, pay_ref, ql_ref, qr_ref, m_ref, v_ref, *refs):
-    g_ref, u_ref, m1_ref, v1_ref, qlt_ref, ql3_ref, qrs_ref, qrp_ref, bs_ref, as_ref, mrot_ref = refs[-11:]
+class Copies:
+    def __init__(self, sems):
+        self.sems, self.used = sems, 0
+
+    def start(self, source, target):
+        copy = pltpu.make_async_copy(source, target, self.sems.at[self.used])
+        self.used += 1
+        copy.start()
+        return copy
+
+
+def premix_kernel(slots, place_ref, count_ref, ql_hbm, qr_hbm, m_hbm, *refs):
+    mq_hbm, done_ref, ql_ref, qr_ref, m_ref, qlt_ref, b_ref, a_ref, sems = refs[-9:]
+    width = ql_ref.shape[0]
+    done_ref[0] = 1
+    for slot in range(slots):
+
+        @pl.when(count_ref[place_ref[1]] > slot)
+        def _():
+            copies = Copies(sems)
+            load_m = copies.start(m_hbm.at[slot], m_ref)
+            load_l = copies.start(ql_hbm.at[slot], ql_ref)
+            load_r = copies.start(qr_hbm.at[slot], qr_ref)
+            load_m.wait()
+            put_rows(b_ref, 0, width, m_ref[...])
+            load_l.wait()
+            put_cols(qlt_ref, slice(None), ql_ref[...].T, LEFT)
+            for t in tiles(width):
+                put_cols(a_ref, t, dot_nn(qlt_ref[t, :], b_ref[...]), LEFT)
+            load_r.wait()
+            put_rows(b_ref, 0, width, qr_ref[...])
+            for t in tiles(width):
+                m_ref[t, :] = dot_nn(a_ref[t, :], b_ref[...])
+            copies.start(m_ref, mq_hbm.at[slot]).wait()
+
+
+def premix(place, counts, ql, qr, m, after):
+    slots, width = ql.shape[:2]
+    flat = pltpu.VMEM((width, width), F32)
+    wide = pltpu.VMEM((width, 3 * width), BF16)
+    tall = pltpu.VMEM((3 * width, width), BF16)
+    return pl.pallas_call(
+        functools.partial(premix_kernel, slots),
+        out_shape=(jax.ShapeDtypeStruct(m.shape, F32), jax.ShapeDtypeStruct((1,), jnp.int32)),
+        in_specs=[SMEM, SMEM] + [ANY] * 3 + [SMEM] * len(after),
+        out_specs=(ANY, SMEM),
+        scratch_shapes=[flat, flat, flat, wide, tall, wide, pltpu.SemaphoreType.DMA((4,))],
+        compiler_params=params(),
+        cost_estimate=cost(slots * 2 * 3 * 2 * width**3, slots * 4 * 4 * width**2),
+        name="premix",
+    )(place, counts, ql, qr, m, *after)
+
+
+def update_kernel(rank, base, place_ref, count_ref, depth_ref, pay_ref, ql_hbm, qr_hbm, m_hbm, v_hbm, mq_hbm, *refs):
+    g_hbm, u_hbm, m1_hbm, v1_hbm = refs[-20:-16]
+    g_ref, u_ref, ql_ref, qr_ref, m_ref, v_ref, mq_ref, qlt_ref, ql3_ref, qrs_ref, qrp_ref, bs_ref, bn_ref, as_ref, ab_ref, sems = refs[-16:]
     width = g_ref.shape[0]
     members = pay_ref.shape[0]
     rows = width // members
@@ -217,61 +275,74 @@
 
     @pl.when(jnp.logical_not(live))
     def _():
+        copies = Copies(sems)
+        loads = [copies.start(m_hbm.at[rank], m_ref), copies.start(v_hbm.at[rank], v_ref)]
         u_ref[...] = jnp.zeros_like(u_ref)
-        m1_ref[0] = m_ref[0]
-        v1_ref[0] = v_ref[0]
+        stores = [copies.start(u_ref, u_hbm)]
+        for load in loads:
+            load.wait()
+        stores += [copies.start(m_ref, m1_hbm.at[rank]), copies.start(v_ref, v1_hbm.at[rank])]
+        for store in stores:
+            store.wait()
 
     @pl.when(live)
     def _():
-        put_cols(qlt_ref, slice(None), ql_ref[0].T, LEFT)
-        put_rows(qrs_ref, 0, width, qr_ref[0])
+        copies = Copies(sems)
+        load_l = copies.start(ql_hbm.at[rank], ql_ref)
+        load_r = copies.start(qr_hbm.at[rank], qr_ref)
+        load_m = copies.start(m_hbm.at[rank], m_ref)
+        load_v = copies.start(v_hbm.at[rank], v_ref)
+        load_q = copies.start(mq_hbm.at[rank], mq_ref)
 
         def bring(member, carry):
             scale = decode_scale(pay_ref, (member,), rows, panels)
             at = pl.multiple_of(member * rows, rows)
             for p in range(panels):
-                g_ref[pl.ds(at, rows), pl.ds(p * LANES, LANES)] = decode(pay_ref, (member,), rows, p, scale)
+                part = decode(pay_ref, (member,), rows, p, scale)
+                g_ref[pl.ds(at, rows), pl.ds(p * LANES, LANES)] = part
+                high, low = split(part)
+                for n, piece in enumerate((high, low, high)):
+                    bs_ref[pl.ds(n * width + at, rows), pl.ds(p * LANES, LANES)] = piece
             return carry
 
         lax.fori_loop(0, members, bring, 0)
-        m1_ref[0] = BETA_ONE * m_ref[0] + (1.0 - BETA_ONE) * g_ref[...]
-
-        put_rows(bs_ref, 0, width, m1_ref[0])
+        stores = [copies.start(g_ref, g_hbm)]
+        load_l.wait()
+        put_cols(qlt_ref, slice(None), ql_ref[...].T, LEFT)
         for t in tiles(width):
             put_cols(as_ref, t, dot_nn(qlt_ref[t, :], bs_ref[...]), LEFT)
-        for t in tiles(width):
-            mrot_ref[t, :] = dot_nn(as_ref[t, :], qrs_ref[...])
-
-        put_rows(bs_ref, 0, width, g_ref[...])
-        for t in tiles(width):
-            put_cols(as_ref, t, dot_nn(qlt_ref[t, :], bs_ref[...]), LEFT)
+        load_r.wait()
+        put_rows(qrs_ref, 0, width, qr_ref[...])
+        load_v.wait()
+        load_q.wait()
         for t in tiles(width):
             rot = dot_nn(as_ref[t, :], qrs_ref[...])
-            second = BETA_TWO * v_ref[0, t, :] + (1.0 - BETA_TWO) * rot * rot
-            v1_ref[0, t, :] = second
-            put_rows(bs_ref, t.start, width, mrot_ref[t, :] / (jnp.sqrt(second) + 1e-08))
-        put_cols(ql3_ref, slice(None), ql_ref[0], LEFT)
-        put_cols(qrp_ref, slice(None), qr_ref[0], (0, 1, 0))
+            second = BETA_TWO * v_ref[t, :] + (1.0 - BETA_TWO) * rot * rot
+            v_ref[t, :] = second
+            first = BETA_ONE * mq_ref[t, :] + (1.0 - BETA_ONE) * rot
+            put_rows(bn_ref, t.start, width, first / (jnp.sqrt(second) + 1e-08))
+        stores.append(copies.start(v_ref, v1_hbm.at[rank]))
+        put_cols(ql3_ref, slice(None), ql_ref[...], LEFT)
+        for t in tiles(width):
+            put_cols(ab_ref, t, dot_nn(ql3_ref[t, :], bn_ref[...]), LEFT)
+        put_cols(qrp_ref, slice(None), qr_ref[...], (0, 1, 0))
         depth = (place_ref[2] - 1 - depth_ref[base + place_ref[1]]).astype(F32)
         factor = jnp.exp(SHRINK * jnp.full((1, width), depth, F32))
         for t in tiles(width):
-            put_cols(as_ref, t, dot_nn(ql3_ref[t, :], bs_ref[...]), LEFT)
-        for t in tiles(width):
-            u_ref[t, :] = (factor * dot_nt(as_ref[t, :], qrp_ref[...])).astype(BF16)
-
-
-def slot_block(slot, width):
-    return pl.BlockSpec((1, width, width), lambda *_: (slot, 0, 0))
-
-
-def update_call(rank, info, pay, ql, qr, m, v, carried):
+            u_ref[t, :] = (factor * dot_nt(ab_ref[t, :], qrp_ref[...])).astype(BF16)
+        stores.append(copies.start(u_ref, u_hbm))
+        load_m.wait()
+        m_ref[...] = BETA_ONE * m_ref[...] + (1.0 - BETA_ONE) * g_ref[...]
+        stores.append(copies.start(m_ref, m1_hbm.at[rank]))
+        for store in stores:
+            store.wait()
+
+
+def update_call(rank, info, pay, ql, qr, m, v, mq, carried):
     width = ql.shape[1]
-    own = slot_block(rank, width)
-    whole = pl.BlockSpec((width, width), lambda *_: (0, 0))
     state = jax.ShapeDtypeStruct(m.shape, F32)
-    operands = list(info) + [pay, ql, qr, m, v] + list(carried)
-    aliases = {8: 2, 9: 3} if carried else {}
-    wide = lambda n: pltpu.VMEM((width, n * width), BF16)
+    flat = pltpu.VMEM((width, width), F32)
+    wide = pltpu.VMEM((width, 3 * width), BF16)
     tall = pltpu.VMEM((3 * width, width), BF16)
     return pl.pallas_call(
         functools.partial(update_kernel, rank, rank * info[1].shape[0]),
@@ -282,82 +353,97 @@
             state,
             state,
         ),
-        in_specs=[SMEM] * 3 + [pl.BlockSpec(pay.shape, lambda *_: (0, 0, 0)), own, own, own, own] + [ANY] * len(carried),
-        out_specs=(whole, whole, own, own),
-        scratch_shapes=[wide(3), wide(3), tall, wide(3), tall, wide(3), pltpu.VMEM((width, width), F32)],
-        input_output_aliases=aliases,
+        in_specs=[SMEM] * 3 + [pl.BlockSpec(pay.shape, lambda *_: (0, 0, 0))] + [ANY] * (5 + len(carried)),
+        out_specs=(ANY,) * 4,
+        scratch_shapes=[flat, pltpu.VMEM((width, width), BF16)]
+        + [flat] * 5
+        + [wide, wide, tall, wide, tall, tall, wide, wide, pltpu.SemaphoreType.DMA((9,))],
+        input_output_aliases={9: 2, 10: 3} if carried else {},
         compiler_params=params(),
-        cost_estimate=cost(6 * 3 * 2 * width**3, 10 * 4 * width**2),
+        cost_estimate=cost(4 * 3 * 2 * width**3, 10 * 4 * width**2),
         name="update",
-    )(*operands)
-
-
-def basis_kernel(rank, left, place_ref, count_ref, g_ref, s_ref, q_ref, *refs):
-    s1_ref, q1_ref, y_ref, cols_ref, a_ref, b_ref = refs[-6:]
+    )(*info, pay, ql, qr, m, v, mq, *carried)
+
+
+def basis_kernel(rank, left, place_ref, count_ref, g_hbm, s_hbm, q_hbm, *refs):
+    s1_hbm, q1_hbm, g_ref, s_ref, q_ref, y_ref, cols_ref, a_ref, b_ref, sems = refs[-10:]
     width = g_ref.shape[0]
     live = count_ref[place_ref[1]] > rank
-    fits = pl.ds(0, 3 * width), pl.ds(width, 3 * width)
+    near, far, one = pl.ds(0, 3 * width), pl.ds(width, 3 * width), pl.ds(0, width)
 
     @pl.when(jnp.logical_not(live))
     def _():
-        s1_ref[0] = s_ref[0]
-        q1_ref[0] = q_ref[0]
+        copies = Copies(sems)
+        loads = [copies.start(s_hbm.at[rank], s_ref), copies.start(q_hbm.at[rank], q_ref)]
+        stores = []
+        for load, ref, out in zip(loads, (s_ref, q_ref), (s1_hbm, q1_hbm)):
+            load.wait()
+            stores.append(copies.start(ref, out.at[rank]))
+        for store in stores:
+            store.wait()
 
     @pl.when(live)
     def _():
-        grad = g_ref[...] if left else g_ref[...].T
-        put_cols(cols_ref, slice(None), grad, BOTH)
-        put_cols(a_ref, slice(None), q_ref[0].T, LEFT)
+        copies = Copies(sems)
+        load_g = copies.start(g_hbm, g_ref)
+        load_q = copies.start(q_hbm.at[rank], q_ref)
+        load_s = copies.start(s_hbm.at[rank], s_ref)
+        load_g.wait()
+        put_cols(cols_ref, slice(None), g_ref[...] if left else g_ref[...].T, BOTH)
+        load_q.wait()
+        put_cols(a_ref, slice(None), q_ref[...].T, LEFT)
+        load_s.wait()
         for t in tiles(width):
-            outer = dot_nt(cols_ref[t, fits[0]], cols_ref[:, fits[1]])
-            stat = BETA_TWO * s_ref[0, t, :] + (1.0 - BETA_TWO) * outer
-            s1_ref[0, t, :] = stat
+            outer = dot_nt(cols_ref[t, near], cols_ref[:, far])
+            stat = BETA_TWO * s_ref[t, :] + (1.0 - BETA_TWO) * outer
+            s_ref[t, :] = stat
             put_rows(b_ref, t.start, width, stat)
-        squares = jnp.zeros((1, width), F32)
-        for t in tiles(width):
-            turned = dot_nn(a_ref[t, :], b_ref[...])
-            y_ref[t, :] = turned
-            squares = squares + jnp.sum(turned * turned, axis=0, keepdims=True)
+        stores = [copies.start(s_ref, s1_hbm.at[rank])]
+        turned = dot_nn(a_ref[...], b_ref[...])
+        squares = jnp.sum(turned * turned, axis=0, keepdims=True)
         mean = jnp.sum(squares, axis=1, keepdims=True) * (1.0 / (width * width))
-        scaling = 0.4 / (math.sqrt(width) * jnp.sqrt(mean + 1e-06))
-        y_ref[...] = y_ref[...] * scaling
+        y_ref[...] = turned * (0.4 / (math.sqrt(width) * jnp.sqrt(mean + 1e-06)))
 
         def step(i, carry):
-            for t in tiles(width):
-                put_cols(cols_ref, t, y_ref[t, :], BOTH)
-                put_rows(b_ref, t.start, width, y_ref[t, :])
-            for t in tiles(width):
-                put_cols(a_ref, t, dot_nt(cols_ref[t, fits[0]], cols_ref[:, fits[1]]), LEFT)
-            for t in tiles(width):
-                y_ref[t, :] = 1.5 * y_ref[t, :] - 0.5 * dot_nn(a_ref[t, :], b_ref[...])
+            put_cols(cols_ref, slice(None), y_ref[...], BOTH)
+            put_rows(b_ref, 0, width, y_ref[...])
+            put_cols(a_ref, slice(None), dot_nt(cols_ref[:, near], cols_ref[:, far]), LEFT)
+            y_ref[...] = 1.5 * y_ref[...] - 0.5 * dot_nn(a_ref[...], b_ref[...])
             return carry
 
-        lax.fori_loop(0, ITERS, step, 0)
-        q1_ref[0] = y_ref[...].T
-
-
-def basis_call(rank, left, info, grad, stat, basis, carried):
+        high = y_ref[...].astype(BF16)
+        cols_ref[:, one] = high
+        b_ref[one, :] = high
+        a_ref[:, one] = dot_nt(cols_ref[:, one], cols_ref[:, one]).astype(BF16)
+        y_ref[...] = 1.5 * y_ref[...] - 0.5 * dot_nn(a_ref[:, one], b_ref[one, :])
+        lax.fori_loop(1, ITERS, step, 0)
+        q_ref[...] = y_ref[...].T
+        stores.append(copies.start(q_ref, q1_hbm.at[rank]))
+        for store in stores:
+            store.wait()
+
+
+def basis_call(rank, left, info, grad, stat, basis, carried, after=()):
     width = grad.shape[0]
-    own = slot_block(rank, width)
-    whole = pl.BlockSpec((width, width), lambda *_: (0, 0))
     state = jax.ShapeDtypeStruct(stat.shape, F32)
+    flat = pltpu.VMEM((width, width), F32)
     return pl.pallas_call(
         functools.partial(basis_kernel, rank, left),
-        grid=(1,),
         out_shape=(state, state),
-        in_specs=[SMEM, SMEM, whole, own, own] + [ANY] * len(carried),
-        out_specs=(own, own),
-        scratch_shapes=[
-            pltpu.VMEM((width, width), F32),
+        in_specs=[SMEM, SMEM] + [ANY] * (3 + len(carried) + len(after)),
+        out_specs=(ANY, ANY),
+        scratch_shapes=[flat] * 4
+        + [
             pltpu.VMEM((width, 4 * width), BF16),
             pltpu.VMEM((width, 3 * width), BF16),
             pltpu.VMEM((3 * width, width), BF16),
+            pltpu.SemaphoreType.DMA((5,)),
         ],
         input_output_aliases={5: 0, 6: 1} if carried else {},
         compiler_params=params(),
         cost_estimate=cost((2 + 2 * ITERS) * 3 * 2 * width**3, 5 * 4 * width**2),
         name="basis_left" if left else "basis_right",
-    )(*info[:2], grad, stat, basis, *carried)
+    )(*info[:2], grad, stat, basis, *carried, *after)
 
 
 def pick_kernel(groups, members, count, place_ref, owner_ref, rank_ref, *refs):
@@ -392,7 +478,7 @@
         in_specs=[SMEM] * 3 + [ANY] * len(sources),
         out_specs=pl.BlockSpec(memory_space=pltpu.VMEM),
         scratch_shapes=[pltpu.SemaphoreType.DMA((count,))],
-        compiler_params=params(),
+        compiler_params=params(ROOMY),
         cost_estimate=cost(0, 4 * count * rows * width),
         name="pick",
     )(place, owner_device, rank_of, *sources)
@@ -430,21 +516,28 @@
     for k in range(1, capacity):
         from_core.append(flip(pack(k, place, block_at, grads, halves, members), 1))
 
+    from_x = [[] for _ in range(capacity)]
+    step = halves // 2
+    mixed, after = None, ()
+    while step:
+        for k in range(capacity):
+            sent, mark = fold(k, step, step, place, block_at, grads, from_core[k], from_x[k], members, after)
+            from_x[k].append(flip(sent, 2 * step))
+            if mixed is None:
+                mixed, mark = premix(place, counts, basis_left, basis_right, moment_first, (mark,))
+            after = (mark,)
+        step //= 2
+
     arrived = []
     for k in range(capacity):
-        from_x = []
-        step = halves // 2
-        while step:
-            sent = fold(k, step, step, place, block_at, grads, from_core[k], from_x, members)
-            from_x.append(flip(sent, 2 * step))
-            step //= 2
-        ready = fold(k, 0, 1, place, block_at, grads, from_core[k], from_x, members)
+        ready, mark = fold(k, 0, 1, place, block_at, grads, from_core[k], from_x[k], members, after)
+        after = (mark,)
         arrived.append(lax.all_to_all(ready[0], "mp", split_axis=0, concat_axis=0, tiled=True))
 
-    sources, gradients, moments = [], [], ()
+    sources, gradients, moments, returned, crossed = [], [], (), [], []
     for k in range(capacity):
         grad, block_update, *moments = update_call(
-            k, info, arrived[k], basis_left, basis_right, moment_first, moment_second, tuple(moments)
+            k, info, arrived[k], basis_left, basis_right, moment_first, moment_second, mixed, tuple(moments)
         )
         gradients.append(grad)
         pieces = lax.all_to_all(
@@ -455,13 +548,16 @@
         while step < halves:
             held = held + [flip(part, 2 * step) for part in held]
             step *= 2
+        returned.append(pieces)
+        crossed.append(held[-1])
         for part in held:
             sources += [part, flip(part, 1)]
 
     lefts, rights = (), ()
+    waits = [(), (returned[-1],)] + [(returned[-1],)] * (2 * capacity - 3) + [(crossed[-1],)]
     for k in range(capacity):
-        lefts = basis_call(k, True, info, gradients[k], stat_left, basis_left, tuple(lefts))
-        rights = basis_call(k, False, info, gradients[k], stat_right, basis_right, tuple(rights))
+        rights = basis_call(k, False, info, gradients[k], stat_right, basis_right, tuple(rights), waits[2 * k])
+        lefts = basis_call(k, True, info, gradients[k], stat_left, basis_left, tuple(lefts), waits[2 * k + 1])
 
     update_rows = pick(place, owner_device, rank_of, sources, groups, members)
     return (update_rows, lefts[0], rights[0], lefts[1], rights[1], moments[0], moments[1])

time: 177 us -> 165 us (0.932)
  waiting for transfers between devices: 30.5 us -> 22.5 us
  starting transfers between devices: 33 us -> 27.4 us
    ppermute x10, waiting for transfers between devices: 29.8 us -> 13.1 us  [flip(): return lax.ppermute(x, 'dp', [(i, i ^ bits) for i in range(groups)])]
    pallas_call x4 -> x5, Pallas kernels: 55.2 us -> 62 us  [the longest x4 51 us: basis_call(): pl.pallas_call(functools.partial(basis_kernel, rank, left), out_shape=(st...]
    pallas_call x2, Pallas kernels: 22.1 us -> 16.8 us  [update_call(): pl.pallas_call(functools.partial(update_kernel, rank, rank * info[1].shap...]
    all_to_all x2, waiting for transfers between devices: 0.6 us -> 5.06 us  [local(): lax.all_to_all(ready[0], 'mp', split_axis=0, concat_axis=0, tiled=True)]
    all_to_all x2, waiting for transfers between devices: 0.16 us -> 4.39 us  [local(): lax.all_to_all(block_update.reshape(members, rows, width), 'mp', split_ax...]
    all_to_all x2, starting transfers between devices: 12.4 us -> 9.24 us  [local(): lax.all_to_all(block_update.reshape(members, rows, width), 'mp', split_ax...]
    ppermute x10, starting transfers between devices: 9.43 us -> 6.86 us  [flip(): return lax.ppermute(x, 'dp', [(i, i ^ bits) for i in range(groups)])]
    unnamed x26 -> x30, local copies, waits for them, and re-layouts: 4.69 us -> 3.93 us
  transfers between devices with their start and end apart: 14 -> 14, of which waited for: 5 -> 3; matrix products, arithmetic and copies ran while one was open for 0% -> 0% of each run, Pallas kernels for 57% -> 58%
where the time goes in v3:
time: 165 us; the launch traced here: 163 us
  Pallas kernels  107 us (65%)
  starting transfers between devices  27.4 us (17%)
  waiting for transfers between devices  22.5 us (14%)
  local copies, waits for them, and re-layouts  3.93 us (2%)
    pallas_call x4, Pallas kernels, basis_call(): pl.pallas_call(functools.partial(basis_kernel, rank, left), out_shape=(st...  51 us
    pallas_call x4, Pallas kernels, fold(): pl.pallas_call(functools.partial(fold_kernel, rank * devices, first, memb...  17.8 us
    pallas_call x2, Pallas kernels, update_call(): pl.pallas_call(functools.partial(update_kernel, rank, rank * info[1].shap...  16.8 us
    ppermute x10, waiting for transfers between devices, flip(): return lax.ppermute(x, 'dp', [(i, i ^ bits) for i in range(groups)])  13.1 us
    all_to_all x2, starting transfers between devices, local(): lax.all_to_all(ready[0], 'mp', split_axis=0, concat_axis=0, tiled=True)  11.3 us
    pallas_call x1, Pallas kernels, premix(): pl.pallas_call(functools.partial(premix_kernel, slots), out_shape=(jax.Sh...  10.9 us
    all_to_all x2, starting transfers between devices, local(): lax.all_to_all(block_update.reshape(members, rows, width), 'mp', split_ax...  9.24 us
    ppermute x10, starting transfers between devices, flip(): return lax.ppermute(x, 'dp', [(i, i ^ bits) for i in range(groups)])  6.86 us
  transfers between devices with their start and end apart: 14, of which 3 were waited for; matrix products, arithmetic and copies ran while one was open for 0% of the time, Pallas kernels for 58%

profile of v3, /device:TPU:5, one launch (start us, length us, event | category | flops | bytes accessed | tf_op | source)
XLA Modules:
  0.0 162.8 jit_solution(14960773220801328509)
XLA Ops:
  0.6 0.6 pad_add_fusion.place_ref
  1.3 3.4 %route.1 = (s32[64]{0:T(128)}, s32[48]{0:T(128)}, s32[32]{0:T(128)}, s32[64]{0:T(128)}, bf16[2,8,64,512]{3,2,1,0:T(8,128)(2,1)}) custom-call(s32[48]{0:T(128)} %owner_ref.3, s32[48]{0:T(128)} %layer_ref.1, s32[3]{0:T(128)} %pad_add_fusion.place_ref, bf16[48,64,512]{2,1,0:T(8,128)(2,1)} %bitcast.7), custom_call_target="tpu_custom_call" | custom-call | bytes 2097152 | tf_op jit(solution)/shard_map/route/pallas_call | solution.py:71
  4.7 0.7 collective-permute-start
  5.5 0.0 copy-start
  5.5 0.0 copy-start.7
  5.5 3.3 %pack.1 = bf16[2,8,64,512]{3,2,1,0:T(8,128)(2,1)} custom-call(s32[3]{0:T(128)} %pad_add_fusion.place_ref, s32[64]{0:T(128)} %get-tuple-element.40.block_ref, bf16[48,64,512]{2,1,0:T(8,128)(2,1)} %bitcast.8), custom_call_target="tpu_custom_call" | custom-call | bytes 2097152 | tf_op jit(solution)/shard_map/pack/pallas_call | solution.py:91
  8.8 0.1 collective-permute-start.2
  8.9 0.0 collective-permute-done.core_ref
  8.9 0.0 copy-done
  8.9 0.0 copy-done.7
  8.9 0.0 copy-done.10
  8.9 4.0 %fold.4 = (s16[1,8,272,128]{3,2,1,0:T(8,128)(2,1)}, s32[1]{0:T(128)}) custom-call(s32[3]{0:T(128)S(1)} %copy-done.7, s32[64]{0:T(128)S(1)} %copy-done.10, bf16[48,64,512]{2,1,0:T(8,128)(2,1)S(1)} %bitcast.9, bf16[2,8,64,512]{3,2,1,0:T(8,128)(2,1)} %collective-permute-done.core_ref), custom_call_target="tpu_custom_call" | custom-call | bytes 2097152 | tf_op jit(solution)/shard_map/fold/pallas_call | solution.py:157
  13.0 1.3 collective-permute-start.1
  14.2 10.9 %premix.1 = (f32[2,512,512]{2,1,0:T(8,128)}, s32[1]{0:T(128)}) custom-call(s32[3]{0:T(128)} %pad_add_fusion.place_ref, s32[32]{0:T(128)} %get-tuple-element.38.count_ref, f32[2,512,512]{2,1,0:T(8,128)} %q_hbm.5, f32[2,512,512]{2,1,0:T(8,128)} %q_hbm.7, f32[2,512,512]{2,1,0:T(8,128)} %m_hbm.5, s32[1]{0:T(128)} %get-tuple-element.43.refs_0_), custom_call_target="tpu_custom_call" | custom-call | flops 3221225472 | bytes 8388608 | tf_op jit(solution)/shard_map/premix/pallas_call | solution.py:255
  25.2 0.0 collective-permute-done.2.core_ref
  25.2 0.0 copy-done.8
  25.2 4.2 %fold.5 = (s16[1,8,272,128]{3,2,1,0:T(8,128)(2,1)S(1)}, s32[1]{0:T(128)}) custom-call(s32[3]{0:T(128)S(1)} %copy-done.8, s32[64]{0:T(128)S(1)} %copy-done.10, bf16[48,64,512]{2,1,0:T(8,128)(2,1)S(1)} %bitcast.10, bf16[2,8,64,512]{3,2,1,0:T(8,128)(2,1)} %collective-permute-done.2.core_ref, s32[1]{0:T(128)} %get-tuple-element.44.refs_0_), custom_call_target="tpu_custom_call" | custom-call | bytes 2097152 | tf_op jit(solution)/shard_map/fold/pallas_call | solution.py:157
  29.4 0.0 copy-start.13
  29.5 0.8 copy-done.13
  30.3 0.0 collective-permute-done.1.refs_0_
  30.3 4.8 %fold.6 = (s16[1,8,272,128]{3,2,1,0:T(8,128)(2,1)S(1)}, s32[1]{0:T(128)}) custom-call(s32[3]{0:T(128)S(1)} %copy-done.8, s32[64]{0:T(128)S(1)} %copy-done.10, bf16[48,64,512]{2,1,0:T(8,128)(2,1)S(1)} %bitcast.11, bf16[2,8,64,512]{3,2,1,0:T(8,128)(2,1)} %collective-permute-done.core_ref, s16[1,8,272,128]{3,2,1,0:T(8,128)(2,1)S(1)} %collective-permute-done.1.refs_0_, ...), custom_call_target="tpu_custom_call" | custom-call | bytes 2097152 | tf_op jit(solution)/shard_map/fold/pallas_call | solution.py:157
  35.0 0.0 copy-start.3
  35.0 0.8 copy-done.3
  35.8 5.8 %all-to-all-start = ((s16[8,272,128]{2,1,0:T(8,128)(2,1)}), s16[8,272,128]{2,1,0:T(8,128)(2,1)}, u32[]{:S(2)}, u32[]{:S(2)}) async-start(s16[8,272,128]{2,1,0:T(8,128)(2,1)} %bitcast.13), calls=%async_computation | async-start | bytes 1114112 | tf_op jit(solution)/shard_map/all_to_all | solution.py:535
  41.6 0.0 collective-permute-start.6
  41.6 13.0 %collective-permute-done.6.refs_0_ = s16[1,8,272,128]{3,2,1,0:T(8,128)(2,1)S(1)} collective-permute-done((s16[1,8,272,128]{3,2,1,0:T(8,128)(2,1)}, s16[1,8,272,128]{3,2,1,0:T(8,128)(2,1)S(1)}, u32[]{:S(2)}, u32[]{:S(2)}) %collective-permute-start.6) | collective-permute-done | bytes 557088 | tf_op jit(solution)/shard_map/ppermute | solution.py:509
  54.7 4.8 %fold.7 = (s16[1,8,272,128]{3,2,1,0:T(8,128)(2,1)S(1)}, s32[1]{0:T(128)}) custom-call(s32[3]{0:T(128)S(1)} %copy-done.8, s32[64]{0:T(128)S(1)} %copy-done.10, bf16[48,64,512]{2,1,0:T(8,128)(2,1)S(1)} %bitcast.12, bf16[2,8,64,512]{3,2,1,0:T(8,128)(2,1)} %collective-permute-done.2.core_ref, s16[1,8,272,128]{3,2,1,0:T(8,128)(2,1)S(1)} %collective-permute-done.6.refs_0_, ...), custom_call_target="tpu_custom_call" | custom-call | bytes 2097152 | tf_op jit(solution)/shard_map/fold/pallas_call | solution.py:157
  59.4 0.0 copy-start.4
  59.5 0.8 copy-done.4
  60.3 0.0 all-to-all-done.pay_ref
  60.3 5.5 %all-to-all-start.2 = ((s16[8,272,128]{2,1,0:T(8,128)(2,1)}), s16[8,272,128]{2,1,0:T(8,128)(2,1)S(1)}, u32[]{:S(2)}, u32[]{:S(2)}) async-start(s16[8,272,128]{2,1,0:T(8,128)(2,1)} %bitcast.14), calls=%async_computation.2 | async-start | bytes 1114112 | tf_op jit(solution)/shard_map/all_to_all | solution.py:535
  65.8 8.3 %update.2 = (f32[512,512]{1,0:T(8,128)}, bf16[512,512]{1,0:T(8,128)(2,1)}, f32[2,512,512]{2,1,0:T(8,128)}, f32[2,512,512]{2,1,0:T(8,128)}) custom-call(s32[3]{0:T(128)} %pad_add_fusion.place_ref, s32[32]{0:T(128)} %get-tuple-element.38.count_ref, s32[64]{0:T(128)} %get-tuple-element.39.depth_ref, s16[8,272,128]{2,1,0:T(8,128)(2,1)} %all-to-all-done.pay_ref, ...), custom_call_target="tpu_custom_call" | custom-call | flops 3221225472 | bytes 10485760 | tf_op jit(solution)/shard_map/update/pallas_call | solution.py:347
  74.1 5.1 %all-to-all-done.2.pay_ref = s16[8,272,128]{2,1,0:T(8,128)(2,1)S(1)} async-done(((s16[8,272,128]{2,1,0:T(8,128)(2,1)}), s16[8,272,128]{2,1,0:T(8,128)(2,1)S(1)}, u32[]{:S(2)}, u32[]{:S(2)}) %all-to-all-start.2) | async-done | bytes 557088 | tf_op jit(solution)/shard_map/all_to_all | solution.py:535
  79.2 4.7 %all-to-all-start.1 = ((bf16[8,64,512]{2,1,0:T(8,128)(2,1)}), bf16[8,64,512]{2,1,0:T(8,128)(2,1)S(1)}, u32[]{:S(2)}, u32[]{:S(2)}) async-start(bf16[8,64,512]{2,1,0:T(8,128)(2,1)} %bitcast.16), calls=%async_computation.1 | async-start | bytes 1048576 | tf_op jit(solution)/shard_map/all_to_all | solution.py:543
  83.9 0.0 copy-done.14
  83.9 8.5 %update.3 = (f32[512,512]{1,0:T(8,128)}, bf16[512,512]{1,0:T(8,128)(2,1)}, f32[2,512,512]{2,1,0:T(8,128)}, f32[2,512,512]{2,1,0:T(8,128)}) custom-call(s32[3]{0:T(128)} %pad_add_fusion.place_ref, s32[32]{0:T(128)} %get-tuple-element.38.count_ref, s32[64]{0:T(128)} %get-tuple-element.39.depth_ref, ...), custom_call_target="tpu_custom_call", output_to_operand_aliasing={{2}: (9, {}), {3}: (10, {})} | custom-call | flops 3221225472 | bytes 10485760 | tf_op jit(solution)/shard_map/update/pallas_call | solution.py:347
  92.4 4.4 %all-to-all-done.1.refs_0_ = bf16[8,64,512]{2,1,0:T(8,128)(2,1)S(1)} async-done(((bf16[8,64,512]{2,1,0:T(8,128)(2,1)}), bf16[8,64,512]{2,1,0:T(8,128)(2,1)S(1)}, u32[]{:S(2)}, u32[]{:S(2)}) %all-to-all-start.1) | async-done | bytes 524320 | tf_op jit(solution)/shard_map/all_to_all | solution.py:543
  96.8 4.5 %all-to-all-start.3 = ((bf16[8,64,512]{2,1,0:T(8,128)(2,1)}), bf16[8,64,512]{2,1,0:T(8,128)(2,1)S(1)}, u32[]{:S(2)}, u32[]{:S(2)}) async-start(bf16[8,64,512]{2,1,0:T(8,128)(2,1)} %bitcast.15), calls=%async_computation.3 | async-start | bytes 1048576 | tf_op jit(solution)/shard_map/all_to_all | solution.py:543
  101.3 12.6 %basis_right.2 = (f32[2,512,512]{2,1,0:T(8,128)}, f32[2,512,512]{2,1,0:T(8,128)}) custom-call(s32[3]{0:T(128)} %pad_add_fusion.place_ref, s32[32]{0:T(128)} %get-tuple-element.38.count_ref, f32[512,512]{1,0:T(8,128)} %get-tuple-element.56.g_hbm, f32[2,512,512]{2,1,0:T(8,128)} %s_hbm.7, f32[2,512,512]{2,1,0:T(8,128)} %q_hbm.7), custom_call_target="tpu_custom_call" | custom-call | flops 8053063680 | bytes 5242880 | tf_op jit(solution)/shard_map/basis_right/pallas_call | solution.py:430
  113.9 0.1 collective-permute-start.4
  114.0 2.0 %collective-permute-start.3 = (bf16[8,64,512]{2,1,0:T(8,128)(2,1)S(1)}, bf16[8,64,512]{2,1,0:T(8,128)(2,1)S(1)}, u32[]{:S(2)}, u32[]{:S(2)}) collective-permute-start(bf16[8,64,512]{2,1,0:T(8,128)(2,1)S(1)} %all-to-all-done.1.refs_0_), channel_id=1, source_target_pairs={{0,8},{8,0},{16,24},{24,16},{1,9},{9,1},{17,25},{25,17},{2,10},{10... | collective-permute-start | bytes 1572872 | tf_op jit(solution)/shard_map/ppermute | solution.py:509
  116.1 0.0 all-to-all-done.3.refs_4_.refs_0_.refs_2_
  116.1 1.7 %collective-permute-start.8 = (bf16[8,64,512]{2,1,0:T(8,128)(2,1)S(1)}, bf16[8,64,512]{2,1,0:T(8,128)(2,1)S(1)}, u32[]{:S(2)}, u32[]{:S(2)}) collective-permute-start(bf16[8,64,512]{2,1,0:T(8,128)(2,1)S(1)} %all-to-all-done.3.refs_4_.refs_0_.refs_2_), channel_id=1, source_target_pairs={{0,16},{8,24},{16,0},{24,8},{1,17},{9,25},{17,1},{25,9},{2,18},{10... | collective-permute-start | bytes 1572872 | tf_op jit(solution)/shard_map/ppermute | solution.py:509
  117.7 0.3 collective-permute-start.7
  118.1 0.0 copy-done.1
  118.1 12.8 %basis_left.2 = (f32[2,512,512]{2,1,0:T(8,128)}, f32[2,512,512]{2,1,0:T(8,128)}) custom-call(s32[3]{0:T(128)} %pad_add_fusion.place_ref, s32[32]{0:T(128)} %get-tuple-element.38.count_ref, f32[512,512]{1,0:T(8,128)} %get-tuple-element.56.g_hbm, f32[2,512,512]{2,1,0:T(8,128)} %s_hbm.5, f32[2,512,512]{2,1,0:T(8,128)} %q_hbm.5, bf16[8,64,512]{2,1,0:T(8,128)(2,1)} %copy-done.1), custom_call_target="tpu_custom_call" | custom-call | flops 8053063680 | bytes 5242880 | tf_op jit(solution)/shard_map/basis_left/pallas_call | solution.py:430
  130.9 12.6 %basis_right.3 = (f32[2,512,512]{2,1,0:T(8,128)}, f32[2,512,512]{2,1,0:T(8,128)}) custom-call(s32[3]{0:T(128)} %pad_add_fusion.place_ref, s32[32]{0:T(128)} %get-tuple-element.38.count_ref, f32[512,512]{1,0:T(8,128)} %get-tuple-element.55.g_hbm, f32[2,512,512]{2,1,0:T(8,128)} %s_hbm.7, ...), custom_call_target="tpu_custom_call", output_to_operand_aliasing={{0}: (5, {}), {1}: (6, {})} | custom-call | flops 8053063680 | bytes 5242880 | tf_op jit(solution)/shard_map/basis_right/pallas_call | solution.py:430
  143.5 0.0 collective-permute-done.4.refs_2_
  143.6 0.2 collective-permute-start.5
  143.8 0.0 collective-permute-done.8.refs_6_.refs_2_
  143.8 0.4 collective-permute-start.9
  144.1 0.5 copy-done.5
  144.6 13.0 %basis_left.3 = (f32[2,512,512]{2,1,0:T(8,128)}, f32[2,512,512]{2,1,0:T(8,128)}) custom-call(s32[3]{0:T(128)} %pad_add_fusion.place_ref, s32[32]{0:T(128)} %get-tuple-element.38.count_ref, f32[512,512]{1,0:T(8,128)} %get-tuple-element.55.g_hbm, f32[2,512,512]{2,1,0:T(8,128)} %s_hbm.5, ...), custom_call_target="tpu_custom_call", output_to_operand_aliasing={{0}: (5, {}), {1}: (6, {})} | custom-call | flops 8053063680 | bytes 5242880 | tf_op jit(solution)/shard_map/basis_left/pallas_call | solution.py:430
  157.6 0.0 collective-permute-done.3.refs_1_
  157.6 0.0 collective-permute-done.7.refs_5_
  157.6 0.0 collective-permute-done.5.refs_3_
  157.6 0.0 collective-permute-done.9.refs_7_
  157.6 0.0 copy-done.2
  157.6 0.0 copy-done.9
  157.7 0.0 copy-done.11
  157.7 0.0 copy-done.12
  157.7 0.0 copy-start.6
  157.7 1.0 copy-done.6
  158.7 3.9 %pick.1 = bf16[12,64,512]{2,1,0:T(8,128)(2,1)} custom-call(s32[3]{0:T(128)S(1)} %copy-done.9, s32[48]{0:T(128)S(1)} %copy-done.11, s32[48]{0:T(128)S(1)} %copy-done.12, bf16[8,64,512]{2,1,0:T(8,128)(2,1)S(1)} %all-to-all-done.1.refs_0_, bf16[8,64,512]{2,1,0:T(8,128)(2,1)S(1)} %collective-permute-done.3.refs_1_, ...), custom_call_target="tpu_custom_call" | custom-call | bytes 1572864 | tf_op jit(solution)/shard_map/pick/pallas_call | solution.py:475
  (9 shorter events, 0.0 us)
Async XLA Ops:
  4.7 4.2 %collective-permute-start = (bf16[2,8,64,512]{3,2,1,0:T(8,128)(2,1)}, bf16[2,8,64,512]{3,2,1,0:T(8,128)(2,1)}, u32[]{:S(2)}, u32[]{:S(2)}) collective-permute-start(bf16[2,8,64,512]{3,2,1,0:T(8,128)(2,1)} %get-tuple-element.41), channel_id=1, source_target_pairs={{0,8},{8,0},{16,24},{24,16},{1,9},{9,1},{17,25},{25,17},{2,10},{10... | collective-permute-start | bytes 3145736 | tf_op jit(solution)/shard_map/ppermute | solution.py:509
  5.5 3.4 %copy-start = (bf16[1,48,64,512]{3,2,1,0:T(8,128)(2,1)S(1)}, bf16[1,48,64,512]{3,2,1,0:T(8,128)(2,1)}, u32[]{:S(2)}) copy-start(bf16[1,48,64,512]{3,2,1,0:T(8,128)(2,1)} %param.9) | copy-start | bytes 9437188
  5.5 3.4 %copy-start.7 = (s32[3]{0:T(128)S(1)}, s32[3]{0:T(128)}, u32[]{:S(2)}) copy-start(s32[3]{0:T(128)} %pad_add_fusion.place_ref) | copy-start | bytes 40
  5.5 3.4 %copy-start.10 = (s32[64]{0:T(128)S(1)}, s32[64]{0:T(128)}, u32[]{:S(2)}) copy-start(s32[64]{0:T(128)} %get-tuple-element.40.block_ref) | copy-start | bytes 772
  8.8 16.4 %collective-permute-start.2 = (bf16[2,8,64,512]{3,2,1,0:T(8,128)(2,1)}, bf16[2,8,64,512]{3,2,1,0:T(8,128)(2,1)}, u32[]{:S(2)}, u32[]{:S(2)}) collective-permute-start(bf16[2,8,64,512]{3,2,1,0:T(8,128)(2,1)} %pack.1), channel_id=1, source_target_pairs={{0,8},{8,0},{16,24},{24,16},{1,9},{9,1},{17,25},{25,17},{2,10},{10... | collective-permute-start | bytes 3145736 | tf_op jit(solution)/shard_map/ppermute | solution.py:509
  13.0 17.3 %collective-permute-start.1 = (s16[1,8,272,128]{3,2,1,0:T(8,128)(2,1)}, s16[1,8,272,128]{3,2,1,0:T(8,128)(2,1)S(1)}, u32[]{:S(2)}, u32[]{:S(2)}) collective-permute-start(s16[1,8,272,128]{3,2,1,0:T(8,128)(2,1)} %get-tuple-element.42), channel_id=1, source_target_pairs={{0,16},{8,24},{16,0},{24,8},{1,17},{9,25},{17,1},{25,9},{2,18},{10... | collective-permute-start | bytes 1671176 | tf_op jit(solution)/shard_map/ppermute | solution.py:509
  14.2 11.0 %copy-start.8 = (s32[3]{0:T(128)S(1)}, s32[3]{0:T(128)}, u32[]{:S(2)}) copy-start(s32[3]{0:T(128)} %pad_add_fusion.place_ref) | copy-start | bytes 40
  29.4 0.8 copy-start.13
  35.0 0.8 copy-start.3
  35.8 24.4 %all-to-all-start = ((s16[8,272,128]{2,1,0:T(8,128)(2,1)}), s16[8,272,128]{2,1,0:T(8,128)(2,1)}, u32[]{:S(2)}, u32[]{:S(2)}) async-start(s16[8,272,128]{2,1,0:T(8,128)(2,1)} %bitcast.13), calls=%async_computation | async-start | bytes 1114112 | tf_op jit(solution)/shard_map/all_to_all | solution.py:535
  41.6 13.1 %collective-permute-start.6 = (s16[1,8,272,128]{3,2,1,0:T(8,128)(2,1)}, s16[1,8,272,128]{3,2,1,0:T(8,128)(2,1)S(1)}, u32[]{:S(2)}, u32[]{:S(2)}) collective-permute-start(s16[1,8,272,128]{3,2,1,0:T(8,128)(2,1)} %copy-done.13), channel_id=1, source_target_pairs={{0,16},{8,24},{16,0},{24,8},{1,17},{9,25},{17,1},{25,9},{2,18},{10... | collective-permute-start | bytes 1671176 | tf_op jit(solution)/shard_map/ppermute | solution.py:509
  59.4 0.8 copy-start.4
  60.3 18.9 %all-to-all-start.2 = ((s16[8,272,128]{2,1,0:T(8,128)(2,1)}), s16[8,272,128]{2,1,0:T(8,128)(2,1)S(1)}, u32[]{:S(2)}, u32[]{:S(2)}) async-start(s16[8,272,128]{2,1,0:T(8,128)(2,1)} %bitcast.14), calls=%async_computation.2 | async-start | bytes 1114112 | tf_op jit(solution)/shard_map/all_to_all | solution.py:535
  79.2 4.7 %copy-start.14 = (s16[8,272,128]{2,1,0:T(8,128)(2,1)}, s16[8,272,128]{2,1,0:T(8,128)(2,1)S(1)}, u32[]{:S(2)}) copy-start(s16[8,272,128]{2,1,0:T(8,128)(2,1)S(1)} %all-to-all-done.2.pay_ref) | copy-start | bytes 1671172
  79.2 17.6 %all-to-all-start.1 = ((bf16[8,64,512]{2,1,0:T(8,128)(2,1)}), bf16[8,64,512]{2,1,0:T(8,128)(2,1)S(1)}, u32[]{:S(2)}, u32[]{:S(2)}) async-start(bf16[8,64,512]{2,1,0:T(8,128)(2,1)} %bitcast.16), calls=%async_computation.1 | async-start | bytes 1048576 | tf_op jit(solution)/shard_map/all_to_all | solution.py:543
  96.8 19.3 %all-to-all-start.3 = ((bf16[8,64,512]{2,1,0:T(8,128)(2,1)}), bf16[8,64,512]{2,1,0:T(8,128)(2,1)S(1)}, u32[]{:S(2)}, u32[]{:S(2)}) async-start(bf16[8,64,512]{2,1,0:T(8,128)(2,1)} %bitcast.15), calls=%async_computation.3 | async-start | bytes 1048576 | tf_op jit(solution)/shard_map/all_to_all | solution.py:543
  113.9 29.6 %collective-permute-start.4 = (bf16[8,64,512]{2,1,0:T(8,128)(2,1)S(1)}, bf16[8,64,512]{2,1,0:T(8,128)(2,1)S(1)}, u32[]{:S(2)}, u32[]{:S(2)}) collective-permute-start(bf16[8,64,512]{2,1,0:T(8,128)(2,1)S(1)} %all-to-all-done.1.refs_0_), channel_id=1, source_target_pairs={{0,16},{8,24},{16,0},{24,8},{1,17},{9,25},{17,1},{25,9},{2,18},{10... | collective-permute-start | bytes 1572872 | tf_op jit(solution)/shard_map/ppermute | solution.py:509
  114.0 43.6 %collective-permute-start.3 = (bf16[8,64,512]{2,1,0:T(8,128)(2,1)S(1)}, bf16[8,64,512]{2,1,0:T(8,128)(2,1)S(1)}, u32[]{:S(2)}, u32[]{:S(2)}) collective-permute-start(bf16[8,64,512]{2,1,0:T(8,128)(2,1)S(1)} %all-to-all-done.1.refs_0_), channel_id=1, source_target_pairs={{0,8},{8,0},{16,24},{24,16},{1,9},{9,1},{17,25},{25,17},{2,10},{10... | collective-permute-start | bytes 1572872 | tf_op jit(solution)/shard_map/ppermute | solution.py:509
  116.1 2.0 %copy-start.1 = (bf16[8,64,512]{2,1,0:T(8,128)(2,1)}, bf16[8,64,512]{2,1,0:T(8,128)(2,1)S(1)}, u32[]{:S(2)}) copy-start(bf16[8,64,512]{2,1,0:T(8,128)(2,1)S(1)} %all-to-all-done.3.refs_4_.refs_0_.refs_2_) | copy-start | bytes 1572868
  116.1 27.7 %collective-permute-start.8 = (bf16[8,64,512]{2,1,0:T(8,128)(2,1)S(1)}, bf16[8,64,512]{2,1,0:T(8,128)(2,1)S(1)}, u32[]{:S(2)}, u32[]{:S(2)}) collective-permute-start(bf16[8,64,512]{2,1,0:T(8,128)(2,1)S(1)} %all-to-all-done.3.refs_4_.refs_0_.refs_2_), channel_id=1, source_target_pairs={{0,16},{8,24},{16,0},{24,8},{1,17},{9,25},{17,1},{25,9},{2,18},{10... | collective-permute-start | bytes 1572872 | tf_op jit(solution)/shard_map/ppermute | solution.py:509
  117.7 39.9 %collective-permute-start.7 = (bf16[8,64,512]{2,1,0:T(8,128)(2,1)S(1)}, bf16[8,64,512]{2,1,0:T(8,128)(2,1)S(1)}, u32[]{:S(2)}, u32[]{:S(2)}) collective-permute-start(bf16[8,64,512]{2,1,0:T(8,128)(2,1)S(1)} %all-to-all-done.3.refs_4_.refs_0_.refs_2_), channel_id=1, source_target_pairs={{0,8},{8,0},{16,24},{24,16},{1,9},{9,1},{17,25},{25,17},{2,10},{10... | collective-permute-start | bytes 1572872 | tf_op jit(solution)/shard_map/ppermute | solution.py:509
  143.6 14.1 %collective-permute-start.5 = (bf16[8,64,512]{2,1,0:T(8,128)(2,1)S(1)}, bf16[8,64,512]{2,1,0:T(8,128)(2,1)}, u32[]{:S(2)}, u32[]{:S(2)}) collective-permute-start(bf16[8,64,512]{2,1,0:T(8,128)(2,1)S(1)} %collective-permute-done.4.refs_2_), channel_id=1, source_target_pairs={{0,8},{8,0},{16,24},{24,16},{1,9},{9,1},{17,25},{25,17},{2,10},{10... | collective-permute-start | bytes 1572872 | tf_op jit(solution)/shard_map/ppermute | solution.py:509
  143.8 0.8 copy-start.5
  143.8 13.8 %collective-permute-start.9 = (bf16[8,64,512]{2,1,0:T(8,128)(2,1)S(1)}, bf16[8,64,512]{2,1,0:T(8,128)(2,1)}, u32[]{:S(2)}, u32[]{:S(2)}) collective-permute-start(bf16[8,64,512]{2,1,0:T(8,128)(2,1)S(1)} %collective-permute-done.8.refs_6_.refs_2_), channel_id=1, source_target_pairs={{0,8},{8,0},{16,24},{24,16},{1,9},{9,1},{17,25},{25,17},{2,10},{10... | collective-permute-start | bytes 1572872 | tf_op jit(solution)/shard_map/ppermute | solution.py:509
  144.6 13.0 %copy-start.2 = (bf16[8,64,512]{2,1,0:T(8,128)(2,1)S(1)}, bf16[8,64,512]{2,1,0:T(8,128)(2,1)}, u32[]{:S(2)}) copy-start(bf16[8,64,512]{2,1,0:T(8,128)(2,1)} %copy-done.1) | copy-start | bytes 1572868
  144.6 13.0 %copy-start.9 = (s32[3]{0:T(128)S(1)}, s32[3]{0:T(128)}, u32[]{:S(2)}) copy-start(s32[3]{0:T(128)} %pad_add_fusion.place_ref) | copy-start | bytes 40
  144.6 13.1 %copy-start.11 = (s32[48]{0:T(128)S(1)}, s32[48]{0:T(128)}, u32[]{:S(2)}) copy-start(s32[48]{0:T(128)} %owner_ref.3) | copy-start | bytes 580
  144.6 13.1 %copy-start.12 = (s32[48]{0:T(128)S(1)}, s32[48]{0:T(128)}, u32[]{:S(2)}) copy-start(s32[48]{0:T(128)} %get-tuple-element.37.rank_ref) | copy-start | bytes 580
  157.7 1.0 copy-start.6

commit v4 on v3

--- a/solution.py
+++ b/solution.py
@@ -17,6 +17,7 @@
 MIB = 1 << 20
 ROOMY = 24 * MIB
 WEIGHT = 1.0
+LATE = 8
 F32 = jnp.float32
 BF16 = jnp.bfloat16
 ANY = pl.BlockSpec(memory_space=pl.ANY)
@@ -149,7 +150,7 @@
     lax.fori_loop(0, count * members, piece, 0)
 
 
-def fold(rank, first, count, place, block_at, grads, from_core, from_x, members, after=()):
+def fold(rank, first, count, place, block_at, grads, from_core, from_x, members, after=(), weight=8):
     rows, width = grads.shape[1:]
     tall = (width // LANES) * rows + TAIL
     devices = 2 * from_core.shape[0] * members
@@ -170,7 +171,7 @@
             pltpu.SemaphoreType.DMA((count * members,)),
         ],
         compiler_params=params(ROOMY),
-        cost_estimate=cost(0, 8 * count * members * rows * width),
+        cost_estimate=cost(0, weight * count * members * rows * width),
         name="fold",
     )(place, block_at, grads, from_core, *from_x, *after)
 
@@ -278,7 +279,7 @@
         copies = Copies(sems)
         loads = [copies.start(m_hbm.at[rank], m_ref), copies.start(v_hbm.at[rank], v_ref)]
         u_ref[...] = jnp.zeros_like(u_ref)
-        stores = [copies.start(u_ref, u_hbm)]
+        stores = [copies.start(u_ref, u_hbm.at[:, rank])]
         for load in loads:
             load.wait()
         stores += [copies.start(m_ref, m1_hbm.at[rank]), copies.start(v_ref, v1_hbm.at[rank])]
@@ -328,9 +329,9 @@
         put_cols(qrp_ref, slice(None), qr_ref[...], (0, 1, 0))
         depth = (place_ref[2] - 1 - depth_ref[base + place_ref[1]]).astype(F32)
         factor = jnp.exp(SHRINK * jnp.full((1, width), depth, F32))
-        for t in tiles(width):
-            u_ref[t, :] = (factor * dot_nt(ab_ref[t, :], qrp_ref[...])).astype(BF16)
-        stores.append(copies.start(u_ref, u_hbm))
+        direction = (factor * dot_nt(ab_ref[...], qrp_ref[...])).astype(BF16)
+        u_ref[...] = direction.reshape(members, rows, width)
+        stores.append(copies.start(u_ref, u_hbm.at[:, rank]))
         load_m.wait()
         m_ref[...] = BETA_ONE * m_ref[...] + (1.0 - BETA_ONE) * g_ref[...]
         stores.append(copies.start(m_ref, m1_hbm.at[rank]))
@@ -339,7 +340,8 @@
 
 
 def update_call(rank, info, pay, ql, qr, m, v, mq, carried):
-    width = ql.shape[1]
+    slots, width = ql.shape[:2]
+    members = pay.shape[0]
     state = jax.ShapeDtypeStruct(m.shape, F32)
     flat = pltpu.VMEM((width, width), F32)
     wide = pltpu.VMEM((width, 3 * width), BF16)
@@ -349,16 +351,16 @@
         grid=(1,),
         out_shape=(
             jax.ShapeDtypeStruct((width, width), F32),
-            jax.ShapeDtypeStruct((width, width), BF16),
+            jax.ShapeDtypeStruct((members, slots, width // members, width), BF16),
             state,
             state,
         ),
         in_specs=[SMEM] * 3 + [pl.BlockSpec(pay.shape, lambda *_: (0, 0, 0))] + [ANY] * (5 + len(carried)),
         out_specs=(ANY,) * 4,
-        scratch_shapes=[flat, pltpu.VMEM((width, width), BF16)]
+        scratch_shapes=[flat, pltpu.VMEM((members, width // members, width), BF16)]
         + [flat] * 5
         + [wide, wide, tall, wide, tall, tall, wide, wide, pltpu.SemaphoreType.DMA((9,))],
-        input_output_aliases={9: 2, 10: 3} if carried else {},
+        input_output_aliases={9: 1, 10: 2, 11: 3} if carried else {},
         compiler_params=params(),
         cost_estimate=cost(4 * 3 * 2 * width**3, 10 * 4 * width**2),
         name="update",
@@ -366,7 +368,8 @@
 
 
 def basis_kernel(rank, left, place_ref, count_ref, g_hbm, s_hbm, q_hbm, *refs):
-    s1_hbm, q1_hbm, g_ref, s_ref, q_ref, y_ref, cols_ref, a_ref, b_ref, sems = refs[-10:]
+    s1_hbm, q1_hbm, done_ref, g_ref, s_ref, q_ref, y_ref, cols_ref, a_ref, b_ref, sems = refs[-11:]
+    done_ref[0] = 1
     width = g_ref.shape[0]
     live = count_ref[place_ref[1]] > rank
     near, far, one = pl.ds(0, 3 * width), pl.ds(width, 3 * width), pl.ds(0, width)
@@ -429,9 +432,9 @@
     flat = pltpu.VMEM((width, width), F32)
     return pl.pallas_call(
         functools.partial(basis_kernel, rank, left),
-        out_shape=(state, state),
-        in_specs=[SMEM, SMEM] + [ANY] * (3 + len(carried) + len(after)),
-        out_specs=(ANY, ANY),
+        out_shape=(state, state, jax.ShapeDtypeStruct((1,), jnp.int32)),
+        in_specs=[SMEM, SMEM] + [ANY] * (3 + len(carried)) + [SMEM] * len(after),
+        out_specs=(ANY, ANY, SMEM),
         scratch_shapes=[flat] * 4
         + [
             pltpu.VMEM((width, 4 * width), BF16),
@@ -446,42 +449,42 @@
     )(*info[:2], grad, stat, basis, *carried, *after)
 
 
-def pick_kernel(groups, members, count, place_ref, owner_ref, rank_ref, *refs):
+def pick_kernel(members, count, place_ref, owner_ref, rank_ref, after_ref, *refs):
     sources, out_ref, sems = refs[:-2], refs[-2], refs[-1]
 
     def start(i, carry):
         block = place_ref[0] * count + i
         owner = owner_ref[block]
-        which = rank_ref[block] * groups + ((owner // members) ^ place_ref[0])
+        which = (owner // members) ^ place_ref[0]
         for n, source in enumerate(sources):
 
             @pl.when(which == n)
             def _():
-                pltpu.make_async_copy(source.at[owner % members], out_ref.at[i], sems.at[i]).start()
+                pltpu.make_async_copy(source.at[owner % members, rank_ref[block]], out_ref.at[i], sems.at[i]).start()
 
         return carry
 
     def wait(i, carry):
-        pltpu.make_async_copy(sources[0].at[0], out_ref.at[i], sems.at[i]).wait()
+        pltpu.make_async_copy(sources[0].at[0, 0], out_ref.at[i], sems.at[i]).wait()
         return carry
 
     lax.fori_loop(0, count, start, 0)
     lax.fori_loop(0, count, wait, 0)
 
 
-def pick(place, owner_device, rank_of, sources, groups, members):
-    rows, width = sources[0].shape[1:]
+def pick(place, owner_device, rank_of, sources, groups, members, after):
+    rows, width = sources[0].shape[2:]
     count = owner_device.shape[0] // groups
     return pl.pallas_call(
-        functools.partial(pick_kernel, groups, members, count),
+        functools.partial(pick_kernel, members, count),
         out_shape=jax.ShapeDtypeStruct((count, rows, width), BF16),
-        in_specs=[SMEM] * 3 + [ANY] * len(sources),
+        in_specs=[SMEM] * 4 + [ANY] * len(sources),
         out_specs=pl.BlockSpec(memory_space=pltpu.VMEM),
         scratch_shapes=[pltpu.SemaphoreType.DMA((count,))],
         compiler_params=params(ROOMY),
         cost_estimate=cost(0, 4 * count * rows * width),
         name="pick",
-    )(place, owner_device, rank_of, *sources)
+    )(place, owner_device, rank_of, after, *sources)
 
 
 def local(
@@ -530,36 +533,36 @@
 
     arrived = []
     for k in range(capacity):
-        ready, mark = fold(k, 0, 1, place, block_at, grads, from_core[k], from_x[k], members, after)
+        ready, mark = fold(k, 0, 1, place, block_at, grads, from_core[k], from_x[k], members, after, LATE if k else 8)
         after = (mark,)
         arrived.append(lax.all_to_all(ready[0], "mp", split_axis=0, concat_axis=0, tiled=True))
 
-    sources, gradients, moments, returned, crossed = [], [], (), [], []
+    gradients, carried = [], ()
     for k in range(capacity):
-        grad, block_update, *moments = update_call(
-            k, info, arrived[k], basis_left, basis_right, moment_first, moment_second, mixed, tuple(moments)
+        grad, *carried = update_call(
+            k, info, arrived[k], basis_left, basis_right, moment_first, moment_second, mixed, tuple(carried)
         )
         gradients.append(grad)
-        pieces = lax.all_to_all(
-            block_update.reshape(members, rows, width), "mp", split_axis=0, concat_axis=0, tiled=True
-        )
-        held = [pieces]
-        step = 1
-        while step < halves:
-            held = held + [flip(part, 2 * step) for part in held]
-            step *= 2
-        returned.append(pieces)
-        crossed.append(held[-1])
-        for part in held:
-            sources += [part, flip(part, 1)]
-
-    lefts, rights = (), ()
-    waits = [(), (returned[-1],)] + [(returned[-1],)] * (2 * capacity - 3) + [(crossed[-1],)]
+    block_updates, *moments = carried
+    returned = lax.all_to_all(block_updates, "mp", split_axis=0, concat_axis=0, tiled=True)
+    lefts, rights, after = (), (), ()
     for k in range(capacity):
-        rights = basis_call(k, False, info, gradients[k], stat_right, basis_right, tuple(rights), waits[2 * k])
-        lefts = basis_call(k, True, info, gradients[k], stat_left, basis_left, tuple(lefts), waits[2 * k + 1])
-
-    update_rows = pick(place, owner_device, rank_of, sources, groups, members)
+        *rights, mark = basis_call(k, False, info, gradients[k], stat_right, basis_right, tuple(rights), after)
+        *lefts, mark = basis_call(k, True, info, gradients[k], stat_left, basis_left, tuple(lefts), (mark,))
+        if k == 0:
+            returned, mark = lax.optimization_barrier((returned, mark))
+            after = (mark,)
+            held = [returned]
+            step = 1
+            while step < halves:
+                held = held + [flip(part, 2 * step) for part in held]
+                step *= 2
+    *far, mark = lax.optimization_barrier((*held[1:], mark))
+    sources = []
+    for part in held[:1] + far:
+        sources += [part, flip(part, 1)]
+
+    update_rows = pick(place, owner_device, rank_of, sources, groups, members, mark)
     return (update_rows, lefts[0], rights[0], lefts[1], rights[1], moments[0], moments[1])
 
 

time: 165 us -> 158 us (0.958)
  starting transfers between devices: 27.4 us -> 20.4 us
  Pallas kernels: 107 us -> 111 us
  waiting for transfers between devices: 22.5 us -> 20.6 us
    all_to_all x2 -> x1, starting transfers between devices: 9.24 us -> 4.73 us  [local(): lax.all_to_all(block_updates, 'mp', split_axis=0, concat_axis=0, tiled=True)]
    all_to_all x2 -> x1, waiting for transfers between devices: 4.39 us -> 0.01 us  [local(): lax.all_to_all(block_updates, 'mp', split_axis=0, concat_axis=0, tiled=True)]
    pallas_call x4, Pallas kernels: 51 us -> 54.8 us  [basis_call(): pl.pallas_call(functools.partial(basis_kernel, rank, left), out_shape=(st...]
    ppermute x10 -> x7, starting transfers between devices: 6.86 us -> 4.35 us  [flip(): return lax.ppermute(x, 'dp', [(i, i ^ bits) for i in range(groups)])]
    ppermute x10 -> x7, waiting for transfers between devices: 13.1 us -> 15.6 us  [flip(): return lax.ppermute(x, 'dp', [(i, i ^ bits) for i in range(groups)])]
    unnamed x30 -> x22, local copies, waits for them, and re-layouts: 3.93 us -> 3.23 us
  transfers between devices with their start and end apart: 14 -> 10, of which waited for: 3 -> 3; matrix products, arithmetic and copies ran while one was open for 0% -> 0% of each run, Pallas kernels for 58% -> 58%
where the time goes in v4:
time: 158 us; the launch traced here: 157 us
  Pallas kernels  111 us (70%)
  waiting for transfers between devices  20.6 us (13%)
  starting transfers between devices  20.4 us (13%)
  local copies, waits for them, and re-layouts  3.23 us (2%)
    pallas_call x4, Pallas kernels, basis_call(): pl.pallas_call(functools.partial(basis_kernel, rank, left), out_shape=(st...  54.8 us
    pallas_call x4, Pallas kernels, fold(): pl.pallas_call(functools.partial(fold_kernel, rank * devices, first, memb...  17.8 us
    pallas_call x2, Pallas kernels, update_call(): pl.pallas_call(functools.partial(update_kernel, rank, rank * info[1].shap...  16.8 us
    ppermute x7, waiting for transfers between devices, flip(): return lax.ppermute(x, 'dp', [(i, i ^ bits) for i in range(groups)])  15.6 us
    all_to_all x2, starting transfers between devices, local(): lax.all_to_all(ready[0], 'mp', split_axis=0, concat_axis=0, tiled=True)  11.3 us
    pallas_call x1, Pallas kernels, premix(): pl.pallas_call(functools.partial(premix_kernel, slots), out_shape=(jax.Sh...  10.9 us
    all_to_all x2, waiting for transfers between devices, local(): lax.all_to_all(ready[0], 'mp', split_axis=0, concat_axis=0, tiled=True)  5.06 us
    all_to_all x1, starting transfers between devices, local(): lax.all_to_all(block_updates, 'mp', split_axis=0, concat_axis=0, tiled=True)  4.73 us
  transfers between devices with their start and end apart: 10, of which 3 were waited for; matrix products, arithmetic and copies ran while one was open for 0% of the time, Pallas kernels for 58%

profile of v4, /device:TPU:5, one launch (start us, length us, event | category | flops | bytes accessed | tf_op | source)
XLA Modules:
  0.0 156.8 jit_solution(56283160186026657)
XLA Ops:
  0.6 0.6 pad_add_fusion.place_ref
  1.2 3.4 %route.1 = (s32[64]{0:T(128)}, s32[48]{0:T(128)}, s32[32]{0:T(128)}, s32[64]{0:T(128)}, bf16[2,8,64,512]{3,2,1,0:T(8,128)(2,1)}) custom-call(s32[48]{0:T(128)} %owner_ref.3, s32[48]{0:T(128)} %layer_ref.1, s32[3]{0:T(128)} %pad_add_fusion.place_ref, bf16[48,64,512]{2,1,0:T(8,128)(2,1)} %bitcast.5), custom_call_target="tpu_custom_call" | custom-call | bytes 2097152 | tf_op jit(solution)/shard_map/route/pallas_call | solution.py:72
  4.7 0.7 collective-permute-start.1
  5.4 0.0 copy-start
  5.4 0.0 copy-start.3
  5.4 0.0 copy-start.6
  5.4 3.4 %pack.1 = bf16[2,8,64,512]{3,2,1,0:T(8,128)(2,1)} custom-call(s32[3]{0:T(128)} %pad_add_fusion.place_ref, s32[64]{0:T(128)} %get-tuple-element.48.block_ref, bf16[48,64,512]{2,1,0:T(8,128)(2,1)} %bitcast.6), custom_call_target="tpu_custom_call" | custom-call | bytes 2097152 | tf_op jit(solution)/shard_map/pack/pallas_call | solution.py:92
  8.8 0.1 collective-permute-start
  8.9 0.0 collective-permute-done.1.core_ref
  8.9 0.0 copy-done
  8.9 0.0 copy-done.3
  8.9 0.0 copy-done.6
  8.9 4.0 %fold.4 = (s16[1,8,272,128]{3,2,1,0:T(8,128)(2,1)}, s32[1]{0:T(128)}) custom-call(s32[3]{0:T(128)S(1)} %copy-done.3, s32[64]{0:T(128)S(1)} %copy-done.6, bf16[48,64,512]{2,1,0:T(8,128)(2,1)S(1)} %bitcast.7, bf16[2,8,64,512]{3,2,1,0:T(8,128)(2,1)} %collective-permute-done.1.core_ref), custom_call_target="tpu_custom_call" | custom-call | bytes 2097152 | tf_op jit(solution)/shard_map/fold/pallas_call | solution.py:158
  12.9 1.3 collective-permute-start.3
  14.2 0.0 copy-start.4
  14.2 10.9 %premix.1 = (f32[2,512,512]{2,1,0:T(8,128)}, s32[1]{0:T(128)}) custom-call(s32[3]{0:T(128)} %pad_add_fusion.place_ref, s32[32]{0:T(128)} %get-tuple-element.46.count_ref, f32[2,512,512]{2,1,0:T(8,128)} %q_hbm.7, f32[2,512,512]{2,1,0:T(8,128)} %q_hbm.6, f32[2,512,512]{2,1,0:T(8,128)} %m_hbm.5, s32[1]{0:T(128)} %get-tuple-element.50.refs_0_), custom_call_target="tpu_custom_call" | custom-call | flops 3221225472 | bytes 8388608 | tf_op jit(solution)/shard_map/premix/pallas_call | solution.py:256
  25.2 0.0 collective-permute-done.core_ref
  25.2 0.0 copy-done.4
  25.2 4.2 %fold.5 = (s16[1,8,272,128]{3,2,1,0:T(8,128)(2,1)S(1)}, s32[1]{0:T(128)}) custom-call(s32[3]{0:T(128)S(1)} %copy-done.4, s32[64]{0:T(128)S(1)} %copy-done.6, bf16[48,64,512]{2,1,0:T(8,128)(2,1)S(1)} %bitcast.8, bf16[2,8,64,512]{3,2,1,0:T(8,128)(2,1)} %collective-permute-done.core_ref, s32[1]{0:T(128)} %get-tuple-element.51.refs_0_), custom_call_target="tpu_custom_call" | custom-call | bytes 2097152 | tf_op jit(solution)/shard_map/fold/pallas_call | solution.py:158
  29.4 0.0 copy-start.9
  29.4 0.8 copy-done.9
  30.2 0.0 collective-permute-done.3.refs_0_
  30.2 4.8 %fold.6 = (s16[1,8,272,128]{3,2,1,0:T(8,128)(2,1)S(1)}, s32[1]{0:T(128)}) custom-call(s32[3]{0:T(128)S(1)} %copy-done.4, s32[64]{0:T(128)S(1)} %copy-done.6, bf16[48,64,512]{2,1,0:T(8,128)(2,1)S(1)} %bitcast.9, bf16[2,8,64,512]{3,2,1,0:T(8,128)(2,1)} %collective-permute-done.1.core_ref, s16[1,8,272,128]{3,2,1,0:T(8,128)(2,1)S(1)} %collective-permute-done.3.refs_0_, ...), custom_call_target="tpu_custom_call" | custom-call | bytes 2097152 | tf_op jit(solution)/shard_map/fold/pallas_call | solution.py:158
  35.0 0.0 copy-start.1
  35.0 0.8 copy-done.1
  35.8 5.8 %all-to-all-start.1 = ((s16[8,272,128]{2,1,0:T(8,128)(2,1)}), s16[8,272,128]{2,1,0:T(8,128)(2,1)}, u32[]{:S(2)}, u32[]{:S(2)}) async-start(s16[8,272,128]{2,1,0:T(8,128)(2,1)} %bitcast.11), calls=%async_computation.1 | async-start | bytes 1114112 | tf_op jit(solution)/shard_map/all_to_all | solution.py:538
  41.6 0.0 collective-permute-start.2
  41.6 13.0 %collective-permute-done.2.refs_0_ = s16[1,8,272,128]{3,2,1,0:T(8,128)(2,1)S(1)} collective-permute-done((s16[1,8,272,128]{3,2,1,0:T(8,128)(2,1)}, s16[1,8,272,128]{3,2,1,0:T(8,128)(2,1)S(1)}, u32[]{:S(2)}, u32[]{:S(2)}) %collective-permute-start.2) | collective-permute-done | bytes 557088 | tf_op jit(solution)/shard_map/ppermute | solution.py:512
  54.6 4.8 %fold.7 = (s16[1,8,272,128]{3,2,1,0:T(8,128)(2,1)S(1)}, s32[1]{0:T(128)}) custom-call(s32[3]{0:T(128)S(1)} %copy-done.4, s32[64]{0:T(128)S(1)} %copy-done.6, bf16[48,64,512]{2,1,0:T(8,128)(2,1)S(1)} %bitcast.10, bf16[2,8,64,512]{3,2,1,0:T(8,128)(2,1)} %collective-permute-done.core_ref, s16[1,8,272,128]{3,2,1,0:T(8,128)(2,1)S(1)} %collective-permute-done.2.refs_0_, ...), custom_call_target="tpu_custom_call" | custom-call | bytes 2097152 | tf_op jit(solution)/shard_map/fold/pallas_call | solution.py:158
  59.4 0.0 copy-start.2
  59.4 0.8 copy-done.2
  60.2 0.0 all-to-all-done.1.pay_ref
  60.2 5.5 %all-to-all-start = ((s16[8,272,128]{2,1,0:T(8,128)(2,1)}), s16[8,272,128]{2,1,0:T(8,128)(2,1)S(1)}, u32[]{:S(2)}, u32[]{:S(2)}) async-start(s16[8,272,128]{2,1,0:T(8,128)(2,1)} %bitcast.12), calls=%async_computation | async-start | bytes 1114112 | tf_op jit(solution)/shard_map/all_to_all | solution.py:538
  65.7 8.3 %update.2 = (f32[512,512]{1,0:T(8,128)}, bf16[8,2,64,512]{3,2,1,0:T(8,128)(2,1)}, f32[2,512,512]{2,1,0:T(8,128)}, f32[2,512,512]{2,1,0:T(8,128)}) custom-call(s32[3]{0:T(128)} %pad_add_fusion.place_ref, s32[32]{0:T(128)} %get-tuple-element.46.count_ref, s32[64]{0:T(128)} %get-tuple-element.47.depth_ref, s16[8,272,128]{2,1,0:T(8,128)(2,1)} %all-to-all-done.1.pay_ref, ...), custom_call_target="tpu_custom_call" | custom-call | flops 3221225472 | bytes 10485760 | tf_op jit(solution)/shard_map/update/pallas_call | solution.py:349
  74.0 5.1 %all-to-all-done.pay_ref = s16[8,272,128]{2,1,0:T(8,128)(2,1)S(1)} async-done(((s16[8,272,128]{2,1,0:T(8,128)(2,1)}), s16[8,272,128]{2,1,0:T(8,128)(2,1)S(1)}, u32[]{:S(2)}, u32[]{:S(2)}) %all-to-all-start) | async-done | bytes 557088 | tf_op jit(solution)/shard_map/all_to_all | solution.py:538
  79.1 0.0 copy-start.10
  79.1 0.8 copy-done.10
  79.9 8.5 %update.3 = (f32[512,512]{1,0:T(8,128)}, bf16[8,2,64,512]{3,2,1,0:T(8,128)(2,1)}, f32[2,512,512]{2,1,0:T(8,128)}, f32[2,512,512]{2,1,0:T(8,128)}) custom-call(s32[3]{0:T(128)} %pad_add_fusion.place_ref, s32[32]{0:T(128)} %get-tuple-element.46.count_ref, s32[64]{0:T(128)} %get-tuple-element.47.depth_ref, ...), custom_call_target="tpu_custom_call", output_to_operand_aliasing={{1}: (9, {}), {2}: (10, {}), {3}: (11, {})} | custom-call | flops 3221225472 | bytes 10485760 | tf_op jit(solution)/shard_map/update/pallas_call | solution.py:349
  88.4 4.7 %all-to-all-start.2 = ((bf16[8,2,64,512]{3,2,1,0:T(8,128)(2,1)}), bf16[8,2,64,512]{3,2,1,0:T(8,128)(2,1)S(1)}, u32[]{:S(2)}, u32[]{:S(2)}) async-start(bf16[8,2,64,512]{3,2,1,0:T(8,128)(2,1)} %get-tuple-element.62), calls=%async_computation.2 | async-start | bytes 2097152 | tf_op jit(solution)/shard_map/all_to_all | solution.py:547
  93.1 13.1 %basis_right.2 = (f32[2,512,512]{2,1,0:T(8,128)}, f32[2,512,512]{2,1,0:T(8,128)}, s32[1]{0:T(128)}) custom-call(s32[3]{0:T(128)} %pad_add_fusion.place_ref, s32[32]{0:T(128)} %get-tuple-element.46.count_ref, f32[512,512]{1,0:T(8,128)} %get-tuple-element.63.g_hbm, f32[2,512,512]{2,1,0:T(8,128)} %s_hbm.6, f32[2,512,512]{2,1,0:T(8,128)} %q_hbm.6), custom_call_target="tpu_custom_call" | custom-call | flops 8053063680 | bytes 5242880 | tf_op jit(solution)/shard_map/basis_right/pallas_call | solution.py:433
  106.3 14.0 %basis_left.2 = (f32[2,512,512]{2,1,0:T(8,128)}, f32[2,512,512]{2,1,0:T(8,128)}, s32[1]{0:T(128)}) custom-call(s32[3]{0:T(128)} %pad_add_fusion.place_ref, s32[32]{0:T(128)} %get-tuple-element.46.count_ref, f32[512,512]{1,0:T(8,128)} %get-tuple-element.63.g_hbm, f32[2,512,512]{2,1,0:T(8,128)} %s_hbm.7, f32[2,512,512]{2,1,0:T(8,128)} %q_hbm.7, ...), custom_call_target="tpu_custom_call" | custom-call | flops 8053063680 | bytes 5242880 | tf_op jit(solution)/shard_map/basis_left/pallas_call | solution.py:433
  120.2 0.0 all-to-all-done.2.refs_0_
  120.3 2.1 %collective-permute-start.5 = (bf16[8,2,64,512]{3,2,1,0:T(8,128)(2,1)S(1)}, bf16[8,2,64,512]{3,2,1,0:T(8,128)(2,1)S(1)}, u32[]{:S(2)}, u32[]{:S(2)}) collective-permute-start(bf16[8,2,64,512]{3,2,1,0:T(8,128)(2,1)S(1)} %all-to-all-done.2.refs_0_), channel_id=1, source_target_pairs={{0,8},{8,0},{16,24},{24,16},{1,9},{9,1},{17,25},{25,17},{2,10},{10... | collective-permute-start | bytes 3145736 | tf_op jit(solution)/shard_map/ppermute | solution.py:512
  122.4 0.0 collective-permute-start.4
  122.4 13.7 %basis_right.3 = (f32[2,512,512]{2,1,0:T(8,128)}, f32[2,512,512]{2,1,0:T(8,128)}, s32[1]{0:T(128)}) custom-call(s32[3]{0:T(128)} %pad_add_fusion.place_ref, s32[32]{0:T(128)} %get-tuple-element.46.count_ref, f32[512,512]{1,0:T(8,128)} %get-tuple-element.67.g_hbm, f32[2,512,512]{2,1,0:T(8,128)} %s_hbm.6, ...), custom_call_target="tpu_custom_call", output_to_operand_aliasing={{0}: (5, {}), {1}: (6, {})} | custom-call | flops 8053063680 | bytes 5242880 | tf_op jit(solution)/shard_map/basis_right/pallas_call | solution.py:433
  136.1 0.0 copy-start.5
  136.1 0.0 copy-start.7
  136.1 0.0 copy-start.8
  136.1 14.0 %basis_left.3 = (f32[2,512,512]{2,1,0:T(8,128)}, f32[2,512,512]{2,1,0:T(8,128)}, s32[1]{0:T(128)}) custom-call(s32[3]{0:T(128)} %pad_add_fusion.place_ref, s32[32]{0:T(128)} %get-tuple-element.46.count_ref, f32[512,512]{1,0:T(8,128)} %get-tuple-element.67.g_hbm, f32[2,512,512]{2,1,0:T(8,128)} %s_hbm.7, ...), custom_call_target="tpu_custom_call", output_to_operand_aliasing={{0}: (5, {}), {1}: (6, {})} | custom-call | flops 8053063680 | bytes 5242880 | tf_op jit(solution)/shard_map/basis_left/pallas_call | solution.py:433
  150.1 0.0 collective-permute-done.4.refs_2_
  150.1 0.2 collective-permute-start.6
  150.3 0.0 collective-permute-done.5.refs_1_
  150.3 2.6 %collective-permute-done.6.refs_3_ = bf16[8,2,64,512]{3,2,1,0:T(8,128)(2,1)S(1)} collective-permute-done((bf16[8,2,64,512]{3,2,1,0:T(8,128)(2,1)S(1)}, bf16[8,2,64,512]{3,2,1,0:T(8,128)(2,1)S(1)}, u32[]{:S(2)}, u32[]{:S(2)}) %collective-permute-start.6) | collective-permute-done | bytes 1048608 | tf_op jit(solution)/shard_map/ppermute | solution.py:512
  152.9 0.0 copy-done.5
  152.9 0.0 copy-done.7
  152.9 0.0 copy-done.8
  152.9 3.7 %pick.1 = bf16[12,64,512]{2,1,0:T(8,128)(2,1)} custom-call(s32[3]{0:T(128)S(1)} %copy-done.5, s32[48]{0:T(128)S(1)} %copy-done.7, s32[48]{0:T(128)S(1)} %copy-done.8, s32[1]{0:T(128)} %get-tuple-element.75.after_ref, bf16[8,2,64,512]{3,2,1,0:T(8,128)(2,1)S(1)} %all-to-all-done.2.refs_0_, bf16[8,2,64,512]{3,2,1,0:T(8,128)(2,1)S(1)} %collective-permute-done.5.refs_1_, ...), custom_call_target="tpu_custom_call" | custom-call | bytes 1572864 | tf_op jit(solution)/shard_map/pick/pallas_call | solution.py:478
Async XLA Ops:
  4.7 4.2 %collective-permute-start.1 = (bf16[2,8,64,512]{3,2,1,0:T(8,128)(2,1)}, bf16[2,8,64,512]{3,2,1,0:T(8,128)(2,1)}, u32[]{:S(2)}, u32[]{:S(2)}) collective-permute-start(bf16[2,8,64,512]{3,2,1,0:T(8,128)(2,1)} %get-tuple-element.49), channel_id=1, source_target_pairs={{0,8},{8,0},{16,24},{24,16},{1,9},{9,1},{17,25},{25,17},{2,10},{10... | collective-permute-start | bytes 3145736 | tf_op jit(solution)/shard_map/ppermute | solution.py:512
  5.4 3.5 %copy-start = (bf16[1,48,64,512]{3,2,1,0:T(8,128)(2,1)S(1)}, bf16[1,48,64,512]{3,2,1,0:T(8,128)(2,1)}, u32[]{:S(2)}) copy-start(bf16[1,48,64,512]{3,2,1,0:T(8,128)(2,1)} %param.9) | copy-start | bytes 9437188
  5.4 3.5 %copy-start.3 = (s32[3]{0:T(128)S(1)}, s32[3]{0:T(128)}, u32[]{:S(2)}) copy-start(s32[3]{0:T(128)} %pad_add_fusion.place_ref) | copy-start | bytes 40
  5.4 3.5 %copy-start.6 = (s32[64]{0:T(128)S(1)}, s32[64]{0:T(128)}, u32[]{:S(2)}) copy-start(s32[64]{0:T(128)} %get-tuple-element.48.block_ref) | copy-start | bytes 772
  8.8 16.4 %collective-permute-start = (bf16[2,8,64,512]{3,2,1,0:T(8,128)(2,1)}, bf16[2,8,64,512]{3,2,1,0:T(8,128)(2,1)}, u32[]{:S(2)}, u32[]{:S(2)}) collective-permute-start(bf16[2,8,64,512]{3,2,1,0:T(8,128)(2,1)} %pack.1), channel_id=1, source_target_pairs={{0,8},{8,0},{16,24},{24,16},{1,9},{9,1},{17,25},{25,17},{2,10},{10... | collective-permute-start | bytes 3145736 | tf_op jit(solution)/shard_map/ppermute | solution.py:512
  12.9 17.3 %collective-permute-start.3 = (s16[1,8,272,128]{3,2,1,0:T(8,128)(2,1)}, s16[1,8,272,128]{3,2,1,0:T(8,128)(2,1)S(1)}, u32[]{:S(2)}, u32[]{:S(2)}) collective-permute-start(s16[1,8,272,128]{3,2,1,0:T(8,128)(2,1)} %get-tuple-element.53), channel_id=1, source_target_pairs={{0,16},{8,24},{16,0},{24,8},{1,17},{9,25},{17,1},{25,9},{2,18},{10... | collective-permute-start | bytes 1671176 | tf_op jit(solution)/shard_map/ppermute | solution.py:512
  14.2 11.0 %copy-start.4 = (s32[3]{0:T(128)S(1)}, s32[3]{0:T(128)}, u32[]{:S(2)}) copy-start(s32[3]{0:T(128)} %pad_add_fusion.place_ref) | copy-start | bytes 40
  29.4 0.8 copy-start.9
  35.0 0.8 copy-start.1
  35.8 24.4 %all-to-all-start.1 = ((s16[8,272,128]{2,1,0:T(8,128)(2,1)}), s16[8,272,128]{2,1,0:T(8,128)(2,1)}, u32[]{:S(2)}, u32[]{:S(2)}) async-start(s16[8,272,128]{2,1,0:T(8,128)(2,1)} %bitcast.11), calls=%async_computation.1 | async-start | bytes 1114112 | tf_op jit(solution)/shard_map/all_to_all | solution.py:538
  41.6 13.0 %collective-permute-start.2 = (s16[1,8,272,128]{3,2,1,0:T(8,128)(2,1)}, s16[1,8,272,128]{3,2,1,0:T(8,128)(2,1)S(1)}, u32[]{:S(2)}, u32[]{:S(2)}) collective-permute-start(s16[1,8,272,128]{3,2,1,0:T(8,128)(2,1)} %copy-done.9), channel_id=1, source_target_pairs={{0,16},{8,24},{16,0},{24,8},{1,17},{9,25},{17,1},{25,9},{2,18},{10... | collective-permute-start | bytes 1671176 | tf_op jit(solution)/shard_map/ppermute | solution.py:512
  59.4 0.8 copy-start.2
  60.2 18.9 %all-to-all-start = ((s16[8,272,128]{2,1,0:T(8,128)(2,1)}), s16[8,272,128]{2,1,0:T(8,128)(2,1)S(1)}, u32[]{:S(2)}, u32[]{:S(2)}) async-start(s16[8,272,128]{2,1,0:T(8,128)(2,1)} %bitcast.12), calls=%async_computation | async-start | bytes 1114112 | tf_op jit(solution)/shard_map/all_to_all | solution.py:538
  79.1 0.8 copy-start.10
  88.4 31.9 %all-to-all-start.2 = ((bf16[8,2,64,512]{3,2,1,0:T(8,128)(2,1)}), bf16[8,2,64,512]{3,2,1,0:T(8,128)(2,1)S(1)}, u32[]{:S(2)}, u32[]{:S(2)}) async-start(bf16[8,2,64,512]{3,2,1,0:T(8,128)(2,1)} %get-tuple-element.62), calls=%async_computation.2 | async-start | bytes 2097152 | tf_op jit(solution)/shard_map/all_to_all | solution.py:547
  120.3 30.0 %collective-permute-start.5 = (bf16[8,2,64,512]{3,2,1,0:T(8,128)(2,1)S(1)}, bf16[8,2,64,512]{3,2,1,0:T(8,128)(2,1)S(1)}, u32[]{:S(2)}, u32[]{:S(2)}) collective-permute-start(bf16[8,2,64,512]{3,2,1,0:T(8,128)(2,1)S(1)} %all-to-all-done.2.refs_0_), channel_id=1, source_target_pairs={{0,8},{8,0},{16,24},{24,16},{1,9},{9,1},{17,25},{25,17},{2,10},{10... | collective-permute-start | bytes 3145736 | tf_op jit(solution)/shard_map/ppermute | solution.py:512
  122.4 27.8 %collective-permute-start.4 = (bf16[8,2,64,512]{3,2,1,0:T(8,128)(2,1)S(1)}, bf16[8,2,64,512]{3,2,1,0:T(8,128)(2,1)S(1)}, u32[]{:S(2)}, u32[]{:S(2)}) collective-permute-start(bf16[8,2,64,512]{3,2,1,0:T(8,128)(2,1)S(1)} %all-to-all-done.2.refs_0_), channel_id=1, source_target_pairs={{0,16},{8,24},{16,0},{24,8},{1,17},{9,25},{17,1},{25,9},{2,18},{10... | collective-permute-start | bytes 3145736 | tf_op jit(solution)/shard_map/ppermute | solution.py:512
  136.1 16.8 %copy-start.5 = (s32[3]{0:T(128)S(1)}, s32[3]{0:T(128)}, u32[]{:S(2)}) copy-start(s32[3]{0:T(128)} %pad_add_fusion.place_ref) | copy-start | bytes 40
  136.1 16.8 %copy-start.7 = (s32[48]{0:T(128)S(1)}, s32[48]{0:T(128)}, u32[]{:S(2)}) copy-start(s32[48]{0:T(128)} %owner_ref.3) | copy-start | bytes 580
  136.1 16.8 %copy-start.8 = (s32[48]{0:T(128)S(1)}, s32[48]{0:T(128)}, u32[]{:S(2)}) copy-start(s32[48]{0:T(128)} %get-tuple-element.45.rank_ref) | copy-start | bytes 580
  150.1 2.7 %collective-permute-start.6 = (bf16[8,2,64,512]{3,2,1,0:T(8,128)(2,1)S(1)}, bf16[8,2,64,512]{3,2,1,0:T(8,128)(2,1)S(1)}, u32[]{:S(2)}, u32[]{:S(2)}) collective-permute-start(bf16[8,2,64,512]{3,2,1,0:T(8,128)(2,1)S(1)} %collective-permute-done.4.refs_2_), channel_id=1, source_target_pairs={{0,8},{8,0},{16,24},{24,16},{1,9},{9,1},{17,25},{25,17},{2,10},{10... | collective-permute-start | bytes 3145736 | tf_op jit(solution)/shard_map/ppermute | solution.py:512
